TPU v7x, 32 devices: a whole 2x2x4 slice. The times are simulated.
32 devices in a mesh: groups: 2 (over y), ctx: 8 (over z, x), head: 2 (over core).
Axes of the slice: x: 2, y: 2, z: 4, core: 2. Of those that a mesh axis runs over, the one named last changes fastest.
Arguments:
- query_tensor: bfloat16 [2048, 4096], P(('groups', 'ctx'), 'head'), parts along dimension 0, may hold values from -110 to 110
- key_tensor: bfloat16 [2048, 1024], P(('groups', 'ctx'), 'head'), parts along dimension 0, may hold values from -6 to 6
- value_tensor: bfloat16 [2048, 1024], P(('groups', 'ctx'), 'head'), parts along dimension 0, may hold values from -6 to 6
- slash_offsets: int32 [16, 2], P(('groups', 'head')), parts along dimension 0, may hold values from 256 to 1023
- vertical_tiles: int32 [16, 2], P(('groups', 'head')), parts along dimension 0, may hold values from 0 to 7, as said below
- kept_rows: int32 [16, 32], P(('groups', 'ctx')), parts along dimension 0, may hold values from 0 to 127, as said below
- kept_count: int32 [16], P('groups'), parts along dimension 0, may hold values from 4 to 32, as said below
- out_weight: bfloat16 [2048, 4096], P('ctx', 'head'), may hold values from -0.09375 to 0.09375
Outputs:
- attended: bfloat16 [2048, 4096], P(('groups', 'ctx'), 'head'), parts along dimension 0
- projected: bfloat16 [256, 2048], P(('groups', 'ctx'), 'head'), parts along dimension 0
There are 2 independent parts, one for each index of `groups`. A program takes and returns all parts, laid end to end along the dimension named above; an argument that names none is the same for every part. Nothing has to cross between parts.
Inputs may be any that keep to these rules, and one draw needn't show every extreme that they name: `vertical_tiles`: the tiles of one KV head differ. `kept_rows`: row c holds distinct local row indices of shard c; its first kept_count[c] entries are the kept rows in increasing order, the other entries are not kept. `kept_count`: each aligned block of 4 consecutive shards keeps exactly 64 rows in all.
All inputs are finite; a program needn't handle non-finite values.
Results may differ from a plain program's by a relative error of at most 0.0056.
Values may be sent and summed in bfloat16 or wider, within the bound.
No kernel may reach another device: no remote copies, remote signals or barrier semaphores. Data moves between devices by JAX's collectives and lax.ppermute only.
A program may use at most 64 MiB of HBM per device.

v0:
```python
import jax
import jax.numpy as jnp
from jax import lax
from jax.sharding import PartitionSpec as P

HEAD_SIZE = 128
SLASH_SPAN = 8
VTILES = 2
LOCAL_BAND_KEYS = 256
SLASH_W = 128
VTILE = 128


def shifted_2(x, axis, by):
    size = lax.axis_size(axis)
    pairs = [(i, i + by) for i in range(size) if 0 <= i + by < size]
    return lax.ppermute(x, axis, pairs)


def broadcast(x, axis, root):
    mine = lax.axis_index(axis) == root
    return lax.psum(jnp.where(mine, x, jnp.zeros_like(x)), axis)


def attend(
    query_rows,
    key_slab,
    value_slab,
    key_pos,
    query_pos,
    slash_shift_list,
    tile_list,
    column_kind,
    group_width,
):
    scores = jnp.dot(query_rows, key_slab.T, preferred_element_type=jnp.float32) * key_slab.shape[
        -1
    ] ** (-0.5)
    distance = query_pos[:, None] - key_pos[None, :]
    key_tile = jnp.where(key_pos >= 0, key_pos // VTILE, -1)
    vertical = jnp.any(key_tile[:, None] == tile_list[None, :], axis=1)[None, :]
    in_band = (distance >= 0) & (distance < LOCAL_BAND_KEYS) & ~vertical
    first_slash = (
        (distance >= slash_shift_list[0]) & (distance < slash_shift_list[0] + SLASH_W) & ~vertical
    )
    second_slash = (
        (distance >= slash_shift_list[1]) & (distance < slash_shift_list[1] + SLASH_W) & ~vertical
    )
    earlier = in_band | first_slash
    kinds = column_kind[None, :]
    allowed = jnp.where(
        kinds == 0,
        in_band,
        jnp.where(
            kinds == 1,
            first_slash & ~in_band,
            jnp.where(kinds == 2, second_slash & ~earlier, distance >= 0),
        ),
    )
    allowed = jnp.tile(allowed & (key_pos >= 0)[None, :], (group_width, 1))
    masked = jnp.where(allowed, scores, -jnp.inf)
    row_max = jnp.max(masked, axis=1, keepdims=True)
    weights = jnp.where(allowed, jnp.exp(masked - row_max), 0.0)
    row_sum = jnp.sum(weights, axis=1, keepdims=True)
    blended = jnp.dot(weights.astype(jnp.bfloat16), value_slab, preferred_element_type=jnp.float32)
    return (blended / row_sum).astype(jnp.bfloat16)


def heads_first(stacked, local_heads, head_dim):
    reordered = jnp.moveaxis(stacked, -2, 0)
    return reordered.reshape(local_heads, -1, head_dim)


def move_near(row_block, is_live, offset, target_slot, keep_rows, sender):
    slot_grid = jnp.arange(keep_rows, dtype=jnp.int32)[:, None]
    gathered = jnp.zeros((keep_rows, row_block.shape[1]), jnp.float32)
    for travel in range(-3, 4):
        chooser = (
            (slot_grid == target_slot[None, :]) & (offset[None, :] == travel) & is_live[None, :]
        ).astype(jnp.bfloat16)
        parcel = jnp.dot(chooser, row_block, preferred_element_type=jnp.float32).astype(
            jnp.bfloat16
        )
        if travel != 0:
            parcel = sender(parcel, travel)
        gathered = gathered + parcel.astype(jnp.float32)
    return gathered.astype(jnp.bfloat16)


def local(
    query_tensor,
    key_tensor,
    value_tensor,
    slash_offsets,
    vertical_tiles,
    kept_rows,
    kept_count,
    out_weight,
):
    shard_length = query_tensor.shape[0]
    head_dim = HEAD_SIZE
    local_heads = key_tensor.shape[1] // head_dim
    group_width = query_tensor.shape[1] // key_tensor.shape[1]
    shard_index = lax.axis_index("ctx")
    first_pos = shard_index * shard_length
    key_heads = key_tensor.reshape(shard_length, local_heads, head_dim)
    value_heads = value_tensor.reshape(shard_length, local_heads, head_dim)
    slash_spans = slash_offsets // shard_length
    own_pair = jnp.stack([key_heads, value_heads])
    moving = jnp.concatenate([own_pair, own_pair], 0)
    member_spans = jnp.stack(
        [slash_spans[:, 0], slash_spans[:, 0], slash_spans[:, 1], slash_spans[:, 1]]
    )
    for bit_number in range((SLASH_SPAN - 1).bit_length()):
        shifted = shifted_2(moving, "ctx", 1 << bit_number)
        head_flags = (member_spans >> bit_number & 1 == 1)[:, None, :, None]
        moving = jnp.where(head_flags, shifted, moving)
    nearby = jnp.concatenate([moving, own_pair], 0)
    distances = [nearby]
    for repeat_factor in range(2):
        nearby = shifted_2(nearby, "ctx", 1)
        distances.append(nearby)
    ordered = jnp.stack([distances[2], distances[1], distances[0]])
    band_pieces = ordered[:, 4:6]
    slash_pieces = jnp.stack([ordered[:, 0:2], ordered[:, 2:4]])
    tile_keys = []
    tile_values = []
    for head_number in range(local_heads):
        for tile_index in range(VTILES):
            fetched = broadcast(
                jnp.stack([key_heads[:, head_number], value_heads[:, head_number]]),
                "ctx",
                vertical_tiles[head_number, tile_index],
            )
            tile_keys.append(fetched[0])
            tile_values.append(fetched[1])
    all_keys = jnp.concatenate(
        [
            heads_first(band_pieces[:, 0], local_heads, head_dim),
            heads_first(slash_pieces[:, :, 0], local_heads, head_dim),
            jnp.stack(tile_keys).reshape(local_heads, VTILES * shard_length, head_dim),
        ],
        1,
    )
    all_values = jnp.concatenate(
        [
            heads_first(band_pieces[:, 1], local_heads, head_dim),
            heads_first(slash_pieces[:, :, 1], local_heads, head_dim),
            jnp.stack(tile_values).reshape(local_heads, VTILES * shard_length, head_dim),
        ],
        1,
    )
    window = jnp.arange(3 * shard_length, dtype=jnp.int32)
    band_pos = jnp.broadcast_to(
        first_pos - 2 * shard_length + window, (local_heads, 3 * shard_length)
    )
    slash_pos = first_pos - (slash_spans[:, :, None] + 2) * shard_length + window[None, None, :]
    tile_pos = (
        vertical_tiles[:, :, None] * shard_length
        + jnp.arange(shard_length, dtype=jnp.int32)[None, None, :]
    )
    key_pos = jnp.concatenate(
        [band_pos, slash_pos.reshape(local_heads, -1), tile_pos.reshape(local_heads, -1)], 1
    )
    column_kind = jnp.concatenate(
        [
            jnp.full((3 * shard_length,), 0, jnp.int32),
            jnp.full((3 * shard_length,), 1, jnp.int32),
            jnp.full((3 * shard_length,), 2, jnp.int32),
            jnp.full((VTILES * shard_length,), 3, jnp.int32),
        ]
    )
    query_pos = first_pos + jnp.arange(shard_length, dtype=jnp.int32)
    query_heads = (
        query_tensor.reshape(shard_length, local_heads, group_width, head_dim)
        .transpose(1, 2, 0, 3)
        .reshape(local_heads, group_width * shard_length, head_dim)
    )

    def attend_head(packed):
        return attend(
            packed[0],
            packed[1],
            packed[2],
            packed[3],
            query_pos,
            packed[4],
            packed[5],
            column_kind,
            group_width,
        )

    mixed_heads = lax.map(
        attend_head, (query_heads, all_keys, all_values, key_pos, slash_offsets, vertical_tiles)
    )
    attended = (
        mixed_heads.reshape(local_heads, group_width, shard_length, head_dim)
        .transpose(2, 0, 1, 3)
        .reshape(shard_length, -1)
    )
    keep_rows = shard_length // 8
    capacity = kept_rows.shape[1]
    starts = jnp.cumsum(kept_count) - kept_count
    slot_ids = jnp.arange(capacity, dtype=jnp.int32)
    is_live = slot_ids < kept_count[shard_index]
    placed_at = starts[shard_index] + slot_ids
    target_shard = placed_at // keep_rows
    target_slot = placed_at % keep_rows
    offset = target_shard - shard_index
    selected = jnp.take(attended, kept_rows[0], axis=0)
    rounded = lax.psum_scatter(
        lax.dot_general(
            selected,
            lax.all_gather(out_weight, "ctx", axis=0, tiled=True),
            (((1,), (1,)), ((), ())),
            preferred_element_type=jnp.float32,
        ),
        "head",
        scatter_dimension=1,
        tiled=True,
    ).astype(jnp.bfloat16)

    def send_output(parcel, travel):
        return shifted_2(parcel, "ctx", travel)

    projected = move_near(rounded, is_live, offset, target_slot, keep_rows, send_output)
    return (attended, projected)


def solution(mesh):
    placed = (
        P(("groups", "ctx"), "head"),
        P(("groups", "ctx"), "head"),
        P(("groups", "ctx"), "head"),
        P(("groups", "head"), None),
        P(("groups", "head"), None),
        P(("groups", "ctx"), None),
        P("groups"),
        P("ctx", "head"),
    )
    return jax.shard_map(
        local,
        mesh=mesh,
        in_specs=placed,
        out_specs=(P(("groups", "ctx"), "head"), P(("groups", "ctx"), "head")),
        check_vma=False,
    )
```

profile of v0, /device:TPU:1, one launch (start us, length us, event | category | flops | bytes accessed | tf_op | source)
XLA Modules:
  0.0 284.1 jit_solution(2545705615501974319)
XLA Ops:
  7.2 1.6 fusion.89
  10.2 1.0 reshape.503
  11.4 0.9 reshape.502
  20.1 4.0 %collective-permute-start = (bf16[4,128,4,128]{3,1,2,0:T(8,128)(2,1)S(1)}, bf16[4,128,4,128]{3,1,2,0:T(8,128)(2,1)S(1)}, u32[]{:S(2)}, u32[]{:S(2)}) collective-permute-start(bf16[4,128,4,128]{3,1,2,0:T(8,128)(2,1)S(1)} %get-tuple-element.200), channel_id=1, source_target_pairs={{0,2},{2,4},{4,6},{6,8},{8,10},{10,12},{12,14},{1,3},{3,5},{5,7},{... | collective-permute-start | bytes 1572872 | tf_op jit(solution)/shard_map/ppermute | solution.py:17
  26.6 9.8 %collective-permute-done = bf16[4,128,4,128]{3,1,2,0:T(8,128)(2,1)S(1)} collective-permute-done((bf16[4,128,4,128]{3,1,2,0:T(8,128)(2,1)S(1)}, bf16[4,128,4,128]{3,1,2,0:T(8,128)(2,1)S(1)}, u32[]{:S(2)}, u32[]{:S(2)}) %collective-permute-start) | collective-permute-done | bytes 524320 | tf_op jit(solution)/shard_map/ppermute | solution.py:17
  36.6 9.0 %collective-permute-start.1 = (bf16[4,128,4,128]{3,1,2,0:T(8,128)(2,1)S(1)}, bf16[4,128,4,128]{3,1,2,0:T(8,128)(2,1)S(1)}, u32[]{:S(2)}, u32[]{:S(2)}) collective-permute-start(bf16[4,128,4,128]{3,1,2,0:T(8,128)(2,1)S(1)} %broadcast_select_fusion), channel_id=1, source_target_pairs={{0,4},{2,6},{4,8},{6,10},{8,12},{10,14},{1,5},{3,7},{5,9},{7,11},{... | collective-permute-start | bytes 1572872 | tf_op jit(solution)/shard_map/ppermute | solution.py:17
  45.6 11.6 %collective-permute-done.1 = bf16[4,128,4,128]{3,1,2,0:T(8,128)(2,1)S(1)} collective-permute-done((bf16[4,128,4,128]{3,1,2,0:T(8,128)(2,1)S(1)}, bf16[4,128,4,128]{3,1,2,0:T(8,128)(2,1)S(1)}, u32[]{:S(2)}, u32[]{:S(2)}) %collective-permute-start.1) | collective-permute-done | bytes 524320 | tf_op jit(solution)/shard_map/ppermute | solution.py:17
  57.3 5.2 %collective-permute-start.2 = (bf16[4,128,4,128]{3,1,2,0:T(8,128)(2,1)S(1)}, bf16[4,128,4,128]{3,1,2,0:T(8,128)(2,1)S(1)}, u32[]{:S(2)}, u32[]{:S(2)}) collective-permute-start(bf16[4,128,4,128]{3,1,2,0:T(8,128)(2,1)S(1)} %broadcast_select_fusion.1), channel_id=1, source_target_pairs={{0,8},{2,10},{4,12},{6,14},{1,9},{3,11},{5,13},{7,15},{16,24},{18,... | collective-permute-start | bytes 1572872 | tf_op jit(solution)/shard_map/ppermute | solution.py:17
  63.1 10.2 %collective-permute-done.2 = bf16[4,128,4,128]{3,1,2,0:T(8,128)(2,1)S(1)} collective-permute-done((bf16[4,128,4,128]{3,1,2,0:T(8,128)(2,1)S(1)}, bf16[4,128,4,128]{3,1,2,0:T(8,128)(2,1)S(1)}, u32[]{:S(2)}, u32[]{:S(2)}) %collective-permute-start.2) | collective-permute-done | bytes 524320 | tf_op jit(solution)/shard_map/ppermute | solution.py:17
  73.5 1.3 collective-permute-start.3
  74.9 24.4 %all-reduce.3.cloned.1.call-done = (bf16[2,128,128]{2,1,0:T(8,128)(2,1)}, bf16[2,128,128]{2,1,0:T(8,128)(2,1)}, bf16[2,128,128]{2,1,0:T(8,128)(2,1)}, bf16[2,128...) async-done(((bf16[2,128,128]{2,1,0:T(8,128)(2,1)}, ...) | async-done | bytes 524304 | tf_op jit(solution)/shard_map/psum | solution.py:22
  99.2 0.8 constant_dynamic-update-slice_fusion.19
  100.0 0.8 constant_dynamic-update-slice_fusion.18
  100.8 0.8 constant_dynamic-update-slice_fusion.17
  101.6 0.8 constant_dynamic-update-slice_fusion.16
  102.4 11.7 %collective-permute-start.4 = (bf16[6,128,4,128]{3,1,2,0:T(8,128)(2,1)S(1)}, bf16[6,128,4,128]{3,1,2,0:T(8,128)(2,1)S(1)}, u32[]{:S(2)}, u32[]{:S(2)}) collective-permute-start(bf16[6,128,4,128]{3,1,2,0:T(8,128)(2,1)S(1)} %collective-permute-done.3), channel_id=1, source_target_pairs={{0,2},{2,4},{4,6},{6,8},{8,10},{10,12},{12,14},{1,3},{3,5},{5,7},{... | collective-permute-start | bytes 2359304 | tf_op jit(solution)/shard_map/ppermute | solution.py:17
  114.1 0.8 constant_dynamic-update-slice_fusion.15
  114.9 0.8 constant_dynamic-update-slice_fusion.14
  115.7 0.8 constant_dynamic-update-slice_fusion.13
  116.5 0.8 constant_dynamic-update-slice_fusion.12
  117.3 22.3 %collective-permute-done.4 = bf16[6,128,4,128]{3,1,2,0:T(8,128)(2,1)S(1)} collective-permute-done((bf16[6,128,4,128]{3,1,2,0:T(8,128)(2,1)S(1)}, bf16[6,128,4,128]{3,1,2,0:T(8,128)(2,1)S(1)}, u32[]{:S(2)}, u32[]{:S(2)}) %collective-permute-start.4) | collective-permute-done | bytes 786464 | tf_op jit(solution)/shard_map/ppermute | solution.py:17
  140.9 27.8 %while.13 = (s32[]{:T(128)}, bf16[4,512,128]{2,1,0:T(8,128)(2,1)}, s32[4,1408]{1,0:T(4,128)S(1)}, s32[4,2]{1,0:T(4,128)S(1)}, s32[4,2]{0,1:T(2,128)S(1)}, /*inde...) while((s32[]{:T(128)}, bf16[4,512,128]{2,1,0:T(8,128)(2,1)}, ...), condition=%wide.region_12.13_spmd.clone, body=%wide.region_8.12_spmd.clone.sunk | while | flops 378271104 | bytes 10238073 | solution.py:193
  143.0 2.0 fusion.113
  145.0 0.8 fusion.114
  145.8 0.9 fusion.115
  146.7 1.2 fusion.116
  150.0 2.0 fusion.113
  152.0 0.8 fusion.114
  152.8 0.9 fusion.115
  153.6 1.2 fusion.116
  156.9 2.0 fusion.113
  159.7 0.9 fusion.115
  160.6 1.2 fusion.116
  163.9 2.0 fusion.113
  166.7 0.9 fusion.115
  167.5 1.2 fusion.116
  168.7 1.4 copy.80
  171.3 71.2 %all-gather.2.cloned.1.call-done = bf16[2048,2048]{1,0:T(8,128)(2,1)} async-done(((bf16[256,2048]{1,0:T(8,128)(2,1)}), bf16[2048,2048]{1,0:T(8,128)(2,1)}) %all-gather.2.cloned.1.call-update) | async-done | bytes 8388624 | tf_op jit(solution)/shard_map/all_gather | solution.py:214
  242.4 6.7 %fusion.32 = f32[32,2048]{1,0:T(8,128)} fusion(bf16[2048,2048]{1,0:T(8,128)(2,1)} %all-gather.2.cloned.1.call-done, bf16[32,2048]{1,0:T(8,128)(2,1)S(1)} %gather_fusion, pred[32]{0:T(512)(128)(4,1)S(1)} %compare_and_fusion), kind=kOutput, calls=%fused_computation.75 | convolution fusion | flops 268500992 | bytes 8781856 | tf_op jit(solution)/shard_map/dot_general | solution.py:212
  251.2 5.1 %reduce-scatter.2.cloned.1.call-done = f32[32,1024]{1,0:T(8,128)} async-done(((f32[32,2048]{1,0:T(8,128)}), f32[32,1024]{1,0:T(8,128)}) %reduce-scatter.2.cloned.1.call-update) | async-done | bytes 131088 | tf_op jit(solution)/shard_map/reduce_scatter | solution.py:211
  256.3 0.9 convert_element_type.67
  257.4 1.3 collective-permute-start.5
  258.8 1.3 collective-permute-start.6
  260.2 1.3 collective-permute-start.7
  261.6 4.1 %collective-permute-start.8 = (bf16[16,1024]{1,0:T(8,128)(2,1)S(1)}, bf16[16,1024]{1,0:T(8,128)(2,1)S(1)}, u32[]{:S(2)}, u32[]{:S(2)}) collective-permute-start(bf16[16,1024]{1,0:T(8,128)(2,1)S(1)} %convolution_convert_fusion.2), channel_id=1, source_target_pairs={{0,2},{2,4},{4,6},{6,8},{8,10},{10,12},{12,14},{1,3},{3,5},{5,7},{... | collective-permute-start | bytes 98312 | tf_op jit(solution)/shard_map/ppermute | solution.py:17
  265.9 4.4 %collective-permute-start.9 = (bf16[16,1024]{1,0:T(8,128)(2,1)S(1)}, bf16[16,1024]{1,0:T(8,128)(2,1)S(1)}, u32[]{:S(2)}, u32[]{:S(2)}) collective-permute-start(bf16[16,1024]{1,0:T(8,128)(2,1)S(1)} %convolution_convert_fusion.1), channel_id=1, source_target_pairs={{0,4},{2,6},{4,8},{6,10},{8,12},{10,14},{1,5},{3,7},{5,9},{7,11},{... | collective-permute-start | bytes 98312 | tf_op jit(solution)/shard_map/ppermute | solution.py:17
  270.4 5.4 %collective-permute-start.10 = (bf16[16,1024]{1,0:T(8,128)(2,1)S(1)}, bf16[16,1024]{1,0:T(8,128)(2,1)S(1)}, u32[]{:S(2)}, u32[]{:S(2)}) collective-permute-start(bf16[16,1024]{1,0:T(8,128)(2,1)S(1)} %convolution_convert_fusion), channel_id=1, source_target_pairs={{0,6},{2,8},{4,10},{6,12},{8,14},{1,7},{3,9},{5,11},{7,13},{9,15},... | collective-permute-start | bytes 98312 | tf_op jit(solution)/shard_map/ppermute | solution.py:17
  275.9 1.0 collective-permute-done.10
  (141 shorter events, 18.6 us)
Async XLA Ops:
  7.2 92.1 %all-reduce.3.cloned.1.call-start = ((), (), s32[]{:S(2)}) async-start(), calls=%async_computation.3 | async-start | bytes 1048576 | tf_op jit(solution)/shard_map/psum | solution.py:22
  10.2 9.6 %copy-start.2 = (bf16[128,512]{1,0:T(8,128)(2,1)S(1)}, bf16[128,512]{1,0:T(8,128)(2,1)}, u32[]{:S(2)}) copy-start(bf16[128,512]{1,0:T(8,128)(2,1)} %param.11) | copy-start | bytes 393220
  11.1 8.7 %copy-start.3 = (bf16[128,512]{1,0:T(8,128)(2,1)S(1)}, bf16[128,512]{1,0:T(8,128)(2,1)}, u32[]{:S(2)}) copy-start(bf16[128,512]{1,0:T(8,128)(2,1)} %param.12) | copy-start | bytes 393220
  16.2 7.9 %copy-start.8 = (s32[4,2]{0,1:T(2,128)S(1)}, s32[4,2]{0,1:T(2,128)}, u32[]{:S(2)}) copy-start(s32[4,2]{0,1:T(2,128)} %param.14) | copy-start | bytes 100
  16.2 8.0 %copy-start.9 = (s32[4,2]{0,1:T(2,128)S(1)}, s32[4,2]{0,1:T(2,128)}, u32[]{:S(2)}) copy-start(s32[4,2]{0,1:T(2,128)} %param.13) | copy-start | bytes 100
  16.2 8.3 %copy-start.1 = (bf16[128,2048]{1,0:T(8,128)(2,1)S(1)}, bf16[128,2048]{1,0:T(8,128)(2,1)}, u32[]{:S(2)}) copy-start(bf16[128,2048]{1,0:T(8,128)(2,1)} %param.10) | copy-start | bytes 1572868
  19.0 6.1 %copy-start.10 = (s32[8]{0:T(128)S(1)}, s32[8]{0:T(128)}, u32[]{:S(2)}) copy-start(s32[8]{0:T(128)} %param.16) | copy-start | bytes 100
  19.0 7.6 %copy-start.11 = (s32[1,32]{1,0:T(1,128)S(1)}, s32[1,32]{1,0:T(1,128)}, u32[]{:S(2)}) copy-start(s32[1,32]{1,0:T(1,128)} %param.15) | copy-start | bytes 388
  19.0 223.5 %all-gather.2.cloned.1.call-start = ((), (), s32[]{:S(2)}) async-start(), calls=%async_computation.1 | async-start | bytes 9437184 | tf_op jit(solution)/shard_map/all_gather | solution.py:214
  19.7 236.6 %reduce-scatter.2.cloned.1.call-start = ((), (), s32[]{:S(2)}) async-start(), calls=%async_computation.2 | async-start | bytes 393216 | tf_op jit(solution)/shard_map/reduce_scatter | solution.py:211
  20.1 16.3 %collective-permute-start = (bf16[4,128,4,128]{3,1,2,0:T(8,128)(2,1)S(1)}, bf16[4,128,4,128]{3,1,2,0:T(8,128)(2,1)S(1)}, u32[]{:S(2)}, u32[]{:S(2)}) collective-permute-start(bf16[4,128,4,128]{3,1,2,0:T(8,128)(2,1)S(1)} %get-tuple-element.200), channel_id=1, source_target_pairs={{0,2},{2,4},{4,6},{6,8},{8,10},{10,12},{12,14},{1,3},{3,5},{5,7},{... | collective-permute-start | bytes 1572872 | tf_op jit(solution)/shard_map/ppermute | solution.py:17
  36.6 20.6 %collective-permute-start.1 = (bf16[4,128,4,128]{3,1,2,0:T(8,128)(2,1)S(1)}, bf16[4,128,4,128]{3,1,2,0:T(8,128)(2,1)S(1)}, u32[]{:S(2)}, u32[]{:S(2)}) collective-permute-start(bf16[4,128,4,128]{3,1,2,0:T(8,128)(2,1)S(1)} %broadcast_select_fusion), channel_id=1, source_target_pairs={{0,4},{2,6},{4,8},{6,10},{8,12},{10,14},{1,5},{3,7},{5,9},{7,11},{... | collective-permute-start | bytes 1572872 | tf_op jit(solution)/shard_map/ppermute | solution.py:17
  57.3 16.0 %collective-permute-start.2 = (bf16[4,128,4,128]{3,1,2,0:T(8,128)(2,1)S(1)}, bf16[4,128,4,128]{3,1,2,0:T(8,128)(2,1)S(1)}, u32[]{:S(2)}, u32[]{:S(2)}) collective-permute-start(bf16[4,128,4,128]{3,1,2,0:T(8,128)(2,1)S(1)} %broadcast_select_fusion.1), channel_id=1, source_target_pairs={{0,8},{2,10},{4,12},{6,14},{1,9},{3,11},{5,13},{7,15},{16,24},{18,... | collective-permute-start | bytes 1572872 | tf_op jit(solution)/shard_map/ppermute | solution.py:17
  73.5 28.9 %collective-permute-start.3 = (bf16[6,128,4,128]{3,1,2,0:T(8,128)(2,1)S(1)}, bf16[6,128,4,128]{3,1,2,0:T(8,128)(2,1)S(1)}, u32[]{:S(2)}, u32[]{:S(2)}) collective-permute-start(bf16[6,128,4,128]{3,1,2,0:T(8,128)(2,1)S(1)} %get-tuple-element.198), channel_id=1, source_target_pairs={{0,2},{2,4},{4,6},{6,8},{8,10},{10,12},{12,14},{1,3},{3,5},{5,7},{... | collective-permute-start | bytes 2359304 | tf_op jit(solution)/shard_map/ppermute | solution.py:17
  102.4 37.2 %collective-permute-start.4 = (bf16[6,128,4,128]{3,1,2,0:T(8,128)(2,1)S(1)}, bf16[6,128,4,128]{3,1,2,0:T(8,128)(2,1)S(1)}, u32[]{:S(2)}, u32[]{:S(2)}) collective-permute-start(bf16[6,128,4,128]{3,1,2,0:T(8,128)(2,1)S(1)} %collective-permute-done.3), channel_id=1, source_target_pairs={{0,2},{2,4},{4,6},{6,8},{8,10},{10,12},{12,14},{1,3},{3,5},{5,7},{... | collective-permute-start | bytes 2359304 | tf_op jit(solution)/shard_map/ppermute | solution.py:17
  140.2 0.7 copy-start.4
  140.2 0.7 copy-start.5
  140.2 0.7 copy-start.6
  140.2 0.7 copy-start.7
  170.6 78.6 %copy-start = (bf16[128,2048]{1,0:T(8,128)(2,1)}, bf16[128,2048]{1,0:T(8,128)(2,1)S(1)}, u32[]{:S(2)}) copy-start(bf16[128,2048]{1,0:T(8,128)(2,1)S(1)} %reshape.509) | copy-start | bytes 1572868
  257.4 13.0 %collective-permute-start.5 = (bf16[16,1024]{1,0:T(8,128)(2,1)S(1)}, bf16[16,1024]{1,0:T(8,128)(2,1)S(1)}, u32[]{:S(2)}, u32[]{:S(2)}) collective-permute-start(bf16[16,1024]{1,0:T(8,128)(2,1)S(1)} %convolution_convert_fusion.6), channel_id=1, source_target_pairs={{6,0},{8,2},{10,4},{12,6},{14,8},{7,1},{9,3},{11,5},{13,7},{15,9},... | collective-permute-start | bytes 98312 | tf_op jit(solution)/shard_map/ppermute | solution.py:17
  258.8 17.0 %collective-permute-start.6 = (bf16[16,1024]{1,0:T(8,128)(2,1)S(1)}, bf16[16,1024]{1,0:T(8,128)(2,1)S(1)}, u32[]{:S(2)}, u32[]{:S(2)}) collective-permute-start(bf16[16,1024]{1,0:T(8,128)(2,1)S(1)} %convolution_convert_fusion.5), channel_id=1, source_target_pairs={{4,0},{6,2},{8,4},{10,6},{12,8},{14,10},{5,1},{7,3},{9,5},{11,7},{... | collective-permute-start | bytes 98312 | tf_op jit(solution)/shard_map/ppermute | solution.py:17
  260.2 15.6 %collective-permute-start.7 = (bf16[16,1024]{1,0:T(8,128)(2,1)S(1)}, bf16[16,1024]{1,0:T(8,128)(2,1)S(1)}, u32[]{:S(2)}, u32[]{:S(2)}) collective-permute-start(bf16[16,1024]{1,0:T(8,128)(2,1)S(1)} %convolution_convert_fusion.4), channel_id=1, source_target_pairs={{2,0},{4,2},{6,4},{8,6},{10,8},{12,10},{14,12},{3,1},{5,3},{7,5},{... | collective-permute-start | bytes 98312 | tf_op jit(solution)/shard_map/ppermute | solution.py:17
  261.6 14.2 %collective-permute-start.8 = (bf16[16,1024]{1,0:T(8,128)(2,1)S(1)}, bf16[16,1024]{1,0:T(8,128)(2,1)S(1)}, u32[]{:S(2)}, u32[]{:S(2)}) collective-permute-start(bf16[16,1024]{1,0:T(8,128)(2,1)S(1)} %convolution_convert_fusion.2), channel_id=1, source_target_pairs={{0,2},{2,4},{4,6},{6,8},{8,10},{10,12},{12,14},{1,3},{3,5},{5,7},{... | collective-permute-start | bytes 98312 | tf_op jit(solution)/shard_map/ppermute | solution.py:17
  265.9 10.0 %collective-permute-start.9 = (bf16[16,1024]{1,0:T(8,128)(2,1)S(1)}, bf16[16,1024]{1,0:T(8,128)(2,1)S(1)}, u32[]{:S(2)}, u32[]{:S(2)}) collective-permute-start(bf16[16,1024]{1,0:T(8,128)(2,1)S(1)} %convolution_convert_fusion.1), channel_id=1, source_target_pairs={{0,4},{2,6},{4,8},{6,10},{8,12},{10,14},{1,5},{3,7},{5,9},{7,11},{... | collective-permute-start | bytes 98312 | tf_op jit(solution)/shard_map/ppermute | solution.py:17
  270.4 6.4 %collective-permute-start.10 = (bf16[16,1024]{1,0:T(8,128)(2,1)S(1)}, bf16[16,1024]{1,0:T(8,128)(2,1)S(1)}, u32[]{:S(2)}, u32[]{:S(2)}) collective-permute-start(bf16[16,1024]{1,0:T(8,128)(2,1)S(1)} %convolution_convert_fusion), channel_id=1, source_target_pairs={{0,6},{2,8},{4,10},{6,12},{8,14},{1,7},{3,9},{5,11},{7,13},{9,15},... | collective-permute-start | bytes 98312 | tf_op jit(solution)/shard_map/ppermute | solution.py:17
Sparse Core Ops, SparseCore 0:
  19.1 80.1 all-reduce.2
  101.4 141.0 all-gather.1
  249.3 6.9 reduce-scatter.1
where the time goes:
time: 288 us; the launch traced here: 284 us
  waiting for transfers between devices  156 us (54%)
  starting transfers between devices  49 us (17%)
  other arithmetic  19.6 us (7%)
  between operations  19.3 us (7%)
  local copies, waits for them, and re-layouts  18.6 us (6%)
  matrix products  16.2 us (6%)
  loops' own time  5.19 us (2%)
    all_gather x1, waiting for transfers between devices, local(): lax.all_gather(out_weight, 'ctx', axis=0, tiled=True)  71.2 us
    ppermute x11, waiting for transfers between devices, shifted_2(): return lax.ppermute(x, axis, pairs)  54.8 us
    ppermute x11, starting transfers between devices, shifted_2(): return lax.ppermute(x, axis, pairs)  48.9 us
    psum x1, waiting for transfers between devices, broadcast(): return lax.psum(jnp.where(mine, x, jnp.zeros_like(x)), axis)  24.4 us
    and x4, other arithmetic, attend(): allowed = jnp.tile(allowed & (key_pos >= 0)[None, :], (group_width, 1))  7.95 us
    dot_general x1, matrix products, local(): lax.dot_general(selected, lax.all_gather(out_weight, 'ctx', axis=0, tiled...  6.71 us
    unnamed x38, local copies, waits for them, and re-layouts  6.43 us
  transfers between devices with their start and end apart: 14, of which 8 were waited for; matrix products, arithmetic and copies ran while one was open for 14% of the time, Pallas kernels for 0%

commit v1 on v0

--- a/solution.py
+++ b/solution.py
@@ -1,6 +1,10 @@
+import math
+
 import jax
 import jax.numpy as jnp
 from jax import lax
+from jax.experimental import pallas as pl
+from jax.experimental.pallas import tpu as pltpu
 from jax.sharding import PartitionSpec as P
 
 HEAD_SIZE = 128
@@ -9,6 +13,312 @@
 LOCAL_BAND_KEYS = 256
 SLASH_W = 128
 VTILE = 128
+PAD_ROWS = 8
+MASKED = -1e30
+
+ANY = pl.BlockSpec(memory_space=pl.ANY)
+SMEM = pl.BlockSpec(memory_space=pltpu.SMEM)
+VMEM = pl.BlockSpec(memory_space=pltpu.VMEM)
+
+
+def xor_pairs(size, k):
+    return [(i, i ^ k) for i in range(size)]
+
+
+def pack_heads(shard_index, query, key, value, kept_rows, heads):
+    length = query.shape[0]
+    width = query.shape[1] // heads
+    hd = HEAD_SIZE
+    capacity = kept_rows.shape[1]
+    total = 2 * hd + width
+
+    def body(c_ref, q_ref, k_ref, v_ref, kept_ref, *rest):
+        out, (kept_buf, sems) = rest[:heads], rest[heads:]
+        slot = c_ref[0] % heads
+        copies = []
+        for j in range(heads):
+            head = slot ^ j
+            q_at = pl.multiple_of(head * width, hd)
+            k_at = pl.multiple_of(head * hd, hd)
+            copies += [
+                (k_ref.at[:, pl.ds(k_at, hd)], out[j].at[pl.ds(0, length), pl.ds(0, hd)]),
+                (v_ref.at[:, pl.ds(k_at, hd)], out[j].at[pl.ds(0, length), pl.ds(hd, hd)]),
+                (q_ref.at[:, pl.ds(q_at, width)], out[j].at[pl.ds(0, length), pl.ds(2 * hd, width)]),
+            ]
+        started = []
+        for number, (source, target) in enumerate(copies):
+            copy = pltpu.make_async_copy(source, target, sems.at[number])
+            copy.start()
+            started.append(copy)
+        kept_buf[...] = jnp.zeros(kept_buf.shape, jnp.bfloat16)
+        kept_buf[0:1, 0:capacity] = kept_ref[...].astype(jnp.float32).astype(jnp.bfloat16)
+        for j in range(heads):
+            copy = pltpu.make_async_copy(
+                kept_buf, out[j].at[pl.ds(length, PAD_ROWS)], sems.at[len(copies) + j]
+            )
+            copy.start()
+            started.append(copy)
+        for copy in started:
+            copy.wait()
+
+    return pl.pallas_call(
+        body,
+        out_shape=[jax.ShapeDtypeStruct((length + PAD_ROWS, total), jnp.bfloat16)] * heads,
+        in_specs=[SMEM, ANY, ANY, ANY, VMEM],
+        out_specs=[ANY] * heads,
+        scratch_shapes=[
+            pltpu.VMEM((PAD_ROWS, total), jnp.bfloat16),
+            pltpu.SemaphoreType.DMA((4 * heads,)),
+        ],
+        name="pack_heads",
+    )(shard_index, query, key, value, kept_rows)
+
+
+def pack_weight(shard_index, weight, heads):
+    width = weight.shape[1] // heads
+
+    def body(c_ref, w_ref, *rest):
+        out, sems = rest[:heads], rest[heads]
+        slot = c_ref[0] % heads
+        copies = []
+        for j in range(heads):
+            at = pl.multiple_of((slot ^ j) * width, HEAD_SIZE)
+            copies.append(pltpu.make_async_copy(w_ref.at[:, pl.ds(at, width)], out[j], sems.at[j]))
+        for copy in copies:
+            copy.start()
+        for copy in copies:
+            copy.wait()
+
+    return pl.pallas_call(
+        body,
+        out_shape=[jax.ShapeDtypeStruct((weight.shape[0], width), jnp.bfloat16)] * heads,
+        in_specs=[SMEM, ANY],
+        out_specs=[ANY] * heads,
+        scratch_shapes=[pltpu.SemaphoreType.DMA((heads,))],
+        name="pack_weight",
+    )(shard_index, weight)
+
+
+def attention(shard_index, slash, tiles, counts, near, far, keep_rows):
+    heads = len(near)
+    pieces = heads + len(far)
+    length = near[0].shape[0] - PAD_ROWS
+    hd = HEAD_SIZE
+    width = near[0].shape[1] - 2 * hd
+    group = width // hd
+    block_rows = heads * keep_rows
+    factor = hd ** (-0.5) * math.log2(math.e)
+
+    def body(c_ref, slash_ref, tile_ref, count_ref, *rest):
+        near_refs, rest = rest[:heads], rest[heads:]
+        far_refs, rest = rest[: len(far)], rest[len(far) :]
+        out_refs, rows_ref = rest[:heads], rest[heads]
+        k_all, v_all, bias = rest[heads + 1 :]
+        c = c_ref[0]
+        slot = c % heads
+        first = c - slot
+        for k in range(pieces):
+            ref = near_refs[k] if k < heads else far_refs[k - heads]
+            k_all[k * length : (k + 1) * length, :] = ref[0:length, 0:hd]
+            v_all[k * length : (k + 1) * length, :] = ref[0:length, hd : 2 * hd]
+        difference = lax.broadcasted_iota(jnp.int32, (length, length), 0) - lax.broadcasted_iota(
+            jnp.int32, (length, length), 1
+        )
+        offsets = [slash_ref[slot, i] for i in range(slash_ref.shape[1])]
+        verticals = [tile_ref[slot, i] for i in range(tile_ref.shape[1])]
+        rows = jnp.zeros((block_rows, width), jnp.float32)
+        for q in range(heads):
+            q_shard = c ^ q
+            for k in range(pieces):
+                k_shard = c ^ k
+                distance = difference + (q_shard - k_shard) * length
+                reach = jnp.int32(LOCAL_BAND_KEYS)
+                for tile in verticals:
+                    reach = jnp.where(tile == k_shard, jnp.int32(1 << 30), reach)
+                allowed = (distance >= 0) & (distance < reach)
+                for offset in offsets:
+                    allowed |= (distance >= offset) & (distance < offset + SLASH_W)
+                bias[:, k * length : (k + 1) * length] = jnp.where(allowed, 0.0, MASKED)
+            for g in range(group):
+                at = 2 * hd + g * hd
+                scores = lax.dot_general(
+                    near_refs[q][0:length, at : at + hd],
+                    k_all[...],
+                    (((1,), (1,)), ((), ())),
+                    preferred_element_type=jnp.float32,
+                )
+                scores = scores + bias[...]
+                top = jnp.max(scores, axis=1, keepdims=True)
+                weights = jnp.exp2((scores - top) * factor)
+                total = jnp.sum(weights, axis=1, keepdims=True)
+                mixed = jnp.dot(
+                    weights.astype(jnp.bfloat16), v_all[...], preferred_element_type=jnp.float32
+                )
+                out_refs[q][:, g * hd : (g + 1) * hd] = (mixed / total).astype(jnp.bfloat16)
+            q_slot = slot ^ q
+            before = jnp.int32(0)
+            for s in range(heads):
+                before = before + jnp.where(s < q_slot, count_ref[first + s], 0)
+            kept = near_refs[q][length : length + 1, 0:hd].astype(jnp.float32).astype(jnp.int32)
+            token = lax.broadcasted_iota(jnp.int32, (length, hd), 0)
+            is_token = (token == kept).astype(jnp.float32).astype(jnp.bfloat16)
+            index = lax.broadcasted_iota(jnp.int32, (hd, block_rows), 0)
+            place = lax.broadcasted_iota(jnp.int32, (hd, block_rows), 1)
+            is_place = ((place - index == before) & (index < count_ref[q_shard])).astype(jnp.float32)
+            chooser = jnp.dot(
+                is_token, is_place.astype(jnp.bfloat16), preferred_element_type=jnp.float32
+            ).astype(jnp.bfloat16)
+            rows = rows + lax.dot_general(
+                chooser,
+                out_refs[q][...],
+                (((0,), (0,)), ((), ())),
+                preferred_element_type=jnp.float32,
+            )
+        rows_ref[...] = rows.astype(jnp.bfloat16)
+
+    return pl.pallas_call(
+        body,
+        out_shape=[jax.ShapeDtypeStruct((length, width), jnp.bfloat16)] * heads
+        + [jax.ShapeDtypeStruct((block_rows, width), jnp.bfloat16)],
+        in_specs=[SMEM] * 4 + [VMEM] * pieces,
+        out_specs=[VMEM] * (heads + 1),
+        scratch_shapes=[
+            pltpu.VMEM((pieces * length, hd), jnp.bfloat16),
+            pltpu.VMEM((pieces * length, hd), jnp.bfloat16),
+            pltpu.VMEM((length, pieces * length), jnp.float32),
+        ],
+        name="attention",
+    )(shard_index, slash, tiles, counts, *near, *far)
+
+
+def project(where, own_rows, other_rows, weights):
+    heads = len(weights)
+    count = own_rows.shape[0]
+    outs = weights[0].shape[0]
+
+    def body(where_ref, own_ref, other_ref, *rest):
+        w_refs, (keep_ref, send_ref) = rest[:heads], rest[heads:]
+        slot = where_ref[0] % heads
+        keeps_own = where_ref[0] // heads == where_ref[1]
+        own, other = own_ref[...], other_ref[...]
+        both = jnp.concatenate(
+            [jnp.where(keeps_own, own, other), jnp.where(keeps_own, other, own)], 0
+        )
+        for j in range(heads):
+            at = pl.multiple_of((slot ^ j) * outs, HEAD_SIZE)
+            share = lax.dot_general(
+                both, w_refs[j][...], (((1,), (1,)), ((), ())), preferred_element_type=jnp.float32
+            )
+            keep_ref[:, pl.ds(at, outs)] = share[:count]
+            send_ref[:, pl.ds(at, outs)] = share[count:]
+
+    return pl.pallas_call(
+        body,
+        out_shape=[jax.ShapeDtypeStruct((count, heads * outs), jnp.float32)] * 2,
+        in_specs=[SMEM] + [VMEM] * (2 + heads),
+        out_specs=[VMEM] * 2,
+        name="project",
+    )(where, own_rows, other_rows, *weights)
+
+
+def split_rows(shard_index, kept, received, heads):
+    keep_rows = kept.shape[0] // heads
+
+    def body(c_ref, a_ref, b_ref, *out):
+        slot = c_ref[0] % heads
+        for j in range(heads):
+            at = pl.multiple_of((slot ^ j) * keep_rows, 8)
+            out[j][...] = (a_ref[pl.ds(at, keep_rows), :] + b_ref[pl.ds(at, keep_rows), :]).astype(
+                jnp.bfloat16
+            )
+
+    return pl.pallas_call(
+        body,
+        out_shape=[jax.ShapeDtypeStruct((keep_rows, kept.shape[1]), jnp.bfloat16)] * heads,
+        in_specs=[SMEM, VMEM, VMEM],
+        out_specs=[VMEM] * heads,
+        name="split_rows",
+    )(shard_index, kept, received)
+
+
+def join_heads(shard_index, pieces):
+    heads = len(pieces)
+    length, width = pieces[0].shape
+
+    def body(c_ref, *rest):
+        ins, (out_ref, sems) = rest[:heads], rest[heads:]
+        slot = c_ref[0] % heads
+        copies = []
+        for j in range(heads):
+            at = pl.multiple_of((slot ^ j) * width, HEAD_SIZE)
+            copies.append(
+                pltpu.make_async_copy(ins[j], out_ref.at[:, pl.ds(at, width)], sems.at[j])
+            )
+        for copy in copies:
+            copy.start()
+        for copy in copies:
+            copy.wait()
+
+    return pl.pallas_call(
+        body,
+        out_shape=jax.ShapeDtypeStruct((length, heads * width), jnp.bfloat16),
+        in_specs=[SMEM] + [ANY] * heads,
+        out_specs=ANY,
+        scratch_shapes=[pltpu.SemaphoreType.DMA((heads,))],
+        name="join_heads",
+    )(shard_index, *pieces)
+
+
+def local_blocks(
+    query_tensor,
+    key_tensor,
+    value_tensor,
+    slash_offsets,
+    vertical_tiles,
+    kept_rows,
+    kept_count,
+    out_weight,
+):
+    size = lax.axis_size("ctx")
+    cores = lax.axis_size("head")
+    heads = key_tensor.shape[1] // HEAD_SIZE
+    keep_rows = query_tensor.shape[0] // 8
+    c = lax.axis_index("ctx").astype(jnp.int32)
+    shard_index = c.reshape(1)
+
+    def swap(x, k):
+        return lax.ppermute(x, "ctx", xor_pairs(size, k))
+
+    packed = pack_heads(shard_index, query_tensor, key_tensor, value_tensor, kept_rows, heads)
+    near = [packed[0]] + [swap(packed[k], k) for k in range(1, heads)]
+    key_values = [x[: query_tensor.shape[0], : 2 * HEAD_SIZE] for x in packed]
+    far = [
+        lax.ppermute(
+            key_values[k % heads], "ctx", [(i, i ^ k) for i in range(size) if i // heads < (i ^ k) // heads]
+        )
+        for k in range(heads, size)
+    ]
+    packed_weight = pack_weight(shard_index, out_weight, heads)
+    weights = [packed_weight[0]] + [swap(packed_weight[k], k) for k in range(1, heads)]
+    *mixed, rows = attention(
+        shard_index, slash_offsets, vertical_tiles, kept_count, near, far, keep_rows
+    )
+    other_rows = swap(rows, heads)
+    returned = [mixed[0]] + [swap(mixed[k], k) for k in range(1, heads)]
+    attended = join_heads(shard_index, returned)
+    where = jnp.stack([c, lax.axis_index("head").astype(jnp.int32)])
+    kept, sent = project(where, rows, other_rows, weights)
+    received = lax.ppermute(sent, "head", [(i, cores - 1 - i) for i in range(cores)])
+    shares = split_rows(shard_index, kept, received, heads)
+    total = jnp.zeros(shares[0].shape, jnp.float32)
+    for k in range(heads):
+        pairs = []
+        for i in range(size):
+            for h in range(cores):
+                target = heads * h + ((i % heads) ^ k)
+                pairs.append((i * cores + h, target * cores + i // heads))
+        total = total + lax.ppermute(shares[k], ("ctx", "head"), pairs).astype(jnp.float32)
+    return (attended, total.astype(jnp.bfloat16))
 
 
 def shifted_2(x, axis, by):
@@ -238,8 +548,18 @@
         P("groups"),
         P("ctx", "head"),
     )
+    def program(*args):
+        heads = args[1].shape[1] // HEAD_SIZE
+        size = lax.axis_size("ctx")
+        power = size & (size - 1) == 0 and heads & (heads - 1) == 0
+        whole_tiles = args[0].shape[0] == VTILE and args[5].shape[1] <= HEAD_SIZE
+        cores = lax.axis_size("head")
+        if power and whole_tiles and cores == 2 and size == heads * cores:
+            return local_blocks(*args)
+        return local(*args)
+
     return jax.shard_map(
-        local,
+        program,
         mesh=mesh,
         in_specs=placed,
         out_specs=(P(("groups", "ctx"), "head"), P(("groups", "ctx"), "head")),

time: 288 us -> 137 us (0.48); the launches traced: 284 us -> 137 us
  waiting for transfers between devices: 156 us -> 4.35 us
  Pallas kernels: 0 us -> 89.5 us
  between operations: 19.3 us -> 0.88 us
  other arithmetic: 19.6 us -> 1.22 us
  starting transfers between devices: 49 us -> 32 us
  matrix products: 16.2 us -> 0 us
  local copies, waits for them, and re-layouts: 18.6 us -> 8.8 us
  loops' own time: 5.19 us -> 0 us
    pallas_call x0 -> x6, Pallas kernels: none -> 89.5 us  [the longest x1 32.9 us: pack_weight(): pl.pallas_call(body, out_shape=[jax.ShapeDtypeStruct((weight.shape[0], wi...]
    all_gather x1 -> x0, waiting for transfers between devices: 71.2 us -> none  [local(): lax.all_gather(out_weight, 'ctx', axis=0, tiled=True)]
    ppermute x11 -> x19, waiting for transfers between devices: 54.8 us -> 4.35 us  [the longest x10 4.32 us: swap(): return lax.ppermute(x, 'ctx', xor_pairs(size, k))]
    psum x1 -> x0, waiting for transfers between devices: 24.4 us -> none  [broadcast(): return lax.psum(jnp.where(mine, x, jnp.zeros_like(x)), axis)]
    ppermute x11 -> x19, starting transfers between devices: 48.9 us -> 32 us  [the longest x10 9.95 us: swap(): return lax.ppermute(x, 'ctx', xor_pairs(size, k))]
    dot_general x16 -> x0, matrix products: 16.2 us -> none  [the longest x1 6.71 us: local(): lax.dot_general(selected, lax.all_gather(out_weight, 'ctx', axis=0, tiled...]
    and x5 -> x0, other arithmetic: 7.96 us -> none  [the longest x4 7.95 us: attend(): allowed = jnp.tile(allowed & (key_pos >= 0)[None, :], (group_width, 1))]
    another operation x1 -> x0, loops' own time: 5.19 us -> none  [local(): lax.map(attend_head, (query_heads, all_keys, all_values, key_pos, slash_o...]
  transfers between devices with their start and end apart: 14 -> 19, of which waited for: 8 -> 1; matrix products, arithmetic and copies ran while one was open for 14% -> 4% of each run, Pallas kernels for 0% -> 45%
where the time goes in v1:
time: 137 us
  Pallas kernels  89.5 us (65%)
  starting transfers between devices  32 us (23%)
  local copies, waits for them, and re-layouts  8.8 us (6%)
  waiting for transfers between devices  4.35 us (3%)
    pallas_call x1, Pallas kernels, pack_weight(): pl.pallas_call(body, out_shape=[jax.ShapeDtypeStruct((weight.shape[0], wi...  32.9 us
    pallas_call x1, Pallas kernels, pack_heads(): pl.pallas_call(body, out_shape=[jax.ShapeDtypeStruct((length + PAD_ROWS,...  25.7 us
    pallas_call x1, Pallas kernels, join_heads(): pl.pallas_call(body, out_shape=jax.ShapeDtypeStruct((length, heads * widt...  17 us
    ppermute x10, starting transfers between devices, swap(): return lax.ppermute(x, 'ctx', xor_pairs(size, k))  9.95 us
    pallas_call x1, Pallas kernels, attention(): pl.pallas_call(body, out_shape=[jax.ShapeDtypeStruct((length, width), jnp...  9.63 us
    ppermute x4, starting transfers between devices, local_blocks(): lax.ppermute(key_values[k % heads], 'ctx', [(i, i ^ k) for i in range(siz...  9.19 us
    ppermute x4, starting transfers between devices, local_blocks(): lax.ppermute(shares[k], ('ctx', 'head'), pairs).astype(jnp.float32)  9.05 us
    unnamed x46, local copies, waits for them, and re-layouts  5.38 us
  transfers between devices with their start and end apart: 19, of which 1 were waited for; matrix products, arithmetic and copies ran while one was open for 4% of the time, Pallas kernels for 45%

profile of v1, /device:TPU:1, one launch (start us, length us, event | category | flops | bytes accessed | tf_op | source)
XLA Modules:
  0.0 136.8 jit_solution(12648527578552091417)
XLA Ops:
  0.6 25.7 %pack_heads.1 = (bf16[136,768]{1,0:T(8,128)(2,1)}, bf16[136,768]{1,0:T(8,128)(2,1)}, bf16[136,768]{1,0:T(8,128)(2,1)}, bf16[136,768]{1,0:T(8,128)(2,1)}) custom-call(s32[1]{0:T(128)} %bitcast.c_ref, bf16[128,2048]{1,0:T(8,128)(2,1)} %q_ref.1, bf16[128,512]{1,0:T(8,128)(2,1)} %k_ref.1, bf16[128,512]{1,0:T(8,128)(2,1)} %v_ref.1, s32[1,32]{1,0:T(1,128)} %kept_ref.1), custom_call_target="tpu_custom_call" | custom-call | tf_op jit(solution)/shard_map/pack_heads/pallas_call | solution.py:64
  26.4 2.1 %collective-permute-start = (bf16[136,768]{1,0:T(8,128)(2,1)}, bf16[136,768]{1,0:T(8,128)(2,1)S(1)}, u32[]{:S(2)}, u32[]{:S(2)}) collective-permute-start(bf16[136,768]{1,0:T(8,128)(2,1)} %get-tuple-element.22), channel_id=1, source_target_pairs={{0,2},{2,0},{4,6},{6,4},{8,10},{10,8},{12,14},{14,12},{1,3},{3,1},... | collective-permute-start | bytes 626696 | tf_op jit(solution)/shard_map/ppermute | solution.py:290
  28.5 0.9 slice.15
  29.4 5.3 %collective-permute-start.6 = (bf16[128,256]{1,0:T(8,128)(2,1)S(1)}, bf16[128,256]{1,0:T(8,128)(2,1)S(1)}, u32[]{:S(2)}, u32[]{:S(2)}) collective-permute-start(bf16[128,256]{1,0:T(8,128)(2,1)S(1)} %slice.15), channel_id=1, source_target_pairs={{0,14},{2,12},{4,10},{6,8},{1,15},{3,13},{5,11},{7,9},{16,30},{18,... | collective-permute-start | bytes 196616 | tf_op jit(solution)/shard_map/ppermute | solution.py:296
  34.7 0.8 slice.14
  35.5 1.3 collective-permute-start.5
  36.8 0.8 slice.13
  37.7 1.3 collective-permute-start.4
  39.0 0.8 slice.12
  39.8 1.3 collective-permute-start.3
  41.1 0.3 collective-permute-start.1
  41.5 2.1 %collective-permute-start.2 = (bf16[136,768]{1,0:T(8,128)(2,1)S(1)}, bf16[136,768]{1,0:T(8,128)(2,1)S(1)}, u32[]{:S(2)}, u32[]{:S(2)}) collective-permute-start(bf16[136,768]{1,0:T(8,128)(2,1)S(1)} %copy-done.15), channel_id=1, source_target_pairs={{0,6},{2,4},{4,2},{6,0},{8,14},{10,12},{12,10},{14,8},{1,7},{3,5},... | collective-permute-start | bytes 626696 | tf_op jit(solution)/shard_map/ppermute | solution.py:290
  43.6 32.9 %pack_weight.1 = (bf16[256,512]{1,0:T(8,128)(2,1)}, bf16[256,512]{1,0:T(8,128)(2,1)}, bf16[256,512]{1,0:T(8,128)(2,1)}, bf16[256,512]{1,0:T(8,128)(2,1)}) custom-call(s32[1]{0:T(128)} %bitcast.c_ref, bf16[256,2048]{1,0:T(8,128)(2,1)} %w_ref.1), custom_call_target="tpu_custom_call" | custom-call | tf_op jit(solution)/shard_map/pack_weight/pallas_call | solution.py:92
  76.6 0.0 collective-permute-done.4.rest_5_
  76.6 0.3 collective-permute-start.11
  77.0 0.3 collective-permute-start.12
  77.2 0.0 collective-permute-done.rest_1_
  77.2 2.1 %collective-permute-start.13 = (bf16[256,512]{1,0:T(8,128)(2,1)}, bf16[256,512]{1,0:T(8,128)(2,1)S(1)}, u32[]{:S(2)}, u32[]{:S(2)}) collective-permute-start(bf16[256,512]{1,0:T(8,128)(2,1)} %get-tuple-element.33), channel_id=1, source_target_pairs={{0,6},{2,4},{4,2},{6,0},{8,14},{10,12},{12,10},{14,8},{1,7},{3,5},... | collective-permute-start | bytes 786440 | tf_op jit(solution)/shard_map/ppermute | solution.py:290
  79.3 0.7 copy-done.17
  80.0 0.7 copy.10.slash_ref
  80.7 0.0 copy-done.18
  80.7 0.7 copy.11.tile_ref
  81.4 0.0 collective-permute-done.1.rest_2_
  81.4 0.0 collective-permute-done.2.rest_3_
  81.4 0.6 copy-done.5
  82.0 0.7 copy-done.6
  82.7 9.6 %attention.1 = (bf16[128,512]{1,0:T(8,128)(2,1)}, bf16[128,512]{1,0:T(8,128)(2,1)}, bf16[128,512]{1,0:T(8,128)(2,1)}, bf16[128,512]{1,0:T(8,128)(2,1)}, bf16[64,512]{1,0:T(8,128)(2,1)}) custom-call(s32[1]{0:T(128)} %bitcast.c_ref, s32[4,2]{1,0:T(4,128)} %copy.10.slash_ref, s32[4,2]{1,0:T(4,128)} %copy.11.tile_ref, s32[8]{0:T(128)} %count_ref.1, ...), custom_call_target="tpu_custom_call" | custom-call | tf_op jit(solution)/shard_map/attention/pallas_call | solution.py:179
  92.4 0.6 pad_add_fusion.where_ref
  93.0 0.0 collective-permute-done.13.rest_3_
  93.0 4.3 %collective-permute-done.10.other_ref = bf16[64,512]{1,0:T(8,128)(2,1)S(1)} collective-permute-done((bf16[64,512]{1,0:T(8,128)(2,1)}, bf16[64,512]{1,0:T(8,128)(2,1)S(1)}, u32[]{:S(2)}, u32[]{:S(2)}) %collective-permute-start.10) | collective-permute-done | bytes 65568 | tf_op jit(solution)/shard_map/ppermute | solution.py:290
  97.3 0.6 copy-done.14
  97.9 2.6 %project.1 = (f32[64,1024]{1,0:T(8,128)}, f32[64,1024]{1,0:T(8,128)}) custom-call(s32[2]{0:T(128)} %pad_add_fusion.where_ref, bf16[64,512]{1,0:T(8,128)(2,1)} %get-tuple-element.29.own_ref, bf16[64,512]{1,0:T(8,128)(2,1)} %copy-done.14, bf16[256,512]{1,0:T(8,128)(2,1)} %get-tuple-element.30.rest_0_, bf16[256,512]{1,0:T(8,128)(2,1)} %copy-done.1, ...), custom_call_target="tpu_custom_call" | custom-call | tf_op jit(solution)/shard_map/project/pallas_call | solution.py:215
  100.5 3.8 %collective-permute-start.14 = (f32[64,1024]{1,0:T(8,128)}, f32[64,1024]{1,0:T(8,128)S(1)}, u32[]{:S(2)}, u32[]{:S(2)}) collective-permute-start(f32[64,1024]{1,0:T(8,128)} %get-tuple-element.35), channel_id=1, source_target_pairs={{0,1},{1,0},{2,3},{3,2},{4,5},{5,4},{6,7},{7,6},{8,9},{9,8},{10,11... | collective-permute-start | bytes 786440 | tf_op jit(solution)/shard_map/ppermute | solution.py:311
  104.3 0.3 collective-permute-start.7
  104.6 0.0 collective-permute-start.8
  104.6 2.4 %collective-permute-start.9 = (bf16[128,512]{1,0:T(8,128)(2,1)S(1)}, bf16[128,512]{1,0:T(8,128)(2,1)S(1)}, u32[]{:S(2)}, u32[]{:S(2)}) collective-permute-start(bf16[128,512]{1,0:T(8,128)(2,1)S(1)} %copy-done.19), channel_id=1, source_target_pairs={{0,6},{2,4},{4,2},{6,0},{8,14},{10,12},{12,10},{14,8},{1,7},{3,5},... | collective-permute-start | bytes 393224 | tf_op jit(solution)/shard_map/ppermute | solution.py:290
  106.9 0.7 copy-done
  107.6 1.7 %split_rows.1 = (bf16[16,1024]{1,0:T(8,128)(2,1)}, bf16[16,1024]{1,0:T(8,128)(2,1)}, bf16[16,1024]{1,0:T(8,128)(2,1)}, bf16[16,1024]{1,0:T(8,128)(2,1)}) custom-call(s32[1]{0:T(128)} %bitcast.c_ref, f32[64,1024]{1,0:T(8,128)} %get-tuple-element.34.a_ref, f32[64,1024]{1,0:T(8,128)} %copy-done), custom_call_target="tpu_custom_call" | custom-call | tf_op jit(solution)/shard_map/split_rows/pallas_call | solution.py:235
  109.3 2.2 %collective-permute-start.15 = (bf16[16,1024]{1,0:T(8,128)(2,1)}, bf16[16,1024]{1,0:T(8,128)(2,1)S(1)}, u32[]{:S(2)}, u32[]{:S(2)}) collective-permute-start(bf16[16,1024]{1,0:T(8,128)(2,1)} %get-tuple-element.36), channel_id=1, source_target_pairs={{0,0},{1,8},{2,2},{3,10},{4,4},{5,12},{6,6},{7,14},{8,1},{9,9},{10... | collective-permute-start | bytes 98312 | tf_op jit(solution)/shard_map/ppermute | solution.py:320
  111.6 2.4 %collective-permute-start.16 = (bf16[16,1024]{1,0:T(8,128)(2,1)}, bf16[16,1024]{1,0:T(8,128)(2,1)S(1)}, u32[]{:S(2)}, u32[]{:S(2)}) collective-permute-start(bf16[16,1024]{1,0:T(8,128)(2,1)} %get-tuple-element.37), channel_id=1, source_target_pairs={{0,2},{1,10},{2,0},{3,8},{4,6},{5,14},{6,4},{7,12},{8,3},{9,11},{1... | collective-permute-start | bytes 98312 | tf_op jit(solution)/shard_map/ppermute | solution.py:320
  113.9 0.0 collective-permute-done.7.rest_1_
  113.9 1.7 %collective-permute-start.17 = (bf16[16,1024]{1,0:T(8,128)(2,1)}, bf16[16,1024]{1,0:T(8,128)(2,1)S(1)}, u32[]{:S(2)}, u32[]{:S(2)}) collective-permute-start(bf16[16,1024]{1,0:T(8,128)(2,1)} %get-tuple-element.38), channel_id=1, source_target_pairs={{0,4},{1,12},{2,6},{3,14},{4,0},{5,8},{6,2},{7,10},{8,5},{9,13},{1... | collective-permute-start | bytes 98312 | tf_op jit(solution)/shard_map/ppermute | solution.py:320
  115.6 2.7 %collective-permute-start.18 = (bf16[16,1024]{1,0:T(8,128)(2,1)}, bf16[16,1024]{1,0:T(8,128)(2,1)S(1)}, u32[]{:S(2)}, u32[]{:S(2)}) collective-permute-start(bf16[16,1024]{1,0:T(8,128)(2,1)} %get-tuple-element.39), channel_id=1, source_target_pairs={{0,6},{1,14},{2,4},{3,12},{4,2},{5,10},{6,0},{7,8},{8,7},{9,15},{1... | collective-permute-start | bytes 98312 | tf_op jit(solution)/shard_map/ppermute | solution.py:320
  118.4 0.6 copy-done.9
  119.1 17.0 %join_heads.1 = bf16[128,2048]{1,0:T(8,128)(2,1)} custom-call(s32[1]{0:T(128)} %bitcast.c_ref, bf16[128,512]{1,0:T(8,128)(2,1)} %get-tuple-element.25.rest_0_, bf16[128,512]{1,0:T(8,128)(2,1)} %copy-done.7, bf16[128,512]{1,0:T(8,128)(2,1)} %copy-done.8, bf16[128,512]{1,0:T(8,128)(2,1)} %copy-done.9), custom_call_target="tpu_custom_call" | custom-call | tf_op jit(solution)/shard_map/join_heads/pallas_call | solution.py:262
  136.1 0.0 collective-permute-done.15
  136.1 0.0 collective-permute-done.18
  136.1 0.6 add_convert_fusion
  (48 shorter events, 0.1 us)
Async XLA Ops:
  26.4 50.9 %collective-permute-start = (bf16[136,768]{1,0:T(8,128)(2,1)}, bf16[136,768]{1,0:T(8,128)(2,1)S(1)}, u32[]{:S(2)}, u32[]{:S(2)}) collective-permute-start(bf16[136,768]{1,0:T(8,128)(2,1)} %get-tuple-element.22), channel_id=1, source_target_pairs={{0,2},{2,0},{4,6},{6,4},{8,10},{10,8},{12,14},{14,12},{1,3},{3,1},... | collective-permute-start | bytes 626696 | tf_op jit(solution)/shard_map/ppermute | solution.py:290
  28.5 12.7 %copy-start.16 = (bf16[136,768]{1,0:T(8,128)(2,1)S(1)}, bf16[136,768]{1,0:T(8,128)(2,1)}, u32[]{:S(2)}) copy-start(bf16[136,768]{1,0:T(8,128)(2,1)} %get-tuple-element.23) | copy-start | bytes 626692
  29.4 12.1 %copy-start.15 = (bf16[136,768]{1,0:T(8,128)(2,1)S(1)}, bf16[136,768]{1,0:T(8,128)(2,1)}, u32[]{:S(2)}) copy-start(bf16[136,768]{1,0:T(8,128)(2,1)} %get-tuple-element.24) | copy-start | bytes 626692
  29.4 11.8 %collective-permute-start.6 = (bf16[128,256]{1,0:T(8,128)(2,1)S(1)}, bf16[128,256]{1,0:T(8,128)(2,1)S(1)}, u32[]{:S(2)}, u32[]{:S(2)}) collective-permute-start(bf16[128,256]{1,0:T(8,128)(2,1)S(1)} %slice.15), channel_id=1, source_target_pairs={{0,14},{2,12},{4,10},{6,8},{1,15},{3,13},{5,11},{7,9},{16,30},{18,... | collective-permute-start | bytes 196616 | tf_op jit(solution)/shard_map/ppermute | solution.py:296
  35.5 6.0 %collective-permute-start.5 = (bf16[128,256]{1,0:T(8,128)(2,1)S(1)}, bf16[128,256]{1,0:T(8,128)(2,1)S(1)}, u32[]{:S(2)}, u32[]{:S(2)}) collective-permute-start(bf16[128,256]{1,0:T(8,128)(2,1)S(1)} %slice.14), channel_id=1, source_target_pairs={{0,12},{2,14},{4,8},{6,10},{1,13},{3,15},{5,9},{7,11},{16,28},{18,... | collective-permute-start | bytes 196616 | tf_op jit(solution)/shard_map/ppermute | solution.py:296
  37.7 38.9 %collective-permute-start.4 = (bf16[128,256]{1,0:T(8,128)(2,1)S(1)}, bf16[128,256]{1,0:T(8,128)(2,1)S(1)}, u32[]{:S(2)}, u32[]{:S(2)}) collective-permute-start(bf16[128,256]{1,0:T(8,128)(2,1)S(1)} %slice.13), channel_id=1, source_target_pairs={{0,10},{2,8},{4,14},{6,12},{1,11},{3,9},{5,15},{7,13},{16,26},{18,... | collective-permute-start | bytes 196616 | tf_op jit(solution)/shard_map/ppermute | solution.py:296
  39.8 37.1 %collective-permute-start.3 = (bf16[128,256]{1,0:T(8,128)(2,1)S(1)}, bf16[128,256]{1,0:T(8,128)(2,1)S(1)}, u32[]{:S(2)}, u32[]{:S(2)}) collective-permute-start(bf16[128,256]{1,0:T(8,128)(2,1)S(1)} %slice.12), channel_id=1, source_target_pairs={{0,8},{2,10},{4,12},{6,14},{1,9},{3,11},{5,13},{7,15},{16,24},{18,... | collective-permute-start | bytes 196616 | tf_op jit(solution)/shard_map/ppermute | solution.py:296
  41.1 35.4 %copy-start.10 = (bf16[128,256]{1,0:T(8,128)(2,1)}, bf16[128,256]{1,0:T(8,128)(2,1)S(1)}, u32[]{:S(2)}) copy-start(bf16[128,256]{1,0:T(8,128)(2,1)S(1)} %collective-permute-done.6.rest_7_) | copy-start | bytes 196612
  41.1 40.2 %collective-permute-start.1 = (bf16[136,768]{1,0:T(8,128)(2,1)S(1)}, bf16[136,768]{1,0:T(8,128)(2,1)S(1)}, u32[]{:S(2)}, u32[]{:S(2)}) collective-permute-start(bf16[136,768]{1,0:T(8,128)(2,1)S(1)} %copy-done.16), channel_id=1, source_target_pairs={{0,4},{2,6},{4,0},{6,2},{8,12},{10,14},{12,8},{14,10},{1,5},{3,7},... | collective-permute-start | bytes 626696 | tf_op jit(solution)/shard_map/ppermute | solution.py:290
  41.5 35.1 %copy-start.11 = (bf16[128,256]{1,0:T(8,128)(2,1)}, bf16[128,256]{1,0:T(8,128)(2,1)S(1)}, u32[]{:S(2)}) copy-start(bf16[128,256]{1,0:T(8,128)(2,1)S(1)} %collective-permute-done.5.rest_6_) | copy-start | bytes 196612
  41.5 39.9 %collective-permute-start.2 = (bf16[136,768]{1,0:T(8,128)(2,1)S(1)}, bf16[136,768]{1,0:T(8,128)(2,1)S(1)}, u32[]{:S(2)}, u32[]{:S(2)}) collective-permute-start(bf16[136,768]{1,0:T(8,128)(2,1)S(1)} %copy-done.15), channel_id=1, source_target_pairs={{0,6},{2,4},{4,2},{6,0},{8,14},{10,12},{12,10},{14,8},{1,7},{3,5},... | collective-permute-start | bytes 626696 | tf_op jit(solution)/shard_map/ppermute | solution.py:290
  76.6 4.8 %copy-start.12 = (bf16[128,256]{1,0:T(8,128)(2,1)}, bf16[128,256]{1,0:T(8,128)(2,1)S(1)}, u32[]{:S(2)}) copy-start(bf16[128,256]{1,0:T(8,128)(2,1)S(1)} %collective-permute-done.4.rest_5_) | copy-start | bytes 196612
  76.6 16.4 %collective-permute-start.11 = (bf16[256,512]{1,0:T(8,128)(2,1)}, bf16[256,512]{1,0:T(8,128)(2,1)S(1)}, u32[]{:S(2)}, u32[]{:S(2)}) collective-permute-start(bf16[256,512]{1,0:T(8,128)(2,1)} %get-tuple-element.31), channel_id=1, source_target_pairs={{0,2},{2,0},{4,6},{6,4},{8,10},{10,8},{12,14},{14,12},{1,3},{3,1},... | collective-permute-start | bytes 786440 | tf_op jit(solution)/shard_map/ppermute | solution.py:290
  76.9 4.4 %copy-start.13 = (bf16[128,256]{1,0:T(8,128)(2,1)}, bf16[128,256]{1,0:T(8,128)(2,1)S(1)}, u32[]{:S(2)}) copy-start(bf16[128,256]{1,0:T(8,128)(2,1)S(1)} %collective-permute-done.3.rest_4_) | copy-start | bytes 196612
  77.0 16.0 %collective-permute-start.12 = (bf16[256,512]{1,0:T(8,128)(2,1)}, bf16[256,512]{1,0:T(8,128)(2,1)S(1)}, u32[]{:S(2)}, u32[]{:S(2)}) collective-permute-start(bf16[256,512]{1,0:T(8,128)(2,1)} %get-tuple-element.32), channel_id=1, source_target_pairs={{0,4},{2,6},{4,0},{6,2},{8,12},{10,14},{12,8},{14,10},{1,5},{3,7},... | collective-permute-start | bytes 786440 | tf_op jit(solution)/shard_map/ppermute | solution.py:290
  77.2 4.2 %copy-start.4 = (bf16[136,768]{1,0:T(8,128)(2,1)}, bf16[136,768]{1,0:T(8,128)(2,1)S(1)}, u32[]{:S(2)}) copy-start(bf16[136,768]{1,0:T(8,128)(2,1)S(1)} %collective-permute-done.rest_1_) | copy-start | bytes 626692
  77.2 15.7 %collective-permute-start.13 = (bf16[256,512]{1,0:T(8,128)(2,1)}, bf16[256,512]{1,0:T(8,128)(2,1)S(1)}, u32[]{:S(2)}, u32[]{:S(2)}) collective-permute-start(bf16[256,512]{1,0:T(8,128)(2,1)} %get-tuple-element.33), channel_id=1, source_target_pairs={{0,6},{2,4},{4,2},{6,0},{8,14},{10,12},{12,10},{14,8},{1,7},{3,5},... | collective-permute-start | bytes 786440 | tf_op jit(solution)/shard_map/ppermute | solution.py:290
  79.3 0.7 copy-start.17
  80.0 0.7 copy-start.18
  81.4 0.7 copy-start.5
  82.0 0.7 copy-start.6
  92.4 4.9 %collective-permute-start.10 = (bf16[64,512]{1,0:T(8,128)(2,1)}, bf16[64,512]{1,0:T(8,128)(2,1)S(1)}, u32[]{:S(2)}, u32[]{:S(2)}) collective-permute-start(bf16[64,512]{1,0:T(8,128)(2,1)} %get-tuple-element.29.own_ref), channel_id=1, source_target_pairs={{0,8},{2,10},{4,12},{6,14},{8,0},{10,2},{12,4},{14,6},{1,9},{3,11}... | collective-permute-start | bytes 196616 | tf_op jit(solution)/shard_map/ppermute | solution.py:290
  93.0 4.3 %copy-start.1 = (bf16[256,512]{1,0:T(8,128)(2,1)}, bf16[256,512]{1,0:T(8,128)(2,1)S(1)}, u32[]{:S(2)}) copy-start(bf16[256,512]{1,0:T(8,128)(2,1)S(1)} %collective-permute-done.11.rest_1_) | copy-start | bytes 786436
  93.0 4.3 %copy-start.2 = (bf16[256,512]{1,0:T(8,128)(2,1)}, bf16[256,512]{1,0:T(8,128)(2,1)S(1)}, u32[]{:S(2)}) copy-start(bf16[256,512]{1,0:T(8,128)(2,1)S(1)} %collective-permute-done.12.rest_2_) | copy-start | bytes 786436
  93.0 4.3 %copy-start.3 = (bf16[256,512]{1,0:T(8,128)(2,1)}, bf16[256,512]{1,0:T(8,128)(2,1)S(1)}, u32[]{:S(2)}) copy-start(bf16[256,512]{1,0:T(8,128)(2,1)S(1)} %collective-permute-done.13.rest_3_) | copy-start | bytes 786436
  97.3 0.6 copy-start.14
  97.9 6.4 %copy-start.21 = (bf16[128,512]{1,0:T(8,128)(2,1)S(1)}, bf16[128,512]{1,0:T(8,128)(2,1)}, u32[]{:S(2)}) copy-start(bf16[128,512]{1,0:T(8,128)(2,1)} %get-tuple-element.26) | copy-start | bytes 393220
  97.9 6.6 %copy-start.20 = (bf16[128,512]{1,0:T(8,128)(2,1)S(1)}, bf16[128,512]{1,0:T(8,128)(2,1)}, u32[]{:S(2)}) copy-start(bf16[128,512]{1,0:T(8,128)(2,1)} %get-tuple-element.27) | copy-start | bytes 393220
  97.9 6.6 %copy-start.19 = (bf16[128,512]{1,0:T(8,128)(2,1)S(1)}, bf16[128,512]{1,0:T(8,128)(2,1)}, u32[]{:S(2)}) copy-start(bf16[128,512]{1,0:T(8,128)(2,1)} %get-tuple-element.28) | copy-start | bytes 393220
  100.5 6.4 %collective-permute-start.14 = (f32[64,1024]{1,0:T(8,128)}, f32[64,1024]{1,0:T(8,128)S(1)}, u32[]{:S(2)}, u32[]{:S(2)}) collective-permute-start(f32[64,1024]{1,0:T(8,128)} %get-tuple-element.35), channel_id=1, source_target_pairs={{0,1},{1,0},{2,3},{3,2},{4,5},{5,4},{6,7},{7,6},{8,9},{9,8},{10,11... | collective-permute-start | bytes 786440 | tf_op jit(solution)/shard_map/ppermute | solution.py:311
  104.3 9.7 %collective-permute-start.7 = (bf16[128,512]{1,0:T(8,128)(2,1)S(1)}, bf16[128,512]{1,0:T(8,128)(2,1)S(1)}, u32[]{:S(2)}, u32[]{:S(2)}) collective-permute-start(bf16[128,512]{1,0:T(8,128)(2,1)S(1)} %copy-done.21), channel_id=1, source_target_pairs={{0,2},{2,0},{4,6},{6,4},{8,10},{10,8},{12,14},{14,12},{1,3},{3,1},... | collective-permute-start | bytes 393224 | tf_op jit(solution)/shard_map/ppermute | solution.py:290
  104.6 11.1 %collective-permute-start.8 = (bf16[128,512]{1,0:T(8,128)(2,1)S(1)}, bf16[128,512]{1,0:T(8,128)(2,1)S(1)}, u32[]{:S(2)}, u32[]{:S(2)}) collective-permute-start(bf16[128,512]{1,0:T(8,128)(2,1)S(1)} %copy-done.20), channel_id=1, source_target_pairs={{0,4},{2,6},{4,0},{6,2},{8,12},{10,14},{12,8},{14,10},{1,5},{3,7},... | collective-permute-start | bytes 393224 | tf_op jit(solution)/shard_map/ppermute | solution.py:290
  104.6 13.8 %collective-permute-start.9 = (bf16[128,512]{1,0:T(8,128)(2,1)S(1)}, bf16[128,512]{1,0:T(8,128)(2,1)S(1)}, u32[]{:S(2)}, u32[]{:S(2)}) collective-permute-start(bf16[128,512]{1,0:T(8,128)(2,1)S(1)} %copy-done.19), channel_id=1, source_target_pairs={{0,6},{2,4},{4,2},{6,0},{8,14},{10,12},{12,10},{14,8},{1,7},{3,5},... | collective-permute-start | bytes 393224 | tf_op jit(solution)/shard_map/ppermute | solution.py:290
  106.9 0.7 copy-start
  109.3 26.8 %collective-permute-start.15 = (bf16[16,1024]{1,0:T(8,128)(2,1)}, bf16[16,1024]{1,0:T(8,128)(2,1)S(1)}, u32[]{:S(2)}, u32[]{:S(2)}) collective-permute-start(bf16[16,1024]{1,0:T(8,128)(2,1)} %get-tuple-element.36), channel_id=1, source_target_pairs={{0,0},{1,8},{2,2},{3,10},{4,4},{5,12},{6,6},{7,14},{8,1},{9,9},{10... | collective-permute-start | bytes 98312 | tf_op jit(solution)/shard_map/ppermute | solution.py:320
  111.6 24.5 %collective-permute-start.16 = (bf16[16,1024]{1,0:T(8,128)(2,1)}, bf16[16,1024]{1,0:T(8,128)(2,1)S(1)}, u32[]{:S(2)}, u32[]{:S(2)}) collective-permute-start(bf16[16,1024]{1,0:T(8,128)(2,1)} %get-tuple-element.37), channel_id=1, source_target_pairs={{0,2},{1,10},{2,0},{3,8},{4,6},{5,14},{6,4},{7,12},{8,3},{9,11},{1... | collective-permute-start | bytes 98312 | tf_op jit(solution)/shard_map/ppermute | solution.py:320
  113.9 4.5 %copy-start.7 = (bf16[128,512]{1,0:T(8,128)(2,1)}, bf16[128,512]{1,0:T(8,128)(2,1)S(1)}, u32[]{:S(2)}) copy-start(bf16[128,512]{1,0:T(8,128)(2,1)S(1)} %collective-permute-done.7.rest_1_) | copy-start | bytes 393220
  113.9 22.2 %collective-permute-start.17 = (bf16[16,1024]{1,0:T(8,128)(2,1)}, bf16[16,1024]{1,0:T(8,128)(2,1)S(1)}, u32[]{:S(2)}, u32[]{:S(2)}) collective-permute-start(bf16[16,1024]{1,0:T(8,128)(2,1)} %get-tuple-element.38), channel_id=1, source_target_pairs={{0,4},{1,12},{2,6},{3,14},{4,0},{5,8},{6,2},{7,10},{8,5},{9,13},{1... | collective-permute-start | bytes 98312 | tf_op jit(solution)/shard_map/ppermute | solution.py:320
  115.6 2.8 %copy-start.8 = (bf16[128,512]{1,0:T(8,128)(2,1)}, bf16[128,512]{1,0:T(8,128)(2,1)S(1)}, u32[]{:S(2)}) copy-start(bf16[128,512]{1,0:T(8,128)(2,1)S(1)} %collective-permute-done.8.rest_2_) | copy-start | bytes 393220
  115.6 20.5 %collective-permute-start.18 = (bf16[16,1024]{1,0:T(8,128)(2,1)}, bf16[16,1024]{1,0:T(8,128)(2,1)S(1)}, u32[]{:S(2)}, u32[]{:S(2)}) collective-permute-start(bf16[16,1024]{1,0:T(8,128)(2,1)} %get-tuple-element.39), channel_id=1, source_target_pairs={{0,6},{1,14},{2,4},{3,12},{4,2},{5,10},{6,0},{7,8},{8,7},{9,15},{1... | collective-permute-start | bytes 98312 | tf_op jit(solution)/shard_map/ppermute | solution.py:320
  118.4 0.7 copy-start.9

commit v2 on v1

--- a/solution.py
+++ b/solution.py
@@ -16,7 +16,6 @@
 PAD_ROWS = 8
 MASKED = -1e30
 
-ANY = pl.BlockSpec(memory_space=pl.ANY)
 SMEM = pl.BlockSpec(memory_space=pltpu.SMEM)
 VMEM = pl.BlockSpec(memory_space=pltpu.VMEM)
 
@@ -25,81 +24,64 @@
     return [(i, i ^ k) for i in range(size)]
 
 
-def pack_heads(shard_index, query, key, value, kept_rows, heads):
+def in_vmem(x):
+    return pltpu.with_memory_space_constraint(x, pltpu.VMEM)
+
+
+def pack_heads(meta, query, key, value, kept_rows, heads):
     length = query.shape[0]
     width = query.shape[1] // heads
     hd = HEAD_SIZE
     capacity = kept_rows.shape[1]
     total = 2 * hd + width
 
-    def body(c_ref, q_ref, k_ref, v_ref, kept_ref, *rest):
-        out, (kept_buf, sems) = rest[:heads], rest[heads:]
-        slot = c_ref[0] % heads
-        copies = []
+    def body(meta_ref, q_ref, k_ref, v_ref, kept_ref, *out):
+        slot = meta_ref[0] % heads
+        kept = jnp.zeros((PAD_ROWS, total), jnp.bfloat16)
         for j in range(heads):
             head = slot ^ j
             q_at = pl.multiple_of(head * width, hd)
             k_at = pl.multiple_of(head * hd, hd)
-            copies += [
-                (k_ref.at[:, pl.ds(k_at, hd)], out[j].at[pl.ds(0, length), pl.ds(0, hd)]),
-                (v_ref.at[:, pl.ds(k_at, hd)], out[j].at[pl.ds(0, length), pl.ds(hd, hd)]),
-                (q_ref.at[:, pl.ds(q_at, width)], out[j].at[pl.ds(0, length), pl.ds(2 * hd, width)]),
-            ]
-        started = []
-        for number, (source, target) in enumerate(copies):
-            copy = pltpu.make_async_copy(source, target, sems.at[number])
-            copy.start()
-            started.append(copy)
-        kept_buf[...] = jnp.zeros(kept_buf.shape, jnp.bfloat16)
-        kept_buf[0:1, 0:capacity] = kept_ref[...].astype(jnp.float32).astype(jnp.bfloat16)
-        for j in range(heads):
-            copy = pltpu.make_async_copy(
-                kept_buf, out[j].at[pl.ds(length, PAD_ROWS)], sems.at[len(copies) + j]
+            k, v = k_ref[:, pl.ds(k_at, hd)], v_ref[:, pl.ds(k_at, hd)]
+            out[j][0:length, 0:hd] = k
+            out[j][0:length, hd : 2 * hd] = v
+            out[j][0:length, 2 * hd :] = q_ref[:, pl.ds(q_at, width)]
+            out[j][length:, :] = kept
+            out[j][length : length + 1, 0:capacity] = (
+                kept_ref[...].astype(jnp.float32).astype(jnp.bfloat16)
             )
-            copy.start()
-            started.append(copy)
-        for copy in started:
-            copy.wait()
+            out[heads + j][:, 0:hd] = k
+            out[heads + j][:, hd:] = v
 
     return pl.pallas_call(
         body,
-        out_shape=[jax.ShapeDtypeStruct((length + PAD_ROWS, total), jnp.bfloat16)] * heads,
-        in_specs=[SMEM, ANY, ANY, ANY, VMEM],
-        out_specs=[ANY] * heads,
-        scratch_shapes=[
-            pltpu.VMEM((PAD_ROWS, total), jnp.bfloat16),
-            pltpu.SemaphoreType.DMA((4 * heads,)),
-        ],
+        out_shape=[pltpu.VMEM((length + PAD_ROWS, total), jnp.bfloat16)] * heads
+        + [pltpu.VMEM((length, 2 * hd), jnp.bfloat16)] * heads,
+        in_specs=[SMEM] + [VMEM] * 4,
+        out_specs=[VMEM] * (2 * heads),
         name="pack_heads",
-    )(shard_index, query, key, value, kept_rows)
-
-
-def pack_weight(shard_index, weight, heads):
+    )(meta, query, key, value, kept_rows)
+
+
+def pack_weight(meta, weight, heads):
     width = weight.shape[1] // heads
 
-    def body(c_ref, w_ref, *rest):
-        out, sems = rest[:heads], rest[heads]
-        slot = c_ref[0] % heads
-        copies = []
+    def body(meta_ref, w_ref, *out):
+        slot = meta_ref[0] % heads
         for j in range(heads):
             at = pl.multiple_of((slot ^ j) * width, HEAD_SIZE)
-            copies.append(pltpu.make_async_copy(w_ref.at[:, pl.ds(at, width)], out[j], sems.at[j]))
-        for copy in copies:
-            copy.start()
-        for copy in copies:
-            copy.wait()
+            out[j][...] = w_ref[:, pl.ds(at, width)]
 
     return pl.pallas_call(
         body,
-        out_shape=[jax.ShapeDtypeStruct((weight.shape[0], width), jnp.bfloat16)] * heads,
-        in_specs=[SMEM, ANY],
-        out_specs=[ANY] * heads,
-        scratch_shapes=[pltpu.SemaphoreType.DMA((heads,))],
+        out_shape=[pltpu.VMEM((weight.shape[0], width), jnp.bfloat16)] * heads,
+        in_specs=[SMEM, VMEM],
+        out_specs=[VMEM] * heads,
         name="pack_weight",
-    )(shard_index, weight)
-
-
-def attention(shard_index, slash, tiles, counts, near, far, keep_rows):
+    )(meta, weight)
+
+
+def attention(meta, offsets_at, tiles_at, counts_at, near, far, keep_rows):
     heads = len(near)
     pieces = heads + len(far)
     length = near[0].shape[0] - PAD_ROWS
@@ -109,14 +91,14 @@
     block_rows = heads * keep_rows
     factor = hd ** (-0.5) * math.log2(math.e)
 
-    def body(c_ref, slash_ref, tile_ref, count_ref, *rest):
+    def body(meta_ref, *rest):
         near_refs, rest = rest[:heads], rest[heads:]
         far_refs, rest = rest[: len(far)], rest[len(far) :]
         out_refs, rows_ref = rest[:heads], rest[heads]
         k_all, v_all, bias = rest[heads + 1 :]
-        c = c_ref[0]
+        c = meta_ref[0]
         slot = c % heads
-        first = c - slot
+        first = counts_at + c - slot
         for k in range(pieces):
             ref = near_refs[k] if k < heads else far_refs[k - heads]
             k_all[k * length : (k + 1) * length, :] = ref[0:length, 0:hd]
@@ -124,8 +106,8 @@
         difference = lax.broadcasted_iota(jnp.int32, (length, length), 0) - lax.broadcasted_iota(
             jnp.int32, (length, length), 1
         )
-        offsets = [slash_ref[slot, i] for i in range(slash_ref.shape[1])]
-        verticals = [tile_ref[slot, i] for i in range(tile_ref.shape[1])]
+        offsets = [meta_ref[offsets_at + i * heads + slot] for i in range(2)]
+        verticals = [meta_ref[tiles_at + i * heads + slot] for i in range(VTILES)]
         rows = jnp.zeros((block_rows, width), jnp.float32)
         for q in range(heads):
             q_shard = c ^ q
@@ -158,13 +140,13 @@
             q_slot = slot ^ q
             before = jnp.int32(0)
             for s in range(heads):
-                before = before + jnp.where(s < q_slot, count_ref[first + s], 0)
+                before = before + jnp.where(s < q_slot, meta_ref[first + s], 0)
             kept = near_refs[q][length : length + 1, 0:hd].astype(jnp.float32).astype(jnp.int32)
             token = lax.broadcasted_iota(jnp.int32, (length, hd), 0)
             is_token = (token == kept).astype(jnp.float32).astype(jnp.bfloat16)
             index = lax.broadcasted_iota(jnp.int32, (hd, block_rows), 0)
             place = lax.broadcasted_iota(jnp.int32, (hd, block_rows), 1)
-            is_place = ((place - index == before) & (index < count_ref[q_shard])).astype(jnp.float32)
+            is_place = ((place - index == before) & (index < meta_ref[counts_at + q_shard])).astype(jnp.float32)
             chooser = jnp.dot(
                 is_token, is_place.astype(jnp.bfloat16), preferred_element_type=jnp.float32
             ).astype(jnp.bfloat16)
@@ -178,9 +160,9 @@
 
     return pl.pallas_call(
         body,
-        out_shape=[jax.ShapeDtypeStruct((length, width), jnp.bfloat16)] * heads
-        + [jax.ShapeDtypeStruct((block_rows, width), jnp.bfloat16)],
-        in_specs=[SMEM] * 4 + [VMEM] * pieces,
+        out_shape=[pltpu.VMEM((length, width), jnp.bfloat16)] * heads
+        + [pltpu.VMEM((block_rows, width), jnp.bfloat16)],
+        in_specs=[SMEM] + [VMEM] * pieces,
         out_specs=[VMEM] * (heads + 1),
         scratch_shapes=[
             pltpu.VMEM((pieces * length, hd), jnp.bfloat16),
@@ -188,18 +170,18 @@
             pltpu.VMEM((length, pieces * length), jnp.float32),
         ],
         name="attention",
-    )(shard_index, slash, tiles, counts, *near, *far)
-
-
-def project(where, own_rows, other_rows, weights):
+    )(meta, *near, *far)
+
+
+def project(meta, own_rows, other_rows, weights):
     heads = len(weights)
     count = own_rows.shape[0]
     outs = weights[0].shape[0]
 
-    def body(where_ref, own_ref, other_ref, *rest):
+    def body(meta_ref, own_ref, other_ref, *rest):
         w_refs, (keep_ref, send_ref) = rest[:heads], rest[heads:]
-        slot = where_ref[0] % heads
-        keeps_own = where_ref[0] // heads == where_ref[1]
+        slot = meta_ref[0] % heads
+        keeps_own = meta_ref[0] // heads == meta_ref[1]
         own, other = own_ref[...], other_ref[...]
         both = jnp.concatenate(
             [jnp.where(keeps_own, own, other), jnp.where(keeps_own, other, own)], 0
@@ -214,18 +196,18 @@
 
     return pl.pallas_call(
         body,
-        out_shape=[jax.ShapeDtypeStruct((count, heads * outs), jnp.float32)] * 2,
+        out_shape=[pltpu.VMEM((count, heads * outs), jnp.float32)] * 2,
         in_specs=[SMEM] + [VMEM] * (2 + heads),
         out_specs=[VMEM] * 2,
         name="project",
-    )(where, own_rows, other_rows, *weights)
-
-
-def split_rows(shard_index, kept, received, heads):
+    )(meta, own_rows, other_rows, *weights)
+
+
+def split_rows(meta, kept, received, heads):
     keep_rows = kept.shape[0] // heads
 
-    def body(c_ref, a_ref, b_ref, *out):
-        slot = c_ref[0] % heads
+    def body(meta_ref, a_ref, b_ref, *out):
+        slot = meta_ref[0] % heads
         for j in range(heads):
             at = pl.multiple_of((slot ^ j) * keep_rows, 8)
             out[j][...] = (a_ref[pl.ds(at, keep_rows), :] + b_ref[pl.ds(at, keep_rows), :]).astype(
@@ -234,39 +216,30 @@
 
     return pl.pallas_call(
         body,
-        out_shape=[jax.ShapeDtypeStruct((keep_rows, kept.shape[1]), jnp.bfloat16)] * heads,
+        out_shape=[pltpu.VMEM((keep_rows, kept.shape[1]), jnp.bfloat16)] * heads,
         in_specs=[SMEM, VMEM, VMEM],
         out_specs=[VMEM] * heads,
         name="split_rows",
-    )(shard_index, kept, received)
-
-
-def join_heads(shard_index, pieces):
+    )(meta, kept, received)
+
+
+def join_heads(meta, pieces):
     heads = len(pieces)
     length, width = pieces[0].shape
 
-    def body(c_ref, *rest):
-        ins, (out_ref, sems) = rest[:heads], rest[heads:]
-        slot = c_ref[0] % heads
-        copies = []
+    def body(meta_ref, *rest):
+        slot = meta_ref[0] % heads
         for j in range(heads):
             at = pl.multiple_of((slot ^ j) * width, HEAD_SIZE)
-            copies.append(
-                pltpu.make_async_copy(ins[j], out_ref.at[:, pl.ds(at, width)], sems.at[j])
-            )
-        for copy in copies:
-            copy.start()
-        for copy in copies:
-            copy.wait()
+            rest[heads][:, pl.ds(at, width)] = rest[j][...]
 
     return pl.pallas_call(
         body,
         out_shape=jax.ShapeDtypeStruct((length, heads * width), jnp.bfloat16),
-        in_specs=[SMEM] + [ANY] * heads,
-        out_specs=ANY,
-        scratch_shapes=[pltpu.SemaphoreType.DMA((heads,))],
+        in_specs=[SMEM] + [VMEM] * heads,
+        out_specs=VMEM,
         name="join_heads",
-    )(shard_index, *pieces)
+    )(meta, *pieces)
 
 
 def local_blocks(
@@ -284,32 +257,37 @@
     heads = key_tensor.shape[1] // HEAD_SIZE
     keep_rows = query_tensor.shape[0] // 8
     c = lax.axis_index("ctx").astype(jnp.int32)
-    shard_index = c.reshape(1)
+    h = lax.axis_index("head").astype(jnp.int32)
+    tables = [jnp.stack([c, h]), slash_offsets.T.reshape(-1), vertical_tiles.T.reshape(-1), kept_count]
+    meta = jnp.concatenate(tables)
+    offsets_at = 2
+    tiles_at = offsets_at + slash_offsets.size
+    counts_at = tiles_at + vertical_tiles.size
 
     def swap(x, k):
-        return lax.ppermute(x, "ctx", xor_pairs(size, k))
-
-    packed = pack_heads(shard_index, query_tensor, key_tensor, value_tensor, kept_rows, heads)
-    near = [packed[0]] + [swap(packed[k], k) for k in range(1, heads)]
-    key_values = [x[: query_tensor.shape[0], : 2 * HEAD_SIZE] for x in packed]
+        return in_vmem(lax.ppermute(x, "ctx", xor_pairs(size, k)))
+
+    packed = pack_heads(c.reshape(1), query_tensor, key_tensor, value_tensor, kept_rows, heads)
+    near = [in_vmem(packed[0])] + [swap(packed[k], k) for k in range(1, heads)]
     far = [
-        lax.ppermute(
-            key_values[k % heads], "ctx", [(i, i ^ k) for i in range(size) if i // heads < (i ^ k) // heads]
+        in_vmem(
+            lax.ppermute(
+                packed[heads + k % heads],
+                "ctx",
+                [(i, i ^ k) for i in range(size) if i // heads < (i ^ k) // heads],
+            )
         )
         for k in range(heads, size)
     ]
-    packed_weight = pack_weight(shard_index, out_weight, heads)
-    weights = [packed_weight[0]] + [swap(packed_weight[k], k) for k in range(1, heads)]
-    *mixed, rows = attention(
-        shard_index, slash_offsets, vertical_tiles, kept_count, near, far, keep_rows
-    )
+    packed_weight = pack_weight(c.reshape(1), out_weight, heads)
+    weights = [in_vmem(packed_weight[0])] + [swap(packed_weight[k], k) for k in range(1, heads)]
+    *mixed, rows = attention(meta, offsets_at, tiles_at, counts_at, near, far, keep_rows)
     other_rows = swap(rows, heads)
-    returned = [mixed[0]] + [swap(mixed[k], k) for k in range(1, heads)]
-    attended = join_heads(shard_index, returned)
-    where = jnp.stack([c, lax.axis_index("head").astype(jnp.int32)])
-    kept, sent = project(where, rows, other_rows, weights)
-    received = lax.ppermute(sent, "head", [(i, cores - 1 - i) for i in range(cores)])
-    shares = split_rows(shard_index, kept, received, heads)
+    returned = [in_vmem(mixed[0])] + [swap(mixed[k], k) for k in range(1, heads)]
+    attended = join_heads(meta, returned)
+    kept, sent = project(meta, in_vmem(rows), other_rows, weights)
+    received = in_vmem(lax.ppermute(sent, "head", [(i, cores - 1 - i) for i in range(cores)]))
+    shares = split_rows(meta, in_vmem(kept), received, heads)
     total = jnp.zeros(shares[0].shape, jnp.float32)
     for k in range(heads):
         pairs = []

time: 137 us -> 63.3 us (0.46)
  the two profiles are of different devices: /device:TPU:1 before, /device:TPU:9 now
where the time goes in v2:
time: 63.3 us; the launch traced here: 62.9 us
  starting transfers between devices  34.2 us (54%)
  Pallas kernels  16.2 us (26%)
  waiting for transfers between devices  8.3 us (13%)
  local copies, waits for them, and re-layouts  2.84 us (4%)
  between operations  0.73 us (1%)
    ppermute x10, starting transfers between devices, swap(): return in_vmem(lax.ppermute(x, 'ctx', xor_pairs(size, k)))  11.1 us
    ppermute x4, starting transfers between devices, local_blocks(): lax.ppermute(shares[k], ('ctx', 'head'), pairs).astype(jnp.float32)  10.2 us
    pallas_call x1, Pallas kernels, attention(): pl.pallas_call(body, out_shape=[pltpu.VMEM((length, width), jnp.bfloat16)...  8.84 us
    ppermute x4, starting transfers between devices, local_blocks(): lax.ppermute(packed[heads + k % heads], 'ctx', [(i, i ^ k) for i in range...  8.08 us
    ppermute x1, starting transfers between devices, local_blocks(): lax.ppermute(sent, 'head', [(i, cores - 1 - i) for i in range(cores)])  4.88 us
    ppermute x4, waiting for transfers between devices, local_blocks(): lax.ppermute(packed[heads + k % heads], 'ctx', [(i, i ^ k) for i in range...  3.49 us
    ppermute x4, waiting for transfers between devices, local_blocks(): lax.ppermute(shares[k], ('ctx', 'head'), pairs).astype(jnp.float32)  2.67 us
    ppermute x10, waiting for transfers between devices, swap(): return in_vmem(lax.ppermute(x, 'ctx', xor_pairs(size, k)))  2.15 us
  transfers between devices with their start and end apart: 19, of which 5 were waited for; matrix products, arithmetic and copies ran while one was open for 1% of the time, Pallas kernels for 21%

profile of v2, /device:TPU:9, one launch (start us, length us, event | category | flops | bytes accessed | tf_op | source)
XLA Modules:
  0.0 62.9 jit_solution(13016557435273693083)
XLA Ops:
  0.6 1.9 %pack_heads.1 = (bf16[136,768]{1,0:T(8,128)(2,1)S(1)}, bf16[136,768]{1,0:T(8,128)(2,1)S(1)}, bf16[136,768]{1,0:T(8,128)(2,1)}, bf16[136,768]{1,0:T(8,128)(2,1)S(...) custom-call(s32[1]{0:T(128)} %bitcast.meta_ref, ...), custom_call_target="tpu_custom_call" | custom-call | tf_op jit(solution)/shard_map/pack_heads/pallas_call | solution.py:56
  2.6 1.2 %collective-permute-start = (bf16[136,768]{1,0:T(8,128)(2,1)S(1)}, bf16[136,768]{1,0:T(8,128)(2,1)S(1)}, u32[]{:S(2)}, u32[]{:S(2)}) collective-permute-start(bf16[136,768]{1,0:T(8,128)(2,1)S(1)} %get-tuple-element.26), channel_id=1, source_target_pairs={{0,2},{2,0},{4,6},{6,4},{8,10},{10,8},{12,14},{14,12},{1,3},{3,1},... | collective-permute-start | bytes 626696 | tf_op jit(solution)/shard_map/ppermute | solution.py:268
  3.8 4.2 %collective-permute-start.3 = (bf16[128,256]{1,0:T(8,128)(2,1)S(1)}, bf16[128,256]{1,0:T(8,128)(2,1)S(1)}, u32[]{:S(2)}, u32[]{:S(2)}) collective-permute-start(bf16[128,256]{1,0:T(8,128)(2,1)S(1)} %get-tuple-element.29), channel_id=1, source_target_pairs={{0,8},{2,10},{4,12},{6,14},{1,9},{3,11},{5,13},{7,15},{16,24},{18,... | collective-permute-start | bytes 196616 | tf_op jit(solution)/shard_map/ppermute | solution.py:274
  8.0 1.3 %collective-permute-start.4 = (bf16[128,256]{1,0:T(8,128)(2,1)S(1)}, bf16[128,256]{1,0:T(8,128)(2,1)S(1)}, u32[]{:S(2)}, u32[]{:S(2)}) collective-permute-start(bf16[128,256]{1,0:T(8,128)(2,1)S(1)} %get-tuple-element.30), channel_id=1, source_target_pairs={{0,10},{2,8},{4,14},{6,12},{1,11},{3,9},{5,15},{7,13},{16,26},{18,... | collective-permute-start | bytes 196616 | tf_op jit(solution)/shard_map/ppermute | solution.py:274
  9.3 1.3 %collective-permute-start.5 = (bf16[128,256]{1,0:T(8,128)(2,1)S(1)}, bf16[128,256]{1,0:T(8,128)(2,1)S(1)}, u32[]{:S(2)}, u32[]{:S(2)}) collective-permute-start(bf16[128,256]{1,0:T(8,128)(2,1)S(1)} %get-tuple-element.31), channel_id=1, source_target_pairs={{0,12},{2,14},{4,8},{6,10},{1,13},{3,15},{5,9},{7,11},{16,28},{18,... | collective-permute-start | bytes 196616 | tf_op jit(solution)/shard_map/ppermute | solution.py:274
  10.6 1.3 %collective-permute-start.6 = (bf16[128,256]{1,0:T(8,128)(2,1)S(1)}, bf16[128,256]{1,0:T(8,128)(2,1)S(1)}, u32[]{:S(2)}, u32[]{:S(2)}) collective-permute-start(bf16[128,256]{1,0:T(8,128)(2,1)S(1)} %get-tuple-element.32), channel_id=1, source_target_pairs={{0,14},{2,12},{4,10},{6,8},{1,15},{3,13},{5,11},{7,9},{16,30},{18,... | collective-permute-start | bytes 196616 | tf_op jit(solution)/shard_map/ppermute | solution.py:274
  11.9 0.0 collective-permute-done.3.rest_4_
  11.9 1.2 %collective-permute-start.1 = (bf16[136,768]{1,0:T(8,128)(2,1)}, bf16[136,768]{1,0:T(8,128)(2,1)S(1)}, u32[]{:S(2)}, u32[]{:S(2)}) collective-permute-start(bf16[136,768]{1,0:T(8,128)(2,1)} %get-tuple-element.27), channel_id=1, source_target_pairs={{0,4},{2,6},{4,0},{6,2},{8,12},{10,14},{12,8},{14,10},{1,5},{3,7},... | collective-permute-start | bytes 626696 | tf_op jit(solution)/shard_map/ppermute | solution.py:268
  13.1 2.4 %collective-permute-done.4.rest_5_ = bf16[128,256]{1,0:T(8,128)(2,1)S(1)} collective-permute-done((bf16[128,256]{1,0:T(8,128)(2,1)S(1)}, bf16[128,256]{1,0:T(8,128)(2,1)S(1)}, u32[]{:S(2)}, u32[]{:S(2)}) %collective-permute-start.4) | collective-permute-done | bytes 65568 | tf_op jit(solution)/shard_map/ppermute | solution.py:274
  15.5 0.0 collective-permute-start.2
  15.5 2.1 %pack_weight.1 = (bf16[256,512]{1,0:T(8,128)(2,1)S(1)}, bf16[256,512]{1,0:T(8,128)(2,1)}, bf16[256,512]{1,0:T(8,128)(2,1)}, bf16[256,512]{1,0:T(8,128)(2,1)S(1)}) custom-call(s32[1]{0:T(128)} %bitcast.meta_ref, bf16[256,2048]{1,0:T(8,128)(2,1)} %w_ref.1), custom_call_target="tpu_custom_call" | custom-call | tf_op jit(solution)/shard_map/pack_weight/pallas_call | solution.py:75
  17.6 0.0 collective-permute-done.5.rest_6_
  17.6 0.2 collective-permute-start.11
  17.8 1.1 %collective-permute-done.6.rest_7_ = bf16[128,256]{1,0:T(8,128)(2,1)S(1)} collective-permute-done((bf16[128,256]{1,0:T(8,128)(2,1)S(1)}, bf16[128,256]{1,0:T(8,128)(2,1)S(1)}, u32[]{:S(2)}, u32[]{:S(2)}) %collective-permute-start.6) | collective-permute-done | bytes 65568 | tf_op jit(solution)/shard_map/ppermute | solution.py:274
  18.9 1.3 %collective-permute-start.12 = (bf16[256,512]{1,0:T(8,128)(2,1)}, bf16[256,512]{1,0:T(8,128)(2,1)S(1)}, u32[]{:S(2)}, u32[]{:S(2)}) collective-permute-start(bf16[256,512]{1,0:T(8,128)(2,1)} %get-tuple-element.40), channel_id=1, source_target_pairs={{0,4},{2,6},{4,0},{6,2},{8,12},{10,14},{12,8},{14,10},{1,5},{3,7},... | collective-permute-start | bytes 786440 | tf_op jit(solution)/shard_map/ppermute | solution.py:268
  20.3 0.0 collective-permute-done.rest_1_
  20.3 0.2 collective-permute-start.13
  20.5 0.7 %copy-done.1 = s32[4,2]{0,1:T(2,128)S(1)} copy-done((s32[4,2]{0,1:T(2,128)S(1)}, s32[4,2]{0,1:T(2,128)}, u32[]{:S(2)}) %copy-start.1) | copy-done | bytes 56
  21.2 0.1 reshape.12
  21.3 0.7 %copy-done.2 = s32[4,2]{0,1:T(2,128)S(1)} copy-done((s32[4,2]{0,1:T(2,128)S(1)}, s32[4,2]{0,1:T(2,128)}, u32[]{:S(2)}) %copy-start.2) | copy-done | bytes 56
  21.9 0.1 reshape.13
  22.0 0.7 %copy-done = s32[8]{0:T(128)S(1)} copy-done((s32[8]{0:T(128)S(1)}, s32[8]{0:T(128)}, u32[]{:S(2)}) %copy-start) | copy-done | bytes 56
  22.7 0.7 %concatenate.3.meta_ref = s32[26]{0:T(128)} concatenate(s32[1]{0:T(128)} %bitcast.meta_ref, s32[1]{0:T(128)} %bitcast.1, s32[8]{0:T(128)S(1)} %reshape.12, s32[8]{0:T(128)S(1)} %reshape.13, s32[8]{0:T(128)S(1)} %copy-done), dimensions={0} | concatenate | bytes 208 | tf_op jit(solution)/shard_map/concatenate | solution.py:262
  23.3 0.0 collective-permute-done.1.rest_2_
  23.3 0.3 collective-permute-done.2.rest_3_
  23.6 8.8 %attention.1 = (bf16[128,512]{1,0:T(8,128)(2,1)S(1)}, bf16[128,512]{1,0:T(8,128)(2,1)}, bf16[128,512]{1,0:T(8,128)(2,1)}, bf16[128,512]{1,0:T(8,128)(2,1)}, bf16[64,512]{1,0:T(8,128)(2,1)S(1)}) custom-call(s32[26]{0:T(128)} %concatenate.3.meta_ref, bf16[136,768]{1,0:T(8,128)(2,1)S(1)} %get-tuple-element.25.rest_0_, ...), custom_call_target="tpu_custom_call" | custom-call | tf_op jit(solution)/shard_map/attention/pallas_call | solution.py:161
  32.4 4.1 %collective-permute-start.10 = (bf16[64,512]{1,0:T(8,128)(2,1)S(1)}, bf16[64,512]{1,0:T(8,128)(2,1)S(1)}, u32[]{:S(2)}, u32[]{:S(2)}) collective-permute-start(bf16[64,512]{1,0:T(8,128)(2,1)S(1)} %get-tuple-element.37.own_ref), channel_id=1, source_target_pairs={{0,8},{2,10},{4,12},{6,14},{8,0},{10,2},{12,4},{14,6},{1,9},{3,11}... | collective-permute-start | bytes 196616 | tf_op jit(solution)/shard_map/ppermute | solution.py:268
  36.5 0.0 collective-permute-done.11.rest_1_
  36.5 0.0 collective-permute-done.12.rest_2_
  36.5 0.0 collective-permute-done.13.rest_3_
  36.5 1.9 %collective-permute-done.10.other_ref = bf16[64,512]{1,0:T(8,128)(2,1)S(1)} collective-permute-done((bf16[64,512]{1,0:T(8,128)(2,1)S(1)}, bf16[64,512]{1,0:T(8,128)(2,1)S(1)}, u32[]{:S(2)}, u32[]{:S(2)}) %collective-permute-start.10) | collective-permute-done | bytes 65568 | tf_op jit(solution)/shard_map/ppermute | solution.py:268
  38.4 1.1 %project.1 = (f32[64,1024]{1,0:T(8,128)S(1)}, f32[64,1024]{1,0:T(8,128)S(1)}) custom-call(s32[26]{0:T(128)} %concatenate.3.meta_ref, bf16[64,512]{1,0:T(8,128)(2,1)S(1)} %get-tuple-element.37.own_ref, bf16[64,512]{1,0:T(8,128)(2,1)S(1)} %collective-permute-done.10.other_ref, bf16[256,512]{1,0:T(8,128)(2,1)S(1)} %get-tuple-element.38.rest_0_, ...), custom_call_target="tpu_custom_call" | custom-call | tf_op jit(solution)/shard_map/project/pallas_call | solution.py:197
  39.5 4.9 %collective-permute-start.14 = (f32[64,1024]{1,0:T(8,128)S(1)}, f32[64,1024]{1,0:T(8,128)S(1)}, u32[]{:S(2)}, u32[]{:S(2)}) collective-permute-start(f32[64,1024]{1,0:T(8,128)S(1)} %get-tuple-element.43), channel_id=1, source_target_pairs={{0,1},{1,0},{2,3},{3,2},{4,5},{5,4},{6,7},{7,6},{8,9},{9,8},{10,11... | collective-permute-start | bytes 786440 | tf_op jit(solution)/shard_map/ppermute | solution.py:289
  44.4 1.6 %collective-permute-start.7 = (bf16[128,512]{1,0:T(8,128)(2,1)}, bf16[128,512]{1,0:T(8,128)(2,1)S(1)}, u32[]{:S(2)}, u32[]{:S(2)}) collective-permute-start(bf16[128,512]{1,0:T(8,128)(2,1)} %get-tuple-element.34), channel_id=1, source_target_pairs={{0,2},{2,0},{4,6},{6,4},{8,10},{10,8},{12,14},{14,12},{1,3},{3,1},... | collective-permute-start | bytes 393224 | tf_op jit(solution)/shard_map/ppermute | solution.py:268
  46.0 0.0 collective-permute-start.8
  46.0 1.2 %collective-permute-start.9 = (bf16[128,512]{1,0:T(8,128)(2,1)}, bf16[128,512]{1,0:T(8,128)(2,1)S(1)}, u32[]{:S(2)}, u32[]{:S(2)}) collective-permute-start(bf16[128,512]{1,0:T(8,128)(2,1)} %get-tuple-element.36), channel_id=1, source_target_pairs={{0,6},{2,4},{4,2},{6,0},{8,14},{10,12},{12,10},{14,8},{1,7},{3,5},... | collective-permute-start | bytes 393224 | tf_op jit(solution)/shard_map/ppermute | solution.py:268
  47.2 0.0 collective-permute-done.14.b_ref
  47.2 0.7 %split_rows.1 = (bf16[16,1024]{1,0:T(8,128)(2,1)S(1)}, bf16[16,1024]{1,0:T(8,128)(2,1)S(1)}, bf16[16,1024]{1,0:T(8,128)(2,1)S(1)}, bf16[16,1024]{1,0:T(8,128)(2,1)S(1)}) custom-call(s32[26]{0:T(128)} %concatenate.3.meta_ref, f32[64,1024]{1,0:T(8,128)S(1)} %get-tuple-element.42.a_ref, f32[64,1024]{1,0:T(8,128)S(1)} %collective-permute-done.14.b_ref), custom_call_target="tpu_custom_call" | custom-call | tf_op jit(solution)/shard_map/split_rows/pallas_call | solution.py:217
  47.9 3.2 %collective-permute-start.18 = (bf16[16,1024]{1,0:T(8,128)(2,1)S(1)}, bf16[16,1024]{1,0:T(8,128)(2,1)S(1)}, u32[]{:S(2)}, u32[]{:S(2)}) collective-permute-start(bf16[16,1024]{1,0:T(8,128)(2,1)S(1)} %get-tuple-element.47), channel_id=1, source_target_pairs={{0,6},{1,14},{2,4},{3,12},{4,2},{5,10},{6,0},{7,8},{8,7},{9,15},{1... | collective-permute-start | bytes 98312 | tf_op jit(solution)/shard_map/ppermute | solution.py:298
  51.2 5.0 %collective-permute-start.16 = (bf16[16,1024]{1,0:T(8,128)(2,1)S(1)}, bf16[16,1024]{1,0:T(8,128)(2,1)S(1)}, u32[]{:S(2)}, u32[]{:S(2)}) collective-permute-start(bf16[16,1024]{1,0:T(8,128)(2,1)S(1)} %get-tuple-element.45), channel_id=1, source_target_pairs={{0,2},{1,10},{2,0},{3,8},{4,6},{5,14},{6,4},{7,12},{8,3},{9,11},{1... | collective-permute-start | bytes 98312 | tf_op jit(solution)/shard_map/ppermute | solution.py:298
  56.2 0.0 collective-permute-done.8.rest_2_
  56.2 1.9 %collective-permute-start.15 = (bf16[16,1024]{1,0:T(8,128)(2,1)S(1)}, bf16[16,1024]{1,0:T(8,128)(2,1)S(1)}, u32[]{:S(2)}, u32[]{:S(2)}) collective-permute-start(bf16[16,1024]{1,0:T(8,128)(2,1)S(1)} %get-tuple-element.44), channel_id=1, source_target_pairs={{0,0},{1,8},{2,2},{3,10},{4,4},{5,12},{6,6},{7,14},{8,1},{9,9},{10... | collective-permute-start | bytes 98312 | tf_op jit(solution)/shard_map/ppermute | solution.py:298
  58.1 0.0 collective-permute-done.9.rest_3_
  58.1 1.5 %join_heads.1 = bf16[128,2048]{1,0:T(8,128)(2,1)} custom-call(s32[26]{0:T(128)} %concatenate.3.meta_ref, bf16[128,512]{1,0:T(8,128)(2,1)S(1)} %get-tuple-element.33.rest_0_, bf16[128,512]{1,0:T(8,128)(2,1)S(1)} %collective-permute-done.7.rest_1_, bf16[128,512]{1,0:T(8,128)(2,1)S(1)} %collective-permute-done.8.rest_2_, ...), custom_call_target="tpu_custom_call" | custom-call | tf_op jit(solution)/shard_map/join_heads/pallas_call | solution.py:236
  59.6 0.0 collective-permute-done.17
  59.6 0.0 collective-permute-done.16
  59.6 2.7 %collective-permute-done.15 = bf16[16,1024]{1,0:T(8,128)(2,1)S(1)} collective-permute-done((bf16[16,1024]{1,0:T(8,128)(2,1)S(1)}, bf16[16,1024]{1,0:T(8,128)(2,1)S(1)}, u32[]{:S(2)}, u32[]{:S(2)}) %collective-permute-start.15) | collective-permute-done | bytes 32800 | tf_op jit(solution)/shard_map/ppermute | solution.py:298
  62.3 0.6 %add_convert_fusion = bf16[16,1024]{1,0:T(8,128)(2,1)} fusion(bf16[16,1024]{1,0:T(8,128)(2,1)S(1)} %collective-permute-done.18, bf16[16,1024]{1,0:T(8,128)(2,1)S(1)} %collective-permute-done.17, bf16[16,1024]{1,0:T(8,128)(2,1)S(1)} %collective-permute-done.16, bf16[16,1024]{1,0:T(8,128)(2,1)S(1)} %collective-permute-done.15), kind=kLoop, calls=%fused_computation | loop fusion | flops 131072 | bytes 163840 | tf_op jit(solution)/shard_map/convert_element_type | solution.py:299
  (6 shorter events, 0.0 us)
Async XLA Ops:
  2.6 17.7 %collective-permute-start = (bf16[136,768]{1,0:T(8,128)(2,1)S(1)}, bf16[136,768]{1,0:T(8,128)(2,1)S(1)}, u32[]{:S(2)}, u32[]{:S(2)}) collective-permute-start(bf16[136,768]{1,0:T(8,128)(2,1)S(1)} %get-tuple-element.26), channel_id=1, source_target_pairs={{0,2},{2,0},{4,6},{6,4},{8,10},{10,8},{12,14},{14,12},{1,3},{3,1},... | collective-permute-start | bytes 626696 | tf_op jit(solution)/shard_map/ppermute | solution.py:268
  3.8 8.1 %collective-permute-start.3 = (bf16[128,256]{1,0:T(8,128)(2,1)S(1)}, bf16[128,256]{1,0:T(8,128)(2,1)S(1)}, u32[]{:S(2)}, u32[]{:S(2)}) collective-permute-start(bf16[128,256]{1,0:T(8,128)(2,1)S(1)} %get-tuple-element.29), channel_id=1, source_target_pairs={{0,8},{2,10},{4,12},{6,14},{1,9},{3,11},{5,13},{7,15},{16,24},{18,... | collective-permute-start | bytes 196616 | tf_op jit(solution)/shard_map/ppermute | solution.py:274
  8.0 7.5 %collective-permute-start.4 = (bf16[128,256]{1,0:T(8,128)(2,1)S(1)}, bf16[128,256]{1,0:T(8,128)(2,1)S(1)}, u32[]{:S(2)}, u32[]{:S(2)}) collective-permute-start(bf16[128,256]{1,0:T(8,128)(2,1)S(1)} %get-tuple-element.30), channel_id=1, source_target_pairs={{0,10},{2,8},{4,14},{6,12},{1,11},{3,9},{5,15},{7,13},{16,26},{18,... | collective-permute-start | bytes 196616 | tf_op jit(solution)/shard_map/ppermute | solution.py:274
  9.3 8.3 %collective-permute-start.5 = (bf16[128,256]{1,0:T(8,128)(2,1)S(1)}, bf16[128,256]{1,0:T(8,128)(2,1)S(1)}, u32[]{:S(2)}, u32[]{:S(2)}) collective-permute-start(bf16[128,256]{1,0:T(8,128)(2,1)S(1)} %get-tuple-element.31), channel_id=1, source_target_pairs={{0,12},{2,14},{4,8},{6,10},{1,13},{3,15},{5,9},{7,11},{16,28},{18,... | collective-permute-start | bytes 196616 | tf_op jit(solution)/shard_map/ppermute | solution.py:274
  10.6 8.3 %collective-permute-start.6 = (bf16[128,256]{1,0:T(8,128)(2,1)S(1)}, bf16[128,256]{1,0:T(8,128)(2,1)S(1)}, u32[]{:S(2)}, u32[]{:S(2)}) collective-permute-start(bf16[128,256]{1,0:T(8,128)(2,1)S(1)} %get-tuple-element.32), channel_id=1, source_target_pairs={{0,14},{2,12},{4,10},{6,8},{1,15},{3,13},{5,11},{7,9},{16,30},{18,... | collective-permute-start | bytes 196616 | tf_op jit(solution)/shard_map/ppermute | solution.py:274
  11.9 11.4 %collective-permute-start.1 = (bf16[136,768]{1,0:T(8,128)(2,1)}, bf16[136,768]{1,0:T(8,128)(2,1)S(1)}, u32[]{:S(2)}, u32[]{:S(2)}) collective-permute-start(bf16[136,768]{1,0:T(8,128)(2,1)} %get-tuple-element.27), channel_id=1, source_target_pairs={{0,4},{2,6},{4,0},{6,2},{8,12},{10,14},{12,8},{14,10},{1,5},{3,7},... | collective-permute-start | bytes 626696 | tf_op jit(solution)/shard_map/ppermute | solution.py:268
  15.5 8.1 %collective-permute-start.2 = (bf16[136,768]{1,0:T(8,128)(2,1)S(1)}, bf16[136,768]{1,0:T(8,128)(2,1)S(1)}, u32[]{:S(2)}, u32[]{:S(2)}) collective-permute-start(bf16[136,768]{1,0:T(8,128)(2,1)S(1)} %get-tuple-element.28), channel_id=1, source_target_pairs={{0,6},{2,4},{4,2},{6,0},{8,14},{10,12},{12,10},{14,8},{1,7},{3,5},... | collective-permute-start | bytes 626696 | tf_op jit(solution)/shard_map/ppermute | solution.py:268
  17.6 18.9 %collective-permute-start.11 = (bf16[256,512]{1,0:T(8,128)(2,1)}, bf16[256,512]{1,0:T(8,128)(2,1)S(1)}, u32[]{:S(2)}, u32[]{:S(2)}) collective-permute-start(bf16[256,512]{1,0:T(8,128)(2,1)} %get-tuple-element.39), channel_id=1, source_target_pairs={{0,2},{2,0},{4,6},{6,4},{8,10},{10,8},{12,14},{14,12},{1,3},{3,1},... | collective-permute-start | bytes 786440 | tf_op jit(solution)/shard_map/ppermute | solution.py:268
  18.9 17.6 %collective-permute-start.12 = (bf16[256,512]{1,0:T(8,128)(2,1)}, bf16[256,512]{1,0:T(8,128)(2,1)S(1)}, u32[]{:S(2)}, u32[]{:S(2)}) collective-permute-start(bf16[256,512]{1,0:T(8,128)(2,1)} %get-tuple-element.40), channel_id=1, source_target_pairs={{0,4},{2,6},{4,0},{6,2},{8,12},{10,14},{12,8},{14,10},{1,5},{3,7},... | collective-permute-start | bytes 786440 | tf_op jit(solution)/shard_map/ppermute | solution.py:268
  20.3 16.3 %collective-permute-start.13 = (bf16[256,512]{1,0:T(8,128)(2,1)S(1)}, bf16[256,512]{1,0:T(8,128)(2,1)S(1)}, u32[]{:S(2)}, u32[]{:S(2)}) collective-permute-start(bf16[256,512]{1,0:T(8,128)(2,1)S(1)} %get-tuple-element.41), channel_id=1, source_target_pairs={{0,6},{2,4},{4,2},{6,0},{8,14},{10,12},{12,10},{14,8},{1,7},{3,5},... | collective-permute-start | bytes 786440 | tf_op jit(solution)/shard_map/ppermute | solution.py:268
  20.5 0.7 %copy-start.1 = (s32[4,2]{0,1:T(2,128)S(1)}, s32[4,2]{0,1:T(2,128)}, u32[]{:S(2)}) copy-start(s32[4,2]{0,1:T(2,128)} %param.11) | copy-start | bytes 100
  21.3 0.7 %copy-start.2 = (s32[4,2]{0,1:T(2,128)S(1)}, s32[4,2]{0,1:T(2,128)}, u32[]{:S(2)}) copy-start(s32[4,2]{0,1:T(2,128)} %param.12) | copy-start | bytes 100
  22.0 0.7 %copy-start = (s32[8]{0:T(128)S(1)}, s32[8]{0:T(128)}, u32[]{:S(2)}) copy-start(s32[8]{0:T(128)} %param.14) | copy-start | bytes 100
  32.4 6.0 %collective-permute-start.10 = (bf16[64,512]{1,0:T(8,128)(2,1)S(1)}, bf16[64,512]{1,0:T(8,128)(2,1)S(1)}, u32[]{:S(2)}, u32[]{:S(2)}) collective-permute-start(bf16[64,512]{1,0:T(8,128)(2,1)S(1)} %get-tuple-element.37.own_ref), channel_id=1, source_target_pairs={{0,8},{2,10},{4,12},{6,14},{8,0},{10,2},{12,4},{14,6},{1,9},{3,11}... | collective-permute-start | bytes 196616 | tf_op jit(solution)/shard_map/ppermute | solution.py:268
  39.5 7.7 %collective-permute-start.14 = (f32[64,1024]{1,0:T(8,128)S(1)}, f32[64,1024]{1,0:T(8,128)S(1)}, u32[]{:S(2)}, u32[]{:S(2)}) collective-permute-start(f32[64,1024]{1,0:T(8,128)S(1)} %get-tuple-element.43), channel_id=1, source_target_pairs={{0,1},{1,0},{2,3},{3,2},{4,5},{5,4},{6,7},{7,6},{8,9},{9,8},{10,11... | collective-permute-start | bytes 786440 | tf_op jit(solution)/shard_map/ppermute | solution.py:289
  44.4 6.8 %collective-permute-start.7 = (bf16[128,512]{1,0:T(8,128)(2,1)}, bf16[128,512]{1,0:T(8,128)(2,1)S(1)}, u32[]{:S(2)}, u32[]{:S(2)}) collective-permute-start(bf16[128,512]{1,0:T(8,128)(2,1)} %get-tuple-element.34), channel_id=1, source_target_pairs={{0,2},{2,0},{4,6},{6,4},{8,10},{10,8},{12,14},{14,12},{1,3},{3,1},... | collective-permute-start | bytes 393224 | tf_op jit(solution)/shard_map/ppermute | solution.py:268
  46.0 10.1 %collective-permute-start.8 = (bf16[128,512]{1,0:T(8,128)(2,1)}, bf16[128,512]{1,0:T(8,128)(2,1)S(1)}, u32[]{:S(2)}, u32[]{:S(2)}) collective-permute-start(bf16[128,512]{1,0:T(8,128)(2,1)} %get-tuple-element.35), channel_id=1, source_target_pairs={{0,4},{2,6},{4,0},{6,2},{8,12},{10,14},{12,8},{14,10},{1,5},{3,7},... | collective-permute-start | bytes 393224 | tf_op jit(solution)/shard_map/ppermute | solution.py:268
  46.0 12.1 %collective-permute-start.9 = (bf16[128,512]{1,0:T(8,128)(2,1)}, bf16[128,512]{1,0:T(8,128)(2,1)S(1)}, u32[]{:S(2)}, u32[]{:S(2)}) collective-permute-start(bf16[128,512]{1,0:T(8,128)(2,1)} %get-tuple-element.36), channel_id=1, source_target_pairs={{0,6},{2,4},{4,2},{6,0},{8,14},{10,12},{12,10},{14,8},{1,7},{3,5},... | collective-permute-start | bytes 393224 | tf_op jit(solution)/shard_map/ppermute | solution.py:268
  47.9 11.7 %collective-permute-start.18 = (bf16[16,1024]{1,0:T(8,128)(2,1)S(1)}, bf16[16,1024]{1,0:T(8,128)(2,1)S(1)}, u32[]{:S(2)}, u32[]{:S(2)}) collective-permute-start(bf16[16,1024]{1,0:T(8,128)(2,1)S(1)} %get-tuple-element.47), channel_id=1, source_target_pairs={{0,6},{1,14},{2,4},{3,12},{4,2},{5,10},{6,0},{7,8},{8,7},{9,15},{1... | collective-permute-start | bytes 98312 | tf_op jit(solution)/shard_map/ppermute | solution.py:298
  51.2 8.4 %collective-permute-start.17 = (bf16[16,1024]{1,0:T(8,128)(2,1)S(1)}, bf16[16,1024]{1,0:T(8,128)(2,1)S(1)}, u32[]{:S(2)}, u32[]{:S(2)}) collective-permute-start(bf16[16,1024]{1,0:T(8,128)(2,1)S(1)} %get-tuple-element.46), channel_id=1, source_target_pairs={{0,4},{1,12},{2,6},{3,14},{4,0},{5,8},{6,2},{7,10},{8,5},{9,13},{1... | collective-permute-start | bytes 98312 | tf_op jit(solution)/shard_map/ppermute | solution.py:298
  51.2 8.4 %collective-permute-start.16 = (bf16[16,1024]{1,0:T(8,128)(2,1)S(1)}, bf16[16,1024]{1,0:T(8,128)(2,1)S(1)}, u32[]{:S(2)}, u32[]{:S(2)}) collective-permute-start(bf16[16,1024]{1,0:T(8,128)(2,1)S(1)} %get-tuple-element.45), channel_id=1, source_target_pairs={{0,2},{1,10},{2,0},{3,8},{4,6},{5,14},{6,4},{7,12},{8,3},{9,11},{1... | collective-permute-start | bytes 98312 | tf_op jit(solution)/shard_map/ppermute | solution.py:298
  56.2 6.1 %collective-permute-start.15 = (bf16[16,1024]{1,0:T(8,128)(2,1)S(1)}, bf16[16,1024]{1,0:T(8,128)(2,1)S(1)}, u32[]{:S(2)}, u32[]{:S(2)}) collective-permute-start(bf16[16,1024]{1,0:T(8,128)(2,1)S(1)} %get-tuple-element.44), channel_id=1, source_target_pairs={{0,0},{1,8},{2,2},{3,10},{4,4},{5,12},{6,6},{7,14},{8,1},{9,9},{10... | collective-permute-start | bytes 98312 | tf_op jit(solution)/shard_map/ppermute | solution.py:298

commit v3 on v2

--- a/solution.py
+++ b/solution.py
@@ -6,6 +6,7 @@
 from jax.experimental import pallas as pl
 from jax.experimental.pallas import tpu as pltpu
 from jax.sharding import PartitionSpec as P
+
 
 HEAD_SIZE = 128
 SLASH_SPAN = 8
@@ -16,6 +17,7 @@
 PAD_ROWS = 8
 MASKED = -1e30
 
+
 SMEM = pl.BlockSpec(memory_space=pltpu.SMEM)
 VMEM = pl.BlockSpec(memory_space=pltpu.VMEM)
 
@@ -28,15 +30,15 @@
     return pltpu.with_memory_space_constraint(x, pltpu.VMEM)
 
 
-def pack_heads(meta, query, key, value, kept_rows, heads):
+def pack_heads(shard_index, query, key, value, kept_rows, heads):
     length = query.shape[0]
     width = query.shape[1] // heads
     hd = HEAD_SIZE
     capacity = kept_rows.shape[1]
     total = 2 * hd + width
 
-    def body(meta_ref, q_ref, k_ref, v_ref, kept_ref, *out):
-        slot = meta_ref[0] % heads
+    def body(c_ref, q_ref, k_ref, v_ref, kept_ref, *out):
+        slot = c_ref[0] % heads
         kept = jnp.zeros((PAD_ROWS, total), jnp.bfloat16)
         for j in range(heads):
             head = slot ^ j
@@ -60,14 +62,14 @@
         in_specs=[SMEM] + [VMEM] * 4,
         out_specs=[VMEM] * (2 * heads),
         name="pack_heads",
-    )(meta, query, key, value, kept_rows)
-
-
-def pack_weight(meta, weight, heads):
+    )(shard_index, query, key, value, kept_rows)
+
+
+def pack_weight(shard_index, weight, heads):
     width = weight.shape[1] // heads
 
-    def body(meta_ref, w_ref, *out):
-        slot = meta_ref[0] % heads
+    def body(c_ref, w_ref, *out):
+        slot = c_ref[0] % heads
         for j in range(heads):
             at = pl.multiple_of((slot ^ j) * width, HEAD_SIZE)
             out[j][...] = w_ref[:, pl.ds(at, width)]
@@ -78,110 +80,133 @@
         in_specs=[SMEM, VMEM],
         out_specs=[VMEM] * heads,
         name="pack_weight",
-    )(meta, weight)
-
-
-def attention(meta, offsets_at, tiles_at, counts_at, near, far, keep_rows):
+    )(shard_index, weight)
+
+
+def attention(shard_index, slash, tiles, counts, near, far, keep_rows):
     heads = len(near)
-    pieces = heads + len(far)
     length = near[0].shape[0] - PAD_ROWS
     hd = HEAD_SIZE
     width = near[0].shape[1] - 2 * hd
     group = width // hd
+    far_keys = len(far) * length
+    keys = far_keys + heads * length
     block_rows = heads * keep_rows
     factor = hd ** (-0.5) * math.log2(math.e)
 
-    def body(meta_ref, *rest):
+    def body(c_ref, slash_ref, tile_ref, count_ref, *rest):
         near_refs, rest = rest[:heads], rest[heads:]
         far_refs, rest = rest[: len(far)], rest[len(far) :]
         out_refs, rows_ref = rest[:heads], rest[heads]
-        k_all, v_all, bias = rest[heads + 1 :]
-        c = meta_ref[0]
+        q_all, k_all, v_all, kept_all, mixed_all = rest[heads + 1 :]
+        c = c_ref[0]
         slot = c % heads
-        first = counts_at + c - slot
-        for k in range(pieces):
-            ref = near_refs[k] if k < heads else far_refs[k - heads]
-            k_all[k * length : (k + 1) * length, :] = ref[0:length, 0:hd]
-            v_all[k * length : (k + 1) * length, :] = ref[0:length, hd : 2 * hd]
+        first = c - slot
+        for k in range(len(far)):
+            k_all[k * length : (k + 1) * length, :] = far_refs[k][:, 0:hd]
+            v_all[k * length : (k + 1) * length, :] = far_refs[k][:, hd:]
+        for k in range(heads):
+            to = slot ^ k
+            at = pl.ds(pl.multiple_of(far_keys + to * length, length), length)
+            k_all[at, :] = near_refs[k][0:length, 0:hd]
+            v_all[at, :] = near_refs[k][0:length, hd : 2 * hd]
+            for g in range(group):
+                q_at = pl.multiple_of((to * group + g) * length, length)
+                q_all[pl.ds(q_at, length), :] = near_refs[k][
+                    0:length, (2 + g) * hd : (3 + g) * hd
+                ]
+            kept_at = pl.ds(pl.multiple_of(to * PAD_ROWS, PAD_ROWS), PAD_ROWS)
+            kept_all[kept_at, :] = near_refs[k][length:, 0:hd].astype(jnp.float32)
         difference = lax.broadcasted_iota(jnp.int32, (length, length), 0) - lax.broadcasted_iota(
             jnp.int32, (length, length), 1
         )
-        offsets = [meta_ref[offsets_at + i * heads + slot] for i in range(2)]
-        verticals = [meta_ref[tiles_at + i * heads + slot] for i in range(VTILES)]
+        offsets = [slash_ref[i, slot] for i in range(2)]
+        verticals = [tile_ref[i, slot] for i in range(VTILES)]
+
+        def bias_of(q_shard, k_shard):
+            distance = difference + (q_shard - k_shard) * length
+            reach = jnp.int32(LOCAL_BAND_KEYS)
+            for tile in verticals:
+                reach = jnp.where(tile == k_shard, jnp.int32(1 << 30), reach)
+            allowed = (distance >= 0) & (distance < reach)
+            for offset in offsets:
+                allowed |= (distance >= offset) & (distance < offset + SLASH_W)
+            return jnp.where(allowed, 0.0, MASKED)
+
         rows = jnp.zeros((block_rows, width), jnp.float32)
-        for q in range(heads):
-            q_shard = c ^ q
-            for k in range(pieces):
-                k_shard = c ^ k
-                distance = difference + (q_shard - k_shard) * length
-                reach = jnp.int32(LOCAL_BAND_KEYS)
-                for tile in verticals:
-                    reach = jnp.where(tile == k_shard, jnp.int32(1 << 30), reach)
-                allowed = (distance >= 0) & (distance < reach)
-                for offset in offsets:
-                    allowed |= (distance >= offset) & (distance < offset + SLASH_W)
-                bias[:, k * length : (k + 1) * length] = jnp.where(allowed, 0.0, MASKED)
+        before = jnp.int32(0)
+        for s in range(heads):
+            q_shard = first + s
+            shards = [c ^ (heads + k) for k in range(len(far))] + [first + t for t in range(s + 1)]
+            bias = jnp.concatenate([bias_of(q_shard, shard) for shard in shards], 1)
+            seen = len(shards) * length
+            rows_at = s * group * length
+            scores = lax.dot_general(
+                q_all[rows_at : rows_at + group * length, :],
+                k_all[0:seen, :],
+                (((1,), (1,)), ((), ())),
+                preferred_element_type=jnp.float32,
+            )
+            scores = (scores.reshape(group, length, seen) + bias[None]).reshape(group * length, seen)
+            top = jnp.max(scores, axis=1, keepdims=True)
+            weights = jnp.exp2((scores - top) * factor)
+            total = jnp.sum(weights, axis=1, keepdims=True)
+            mixed = jnp.dot(
+                weights.astype(jnp.bfloat16), v_all[0:seen, :], preferred_element_type=jnp.float32
+            )
+            mixed = (mixed / total).astype(jnp.bfloat16)
             for g in range(group):
-                at = 2 * hd + g * hd
-                scores = lax.dot_general(
-                    near_refs[q][0:length, at : at + hd],
-                    k_all[...],
-                    (((1,), (1,)), ((), ())),
-                    preferred_element_type=jnp.float32,
-                )
-                scores = scores + bias[...]
-                top = jnp.max(scores, axis=1, keepdims=True)
-                weights = jnp.exp2((scores - top) * factor)
-                total = jnp.sum(weights, axis=1, keepdims=True)
-                mixed = jnp.dot(
-                    weights.astype(jnp.bfloat16), v_all[...], preferred_element_type=jnp.float32
-                )
-                out_refs[q][:, g * hd : (g + 1) * hd] = (mixed / total).astype(jnp.bfloat16)
-            q_slot = slot ^ q
-            before = jnp.int32(0)
-            for s in range(heads):
-                before = before + jnp.where(s < q_slot, meta_ref[first + s], 0)
-            kept = near_refs[q][length : length + 1, 0:hd].astype(jnp.float32).astype(jnp.int32)
+                mixed_all[s * length : (s + 1) * length, g * hd : (g + 1) * hd] = mixed[
+                    g * length : (g + 1) * length
+                ]
+            count = count_ref[q_shard]
+            kept = kept_all[s * PAD_ROWS : s * PAD_ROWS + 1, :].astype(jnp.int32)
             token = lax.broadcasted_iota(jnp.int32, (length, hd), 0)
             is_token = (token == kept).astype(jnp.float32).astype(jnp.bfloat16)
             index = lax.broadcasted_iota(jnp.int32, (hd, block_rows), 0)
             place = lax.broadcasted_iota(jnp.int32, (hd, block_rows), 1)
-            is_place = ((place - index == before) & (index < meta_ref[counts_at + q_shard])).astype(jnp.float32)
+            is_place = ((place - index == before) & (index < count)).astype(jnp.float32)
             chooser = jnp.dot(
                 is_token, is_place.astype(jnp.bfloat16), preferred_element_type=jnp.float32
             ).astype(jnp.bfloat16)
             rows = rows + lax.dot_general(
                 chooser,
-                out_refs[q][...],
+                mixed_all[s * length : (s + 1) * length, :],
                 (((0,), (0,)), ((), ())),
                 preferred_element_type=jnp.float32,
             )
+            before = before + count
         rows_ref[...] = rows.astype(jnp.bfloat16)
+        for k in range(heads):
+            at = pl.multiple_of((slot ^ k) * length, length)
+            out_refs[k][...] = mixed_all[pl.ds(at, length), :]
 
     return pl.pallas_call(
         body,
         out_shape=[pltpu.VMEM((length, width), jnp.bfloat16)] * heads
         + [pltpu.VMEM((block_rows, width), jnp.bfloat16)],
-        in_specs=[SMEM] + [VMEM] * pieces,
+        in_specs=[SMEM] * 4 + [VMEM] * (heads + len(far)),
         out_specs=[VMEM] * (heads + 1),
         scratch_shapes=[
-            pltpu.VMEM((pieces * length, hd), jnp.bfloat16),
-            pltpu.VMEM((pieces * length, hd), jnp.bfloat16),
-            pltpu.VMEM((length, pieces * length), jnp.float32),
+            pltpu.VMEM((heads * group * length, hd), jnp.bfloat16),
+            pltpu.VMEM((keys, hd), jnp.bfloat16),
+            pltpu.VMEM((keys, hd), jnp.bfloat16),
+            pltpu.VMEM((heads * PAD_ROWS, hd), jnp.float32),
+            pltpu.VMEM((heads * length, width), jnp.bfloat16),
         ],
         name="attention",
-    )(meta, *near, *far)
-
-
-def project(meta, own_rows, other_rows, weights):
+    )(shard_index, slash, tiles, counts, *near, *far)
+
+
+def project(shard_index, core_index, own_rows, other_rows, weights):
     heads = len(weights)
     count = own_rows.shape[0]
     outs = weights[0].shape[0]
 
-    def body(meta_ref, own_ref, other_ref, *rest):
+    def body(c_ref, h_ref, own_ref, other_ref, *rest):
         w_refs, (keep_ref, send_ref) = rest[:heads], rest[heads:]
-        slot = meta_ref[0] % heads
-        keeps_own = meta_ref[0] // heads == meta_ref[1]
+        slot = c_ref[0] % heads
+        keeps_own = c_ref[0] // heads == h_ref[0]
         own, other = own_ref[...], other_ref[...]
         both = jnp.concatenate(
             [jnp.where(keeps_own, own, other), jnp.where(keeps_own, other, own)], 0
@@ -197,17 +222,17 @@
     return pl.pallas_call(
         body,
         out_shape=[pltpu.VMEM((count, heads * outs), jnp.float32)] * 2,
-        in_specs=[SMEM] + [VMEM] * (2 + heads),
+        in_specs=[SMEM] * 2 + [VMEM] * (2 + heads),
         out_specs=[VMEM] * 2,
         name="project",
-    )(meta, own_rows, other_rows, *weights)
-
-
-def split_rows(meta, kept, received, heads):
+    )(shard_index, core_index, own_rows, other_rows, *weights)
+
+
+def split_rows(shard_index, kept, received, heads):
     keep_rows = kept.shape[0] // heads
 
-    def body(meta_ref, a_ref, b_ref, *out):
-        slot = meta_ref[0] % heads
+    def body(c_ref, a_ref, b_ref, *out):
+        slot = c_ref[0] % heads
         for j in range(heads):
             at = pl.multiple_of((slot ^ j) * keep_rows, 8)
             out[j][...] = (a_ref[pl.ds(at, keep_rows), :] + b_ref[pl.ds(at, keep_rows), :]).astype(
@@ -220,15 +245,15 @@
         in_specs=[SMEM, VMEM, VMEM],
         out_specs=[VMEM] * heads,
         name="split_rows",
-    )(meta, kept, received)
-
-
-def join_heads(meta, pieces):
+    )(shard_index, kept, received)
+
+
+def join_heads(shard_index, pieces):
     heads = len(pieces)
     length, width = pieces[0].shape
 
-    def body(meta_ref, *rest):
-        slot = meta_ref[0] % heads
+    def body(c_ref, *rest):
+        slot = c_ref[0] % heads
         for j in range(heads):
             at = pl.multiple_of((slot ^ j) * width, HEAD_SIZE)
             rest[heads][:, pl.ds(at, width)] = rest[j][...]
@@ -239,7 +264,7 @@
         in_specs=[SMEM] + [VMEM] * heads,
         out_specs=VMEM,
         name="join_heads",
-    )(meta, *pieces)
+    )(shard_index, *pieces)
 
 
 def local_blocks(
@@ -257,37 +282,33 @@
     heads = key_tensor.shape[1] // HEAD_SIZE
     keep_rows = query_tensor.shape[0] // 8
     c = lax.axis_index("ctx").astype(jnp.int32)
-    h = lax.axis_index("head").astype(jnp.int32)
-    tables = [jnp.stack([c, h]), slash_offsets.T.reshape(-1), vertical_tiles.T.reshape(-1), kept_count]
-    meta = jnp.concatenate(tables)
-    offsets_at = 2
-    tiles_at = offsets_at + slash_offsets.size
-    counts_at = tiles_at + vertical_tiles.size
+    shard_index = c.reshape(1)
+    core_index = lax.axis_index("head").astype(jnp.int32).reshape(1)
+
+    def move(x, axis, pairs):
+        return in_vmem(lax.ppermute(x, axis, pairs))
 
     def swap(x, k):
-        return in_vmem(lax.ppermute(x, "ctx", xor_pairs(size, k)))
-
-    packed = pack_heads(c.reshape(1), query_tensor, key_tensor, value_tensor, kept_rows, heads)
+        return move(x, "ctx", xor_pairs(size, k))
+
+    packed = pack_heads(shard_index, query_tensor, key_tensor, value_tensor, kept_rows, heads)
     near = [in_vmem(packed[0])] + [swap(packed[k], k) for k in range(1, heads)]
-    far = [
-        in_vmem(
-            lax.ppermute(
-                packed[heads + k % heads],
-                "ctx",
-                [(i, i ^ k) for i in range(size) if i // heads < (i ^ k) // heads],
-            )
-        )
-        for k in range(heads, size)
-    ]
-    packed_weight = pack_weight(c.reshape(1), out_weight, heads)
-    weights = [in_vmem(packed_weight[0])] + [swap(packed_weight[k], k) for k in range(1, heads)]
-    *mixed, rows = attention(meta, offsets_at, tiles_at, counts_at, near, far, keep_rows)
-    other_rows = swap(rows, heads)
+    far = []
+    for k in range(heads, size):
+        pairs = [(i, i ^ k) for i in range(size) if i // heads < (i ^ k) // heads]
+        far.append(move(packed[heads + k % heads], "ctx", pairs))
+    packed_weight = pack_weight(shard_index, out_weight, heads)
+    weights = [in_vmem(packed_weight[0])]
+    weights += [swap(packed_weight[k], k) for k in range(1, heads)]
+    *mixed, rows = attention(
+        shard_index, slash_offsets.T, vertical_tiles.T, kept_count, near, far, keep_rows
+    )
+    other_rows = move(rows, "ctx", xor_pairs(size, heads))
     returned = [in_vmem(mixed[0])] + [swap(mixed[k], k) for k in range(1, heads)]
-    attended = join_heads(meta, returned)
-    kept, sent = project(meta, in_vmem(rows), other_rows, weights)
-    received = in_vmem(lax.ppermute(sent, "head", [(i, cores - 1 - i) for i in range(cores)]))
-    shares = split_rows(meta, in_vmem(kept), received, heads)
+    attended = join_heads(shard_index, returned)
+    kept, sent = project(shard_index, core_index, in_vmem(rows), other_rows, weights)
+    received = move(sent, "head", [(i, cores - 1 - i) for i in range(cores)])
+    shares = split_rows(shard_index, in_vmem(kept), received, heads)
     total = jnp.zeros(shares[0].shape, jnp.float32)
     for k in range(heads):
         pairs = []
@@ -295,7 +316,8 @@
             for h in range(cores):
                 target = heads * h + ((i % heads) ^ k)
                 pairs.append((i * cores + h, target * cores + i // heads))
-        total = total + lax.ppermute(shares[k], ("ctx", "head"), pairs).astype(jnp.float32)
+        share = lax.ppermute(shares[k], ("ctx", "head"), pairs)
+        total = total + share.astype(jnp.float32)
     return (attended, total.astype(jnp.bfloat16))
 
 
@@ -405,7 +427,7 @@
         moving = jnp.where(head_flags, shifted, moving)
     nearby = jnp.concatenate([moving, own_pair], 0)
     distances = [nearby]
-    for repeat_factor in range(2):
+    for _ in range(2):
         nearby = shifted_2(nearby, "ctx", 1)
         distances.append(nearby)
     ordered = jnp.stack([distances[2], distances[1], distances[0]])
@@ -526,20 +548,27 @@
         P("groups"),
         P("ctx", "head"),
     )
+    size, cores = mesh.shape["ctx"], mesh.shape["head"]
+
+    def blocks_fit(args):
+        heads = args[1].shape[1] // cores // HEAD_SIZE
+        length = args[0].shape[0] // size // mesh.shape["groups"]
+        power = size & (size - 1) == 0 and heads & (heads - 1) == 0
+        whole_tiles = length == VTILE and args[5].shape[1] <= HEAD_SIZE
+        return power and whole_tiles and cores == 2 and size == heads * cores
+
+    def sharded(body):
+        return jax.shard_map(
+            body,
+            mesh=mesh,
+            in_specs=placed,
+            out_specs=(P(("groups", "ctx"), "head"), P(("groups", "ctx"), "head")),
+            check_vma=False,
+        )
+
     def program(*args):
-        heads = args[1].shape[1] // HEAD_SIZE
-        size = lax.axis_size("ctx")
-        power = size & (size - 1) == 0 and heads & (heads - 1) == 0
-        whole_tiles = args[0].shape[0] == VTILE and args[5].shape[1] <= HEAD_SIZE
-        cores = lax.axis_size("head")
-        if power and whole_tiles and cores == 2 and size == heads * cores:
-            return local_blocks(*args)
-        return local(*args)
-
-    return jax.shard_map(
-        program,
-        mesh=mesh,
-        in_specs=placed,
-        out_specs=(P(("groups", "ctx"), "head"), P(("groups", "ctx"), "head")),
-        check_vma=False,
-    )
+        if not blocks_fit(args):
+            return sharded(local)(*args)
+        return sharded(local_blocks)(*args)
+
+    return program

time: 63.3 us -> 59.9 us (0.946)
  the two profiles are of different devices: /device:TPU:9 before, /device:TPU:11 now
where the time goes in v3:
time: 59.9 us; the launch traced here: 59.6 us
  starting transfers between devices  36.4 us (61%)
  Pallas kernels  10.8 us (18%)
  waiting for transfers between devices  9.74 us (16%)
  local copies, waits for them, and re-layouts  1.29 us (2%)
  between operations  0.76 us (1%)
  other arithmetic  0.63 us (1%)
    ppermute x15, starting transfers between devices, move(): return in_vmem(lax.ppermute(x, axis, pairs))  26.2 us
    ppermute x4, starting transfers between devices, local_blocks(): share = lax.ppermute(shares[k], ('ctx', 'head'), pairs)  10.1 us
    ppermute x15, waiting for transfers between devices, move(): return in_vmem(lax.ppermute(x, axis, pairs))  6.39 us
    pallas_call x1, Pallas kernels, attention(): pl.pallas_call(body, out_shape=[pltpu.VMEM((length, width), jnp.bfloat16)...  6.17 us
    ppermute x4, waiting for transfers between devices, local_blocks(): share = lax.ppermute(shares[k], ('ctx', 'head'), pairs)  3.35 us
    pallas_call x1, Pallas kernels, pack_weight(): pl.pallas_call(body, out_shape=[pltpu.VMEM((weight.shape[0], width), jnp....  2.09 us
    unnamed x8, local copies, waits for them, and re-layouts  1.29 us
    pallas_call x1, Pallas kernels, pack_heads(): pl.pallas_call(body, out_shape=[pltpu.VMEM((length + PAD_ROWS, total), jn...  1.25 us
  transfers between devices with their start and end apart: 19, of which 5 were waited for; matrix products, arithmetic and copies ran while one was open for 0% of the time, Pallas kernels for 15%

profile of v3, /device:TPU:11, one launch (start us, length us, event | category | flops | bytes accessed | tf_op | source)
XLA Modules:
  0.0 59.6 jit_solution(6428405909168695513)
XLA Ops:
  0.6 1.2 %pack_heads.1 = (bf16[136,768]{1,0:T(8,128)(2,1)S(1)}, bf16[136,768]{1,0:T(8,128)(2,1)S(1)}, bf16[136,768]{1,0:T(8,128)(2,1)S(1)}, bf16[136,768]{1,0:T(8,128)(2,...) custom-call(s32[1]{0:T(128)} %bitcast.c_ref, ...), custom_call_target="tpu_custom_call" | custom-call | tf_op jit(solution)/shard_map/pack_heads/pallas_call | solution.py:58
  1.9 0.3 collective-permute-start
  2.2 4.2 %collective-permute-start.3 = (bf16[128,256]{1,0:T(8,128)(2,1)S(1)}, bf16[128,256]{1,0:T(8,128)(2,1)S(1)}, u32[]{:S(2)}, u32[]{:S(2)}) collective-permute-start(bf16[128,256]{1,0:T(8,128)(2,1)S(1)} %get-tuple-element.29), channel_id=1, source_target_pairs={{0,8},{2,10},{4,12},{6,14},{1,9},{3,11},{5,13},{7,15},{16,24},{18,... | collective-permute-start | bytes 196616 | tf_op jit(solution)/shard_map/ppermute | solution.py:289
  6.4 2.2 %collective-permute-start.4 = (bf16[128,256]{1,0:T(8,128)(2,1)S(1)}, bf16[128,256]{1,0:T(8,128)(2,1)S(1)}, u32[]{:S(2)}, u32[]{:S(2)}) collective-permute-start(bf16[128,256]{1,0:T(8,128)(2,1)S(1)} %get-tuple-element.30), channel_id=1, source_target_pairs={{0,10},{2,8},{4,14},{6,12},{1,11},{3,9},{5,15},{7,13},{16,26},{18,... | collective-permute-start | bytes 196616 | tf_op jit(solution)/shard_map/ppermute | solution.py:289
  8.7 1.3 %collective-permute-start.5 = (bf16[128,256]{1,0:T(8,128)(2,1)S(1)}, bf16[128,256]{1,0:T(8,128)(2,1)S(1)}, u32[]{:S(2)}, u32[]{:S(2)}) collective-permute-start(bf16[128,256]{1,0:T(8,128)(2,1)S(1)} %get-tuple-element.31), channel_id=1, source_target_pairs={{0,12},{2,14},{4,8},{6,10},{1,13},{3,15},{5,9},{7,11},{16,28},{18,... | collective-permute-start | bytes 196616 | tf_op jit(solution)/shard_map/ppermute | solution.py:289
  10.0 1.3 %collective-permute-start.6 = (bf16[128,256]{1,0:T(8,128)(2,1)S(1)}, bf16[128,256]{1,0:T(8,128)(2,1)S(1)}, u32[]{:S(2)}, u32[]{:S(2)}) collective-permute-start(bf16[128,256]{1,0:T(8,128)(2,1)S(1)} %get-tuple-element.32), channel_id=1, source_target_pairs={{0,14},{2,12},{4,10},{6,8},{1,15},{3,13},{5,11},{7,9},{16,30},{18,... | collective-permute-start | bytes 196616 | tf_op jit(solution)/shard_map/ppermute | solution.py:289
  11.3 0.0 collective-permute-done.3.rest_4_
  11.3 1.2 %collective-permute-start.1 = (bf16[136,768]{1,0:T(8,128)(2,1)S(1)}, bf16[136,768]{1,0:T(8,128)(2,1)S(1)}, u32[]{:S(2)}, u32[]{:S(2)}) collective-permute-start(bf16[136,768]{1,0:T(8,128)(2,1)S(1)} %get-tuple-element.27), channel_id=1, source_target_pairs={{0,4},{2,6},{4,0},{6,2},{8,12},{10,14},{12,8},{14,10},{1,5},{3,7},... | collective-permute-start | bytes 626696 | tf_op jit(solution)/shard_map/ppermute | solution.py:289
  12.5 1.4 %collective-permute-done.4.rest_5_ = bf16[128,256]{1,0:T(8,128)(2,1)S(1)} collective-permute-done((bf16[128,256]{1,0:T(8,128)(2,1)S(1)}, bf16[128,256]{1,0:T(8,128)(2,1)S(1)}, u32[]{:S(2)}, u32[]{:S(2)}) %collective-permute-start.4) | collective-permute-done | bytes 65568 | tf_op jit(solution)/shard_map/ppermute | solution.py:289
  13.9 0.0 collective-permute-start.2
  13.9 2.1 %pack_weight.1 = (bf16[256,512]{1,0:T(8,128)(2,1)S(1)}, bf16[256,512]{1,0:T(8,128)(2,1)}, bf16[256,512]{1,0:T(8,128)(2,1)}, bf16[256,512]{1,0:T(8,128)(2,1)S(1)}) custom-call(s32[1]{0:T(128)} %bitcast.c_ref, bf16[256,2048]{1,0:T(8,128)(2,1)} %w_ref.1), custom_call_target="tpu_custom_call" | custom-call | tf_op jit(solution)/shard_map/pack_weight/pallas_call | solution.py:77
  16.0 0.0 collective-permute-done.5.rest_6_
  16.0 1.2 %collective-permute-start.11 = (bf16[256,512]{1,0:T(8,128)(2,1)}, bf16[256,512]{1,0:T(8,128)(2,1)S(1)}, u32[]{:S(2)}, u32[]{:S(2)}) collective-permute-start(bf16[256,512]{1,0:T(8,128)(2,1)} %get-tuple-element.39), channel_id=1, source_target_pairs={{0,2},{2,0},{4,6},{6,4},{8,10},{10,8},{12,14},{14,12},{1,3},{3,1},... | collective-permute-start | bytes 786440 | tf_op jit(solution)/shard_map/ppermute | solution.py:289
  17.2 0.2 collective-permute-done.6.rest_7_
  17.5 1.2 %collective-permute-start.12 = (bf16[256,512]{1,0:T(8,128)(2,1)}, bf16[256,512]{1,0:T(8,128)(2,1)S(1)}, u32[]{:S(2)}, u32[]{:S(2)}) collective-permute-start(bf16[256,512]{1,0:T(8,128)(2,1)} %get-tuple-element.40), channel_id=1, source_target_pairs={{0,4},{2,6},{4,0},{6,2},{8,12},{10,14},{12,8},{14,10},{1,5},{3,7},... | collective-permute-start | bytes 786440 | tf_op jit(solution)/shard_map/ppermute | solution.py:289
  18.6 0.0 collective-permute-done.rest_1_
  18.7 1.1 %collective-permute-start.13 = (bf16[256,512]{1,0:T(8,128)(2,1)S(1)}, bf16[256,512]{1,0:T(8,128)(2,1)S(1)}, u32[]{:S(2)}, u32[]{:S(2)}) collective-permute-start(bf16[256,512]{1,0:T(8,128)(2,1)S(1)} %get-tuple-element.41), channel_id=1, source_target_pairs={{0,6},{2,4},{4,2},{6,0},{8,14},{10,12},{12,10},{14,8},{1,7},{3,5},... | collective-permute-start | bytes 786440 | tf_op jit(solution)/shard_map/ppermute | solution.py:289
  19.8 0.0 collective-permute-done.1.rest_2_
  19.8 2.1 %collective-permute-done.2.rest_3_ = bf16[136,768]{1,0:T(8,128)(2,1)S(1)} collective-permute-done((bf16[136,768]{1,0:T(8,128)(2,1)S(1)}, bf16[136,768]{1,0:T(8,128)(2,1)S(1)}, u32[]{:S(2)}, u32[]{:S(2)}) %collective-permute-start.2) | collective-permute-done | bytes 208928 | tf_op jit(solution)/shard_map/ppermute | solution.py:289
  21.9 6.2 %attention.1 = (bf16[128,512]{1,0:T(8,128)(2,1)S(1)}, bf16[128,512]{1,0:T(8,128)(2,1)S(1)}, bf16[128,512]{1,0:T(8,128)(2,1)S(1)}, bf16[128,512]{1,0:T(8,128)(2,1)S(1)}, bf16[64,512]{1,0:T(8,128)(2,1)S(1)}) custom-call(s32[1]{0:T(128)} %bitcast.c_ref, s32[2,4]{1,0:T(2,128)} %bitcast.4, s32[2,4]{1,0:T(2,128)} %bitcast.5, s32[8]{0:T(128)} %count_ref.1, ...), custom_call_target="tpu_custom_call" | custom-call | tf_op jit(solution)/shard_map/attention/pallas_call | solution.py:184
  28.0 0.0 copy-start
  28.0 0.6 %copy-done = bf16[128,512]{1,0:T(8,128)(2,1)} copy-done((bf16[128,512]{1,0:T(8,128)(2,1)}, bf16[128,512]{1,0:T(8,128)(2,1)S(1)}, u32[]{:S(2)}) %copy-start) | copy-done | bytes 131096
  28.7 0.6 %copy-done.2 = bf16[128,512]{1,0:T(8,128)(2,1)} copy-done((bf16[128,512]{1,0:T(8,128)(2,1)}, bf16[128,512]{1,0:T(8,128)(2,1)S(1)}, u32[]{:S(2)}) %copy-start.2) | copy-done | bytes 131096
  29.3 4.4 %collective-permute-start.10 = (bf16[64,512]{1,0:T(8,128)(2,1)S(1)}, bf16[64,512]{1,0:T(8,128)(2,1)S(1)}, u32[]{:S(2)}, u32[]{:S(2)}) collective-permute-start(bf16[64,512]{1,0:T(8,128)(2,1)S(1)} %get-tuple-element.37.own_ref), channel_id=1, source_target_pairs={{0,8},{2,10},{4,12},{6,14},{8,0},{10,2},{12,4},{14,6},{1,9},{3,11}... | collective-permute-start | bytes 196616 | tf_op jit(solution)/shard_map/ppermute | solution.py:289
  33.7 0.0 collective-permute-done.11.rest_1_
  33.7 0.0 collective-permute-done.12.rest_2_
  33.7 0.0 collective-permute-done.13.rest_3_
  33.7 2.6 %collective-permute-done.10.other_ref = bf16[64,512]{1,0:T(8,128)(2,1)S(1)} collective-permute-done((bf16[64,512]{1,0:T(8,128)(2,1)S(1)}, bf16[64,512]{1,0:T(8,128)(2,1)S(1)}, u32[]{:S(2)}, u32[]{:S(2)}) %collective-permute-start.10) | collective-permute-done | bytes 65568 | tf_op jit(solution)/shard_map/ppermute | solution.py:289
  36.4 0.5 project.1
  36.8 5.1 %collective-permute-start.14 = (f32[64,1024]{1,0:T(8,128)S(1)}, f32[64,1024]{1,0:T(8,128)S(1)}, u32[]{:S(2)}, u32[]{:S(2)}) collective-permute-start(f32[64,1024]{1,0:T(8,128)S(1)} %get-tuple-element.43), channel_id=1, source_target_pairs={{0,1},{1,0},{2,3},{3,2},{4,5},{5,4},{6,7},{7,6},{8,9},{9,8},{10,11... | collective-permute-start | bytes 786440 | tf_op jit(solution)/shard_map/ppermute | solution.py:289
  42.0 0.0 copy-done.3
  42.0 0.0 collective-permute-start.7
  42.0 0.1 collective-permute-start.8
  42.0 2.6 %collective-permute-start.9 = (bf16[128,512]{1,0:T(8,128)(2,1)S(1)}, bf16[128,512]{1,0:T(8,128)(2,1)S(1)}, u32[]{:S(2)}, u32[]{:S(2)}) collective-permute-start(bf16[128,512]{1,0:T(8,128)(2,1)S(1)} %get-tuple-element.36), channel_id=1, source_target_pairs={{0,6},{2,4},{4,2},{6,0},{8,14},{10,12},{12,10},{14,8},{1,7},{3,5},... | collective-permute-start | bytes 393224 | tf_op jit(solution)/shard_map/ppermute | solution.py:289
  44.6 0.0 collective-permute-done.14.b_ref
  44.6 2.3 %collective-permute-start.18 = (bf16[16,1024]{1,0:T(8,128)(2,1)S(1)}, bf16[16,1024]{1,0:T(8,128)(2,1)S(1)}, u32[]{:S(2)}, u32[]{:S(2)}) collective-permute-start(bf16[16,1024]{1,0:T(8,128)(2,1)S(1)} %get-tuple-element.47), channel_id=1, source_target_pairs={{0,6},{1,14},{2,4},{3,12},{4,2},{5,10},{6,0},{7,8},{8,7},{9,15},{1... | collective-permute-start | bytes 98312 | tf_op jit(solution)/shard_map/ppermute | solution.py:319
  47.0 0.1 collective-permute-start.17
  47.1 0.0 collective-permute-done.7.rest_1_
  47.1 5.8 %collective-permute-start.16 = (bf16[16,1024]{1,0:T(8,128)(2,1)S(1)}, bf16[16,1024]{1,0:T(8,128)(2,1)S(1)}, u32[]{:S(2)}, u32[]{:S(2)}) collective-permute-start(bf16[16,1024]{1,0:T(8,128)(2,1)S(1)} %get-tuple-element.45), channel_id=1, source_target_pairs={{0,2},{1,10},{2,0},{3,8},{4,6},{5,14},{6,4},{7,12},{8,3},{9,11},{1... | collective-permute-start | bytes 98312 | tf_op jit(solution)/shard_map/ppermute | solution.py:319
  52.9 0.0 collective-permute-done.8.rest_2_
  52.9 1.9 %collective-permute-start.15 = (bf16[16,1024]{1,0:T(8,128)(2,1)S(1)}, bf16[16,1024]{1,0:T(8,128)(2,1)S(1)}, u32[]{:S(2)}, u32[]{:S(2)}) collective-permute-start(bf16[16,1024]{1,0:T(8,128)(2,1)S(1)} %get-tuple-element.44), channel_id=1, source_target_pairs={{0,0},{1,8},{2,2},{3,10},{4,4},{5,12},{6,6},{7,14},{8,1},{9,9},{10... | collective-permute-start | bytes 98312 | tf_op jit(solution)/shard_map/ppermute | solution.py:319
  54.8 0.0 collective-permute-done.9.rest_3_
  54.8 0.8 %join_heads.1 = bf16[128,2048]{1,0:T(8,128)(2,1)} custom-call(s32[1]{0:T(128)} %bitcast.c_ref, bf16[128,512]{1,0:T(8,128)(2,1)S(1)} %get-tuple-element.33.rest_0_, bf16[128,512]{1,0:T(8,128)(2,1)S(1)} %collective-permute-done.7.rest_1_, bf16[128,512]{1,0:T(8,128)(2,1)S(1)} %collective-permute-done.8.rest_2_, bf16[128,512]{1,0:T(8,128)(2,1)S(1)} %collective-permute-done.9.rest_3_), custom_call_target="tpu_custom_call" | custom-call | tf_op jit(solution)/shard_map/join_heads/pallas_call | solution.py:261
  55.6 0.0 collective-permute-done.18
  55.7 0.0 collective-permute-done.17
  55.7 0.0 collective-permute-done.16
  55.7 3.3 %collective-permute-done.15 = bf16[16,1024]{1,0:T(8,128)(2,1)S(1)} collective-permute-done((bf16[16,1024]{1,0:T(8,128)(2,1)S(1)}, bf16[16,1024]{1,0:T(8,128)(2,1)S(1)}, u32[]{:S(2)}, u32[]{:S(2)}) %collective-permute-start.15) | collective-permute-done | bytes 32800 | tf_op jit(solution)/shard_map/ppermute | solution.py:319
  59.0 0.6 %add_convert_fusion = bf16[16,1024]{1,0:T(8,128)(2,1)} fusion(bf16[16,1024]{1,0:T(8,128)(2,1)S(1)} %collective-permute-done.18, bf16[16,1024]{1,0:T(8,128)(2,1)S(1)} %collective-permute-done.17, bf16[16,1024]{1,0:T(8,128)(2,1)S(1)} %collective-permute-done.16, bf16[16,1024]{1,0:T(8,128)(2,1)S(1)} %collective-permute-done.15), kind=kLoop, calls=%fused_computation | loop fusion | flops 131072 | bytes 163840 | tf_op jit(solution)/shard_map/convert_element_type | solution.py:321
  (5 shorter events, 0.0 us)
Async XLA Ops:
  1.9 16.8 %collective-permute-start = (bf16[136,768]{1,0:T(8,128)(2,1)S(1)}, bf16[136,768]{1,0:T(8,128)(2,1)S(1)}, u32[]{:S(2)}, u32[]{:S(2)}) collective-permute-start(bf16[136,768]{1,0:T(8,128)(2,1)S(1)} %get-tuple-element.26), channel_id=1, source_target_pairs={{0,2},{2,0},{4,6},{6,4},{8,10},{10,8},{12,14},{14,12},{1,3},{3,1},... | collective-permute-start | bytes 626696 | tf_op jit(solution)/shard_map/ppermute | solution.py:289
  2.2 9.0 %collective-permute-start.3 = (bf16[128,256]{1,0:T(8,128)(2,1)S(1)}, bf16[128,256]{1,0:T(8,128)(2,1)S(1)}, u32[]{:S(2)}, u32[]{:S(2)}) collective-permute-start(bf16[128,256]{1,0:T(8,128)(2,1)S(1)} %get-tuple-element.29), channel_id=1, source_target_pairs={{0,8},{2,10},{4,12},{6,14},{1,9},{3,11},{5,13},{7,15},{16,24},{18,... | collective-permute-start | bytes 196616 | tf_op jit(solution)/shard_map/ppermute | solution.py:289
  6.4 7.5 %collective-permute-start.4 = (bf16[128,256]{1,0:T(8,128)(2,1)S(1)}, bf16[128,256]{1,0:T(8,128)(2,1)S(1)}, u32[]{:S(2)}, u32[]{:S(2)}) collective-permute-start(bf16[128,256]{1,0:T(8,128)(2,1)S(1)} %get-tuple-element.30), channel_id=1, source_target_pairs={{0,10},{2,8},{4,14},{6,12},{1,11},{3,9},{5,15},{7,13},{16,26},{18,... | collective-permute-start | bytes 196616 | tf_op jit(solution)/shard_map/ppermute | solution.py:289
  8.7 7.3 %collective-permute-start.5 = (bf16[128,256]{1,0:T(8,128)(2,1)S(1)}, bf16[128,256]{1,0:T(8,128)(2,1)S(1)}, u32[]{:S(2)}, u32[]{:S(2)}) collective-permute-start(bf16[128,256]{1,0:T(8,128)(2,1)S(1)} %get-tuple-element.31), channel_id=1, source_target_pairs={{0,12},{2,14},{4,8},{6,10},{1,13},{3,15},{5,9},{7,11},{16,28},{18,... | collective-permute-start | bytes 196616 | tf_op jit(solution)/shard_map/ppermute | solution.py:289
  10.0 7.5 %collective-permute-start.6 = (bf16[128,256]{1,0:T(8,128)(2,1)S(1)}, bf16[128,256]{1,0:T(8,128)(2,1)S(1)}, u32[]{:S(2)}, u32[]{:S(2)}) collective-permute-start(bf16[128,256]{1,0:T(8,128)(2,1)S(1)} %get-tuple-element.32), channel_id=1, source_target_pairs={{0,14},{2,12},{4,10},{6,8},{1,15},{3,13},{5,11},{7,9},{16,30},{18,... | collective-permute-start | bytes 196616 | tf_op jit(solution)/shard_map/ppermute | solution.py:289
  11.3 8.5 %collective-permute-start.1 = (bf16[136,768]{1,0:T(8,128)(2,1)S(1)}, bf16[136,768]{1,0:T(8,128)(2,1)S(1)}, u32[]{:S(2)}, u32[]{:S(2)}) collective-permute-start(bf16[136,768]{1,0:T(8,128)(2,1)S(1)} %get-tuple-element.27), channel_id=1, source_target_pairs={{0,4},{2,6},{4,0},{6,2},{8,12},{10,14},{12,8},{14,10},{1,5},{3,7},... | collective-permute-start | bytes 626696 | tf_op jit(solution)/shard_map/ppermute | solution.py:289
  13.9 8.0 %collective-permute-start.2 = (bf16[136,768]{1,0:T(8,128)(2,1)S(1)}, bf16[136,768]{1,0:T(8,128)(2,1)S(1)}, u32[]{:S(2)}, u32[]{:S(2)}) collective-permute-start(bf16[136,768]{1,0:T(8,128)(2,1)S(1)} %get-tuple-element.28), channel_id=1, source_target_pairs={{0,6},{2,4},{4,2},{6,0},{8,14},{10,12},{12,10},{14,8},{1,7},{3,5},... | collective-permute-start | bytes 626696 | tf_op jit(solution)/shard_map/ppermute | solution.py:289
  16.0 17.7 %collective-permute-start.11 = (bf16[256,512]{1,0:T(8,128)(2,1)}, bf16[256,512]{1,0:T(8,128)(2,1)S(1)}, u32[]{:S(2)}, u32[]{:S(2)}) collective-permute-start(bf16[256,512]{1,0:T(8,128)(2,1)} %get-tuple-element.39), channel_id=1, source_target_pairs={{0,2},{2,0},{4,6},{6,4},{8,10},{10,8},{12,14},{14,12},{1,3},{3,1},... | collective-permute-start | bytes 786440 | tf_op jit(solution)/shard_map/ppermute | solution.py:289
  17.5 16.2 %collective-permute-start.12 = (bf16[256,512]{1,0:T(8,128)(2,1)}, bf16[256,512]{1,0:T(8,128)(2,1)S(1)}, u32[]{:S(2)}, u32[]{:S(2)}) collective-permute-start(bf16[256,512]{1,0:T(8,128)(2,1)} %get-tuple-element.40), channel_id=1, source_target_pairs={{0,4},{2,6},{4,0},{6,2},{8,12},{10,14},{12,8},{14,10},{1,5},{3,7},... | collective-permute-start | bytes 786440 | tf_op jit(solution)/shard_map/ppermute | solution.py:289
  18.7 15.1 %collective-permute-start.13 = (bf16[256,512]{1,0:T(8,128)(2,1)S(1)}, bf16[256,512]{1,0:T(8,128)(2,1)S(1)}, u32[]{:S(2)}, u32[]{:S(2)}) collective-permute-start(bf16[256,512]{1,0:T(8,128)(2,1)S(1)} %get-tuple-element.41), channel_id=1, source_target_pairs={{0,6},{2,4},{4,2},{6,0},{8,14},{10,12},{12,10},{14,8},{1,7},{3,5},... | collective-permute-start | bytes 786440 | tf_op jit(solution)/shard_map/ppermute | solution.py:289
  28.0 0.6 %copy-start = (bf16[128,512]{1,0:T(8,128)(2,1)}, bf16[128,512]{1,0:T(8,128)(2,1)S(1)}, u32[]{:S(2)}) copy-start(bf16[128,512]{1,0:T(8,128)(2,1)S(1)} %get-tuple-element.35) | copy-start | bytes 393220
  28.7 0.6 %copy-start.2 = (bf16[128,512]{1,0:T(8,128)(2,1)}, bf16[128,512]{1,0:T(8,128)(2,1)S(1)}, u32[]{:S(2)}) copy-start(bf16[128,512]{1,0:T(8,128)(2,1)S(1)} %get-tuple-element.34) | copy-start | bytes 393220
  29.3 7.0 %collective-permute-start.10 = (bf16[64,512]{1,0:T(8,128)(2,1)S(1)}, bf16[64,512]{1,0:T(8,128)(2,1)S(1)}, u32[]{:S(2)}, u32[]{:S(2)}) collective-permute-start(bf16[64,512]{1,0:T(8,128)(2,1)S(1)} %get-tuple-element.37.own_ref), channel_id=1, source_target_pairs={{0,8},{2,10},{4,12},{6,14},{8,0},{10,2},{12,4},{14,6},{1,9},{3,11}... | collective-permute-start | bytes 196616 | tf_op jit(solution)/shard_map/ppermute | solution.py:289
  36.4 5.6 %copy-start.3 = (bf16[128,512]{1,0:T(8,128)(2,1)S(1)}, bf16[128,512]{1,0:T(8,128)(2,1)}, u32[]{:S(2)}) copy-start(bf16[128,512]{1,0:T(8,128)(2,1)} %copy-done.2) | copy-start | bytes 393220
  36.4 5.6 %copy-start.1 = (bf16[128,512]{1,0:T(8,128)(2,1)S(1)}, bf16[128,512]{1,0:T(8,128)(2,1)}, u32[]{:S(2)}) copy-start(bf16[128,512]{1,0:T(8,128)(2,1)} %copy-done) | copy-start | bytes 393220
  36.8 7.8 %collective-permute-start.14 = (f32[64,1024]{1,0:T(8,128)S(1)}, f32[64,1024]{1,0:T(8,128)S(1)}, u32[]{:S(2)}, u32[]{:S(2)}) collective-permute-start(f32[64,1024]{1,0:T(8,128)S(1)} %get-tuple-element.43), channel_id=1, source_target_pairs={{0,1},{1,0},{2,3},{3,2},{4,5},{5,4},{6,7},{7,6},{8,9},{9,8},{10,11... | collective-permute-start | bytes 786440 | tf_op jit(solution)/shard_map/ppermute | solution.py:289
  42.0 5.1 %collective-permute-start.7 = (bf16[128,512]{1,0:T(8,128)(2,1)S(1)}, bf16[128,512]{1,0:T(8,128)(2,1)S(1)}, u32[]{:S(2)}, u32[]{:S(2)}) collective-permute-start(bf16[128,512]{1,0:T(8,128)(2,1)S(1)} %copy-done.3), channel_id=1, source_target_pairs={{0,2},{2,0},{4,6},{6,4},{8,10},{10,8},{12,14},{14,12},{1,3},{3,1},... | collective-permute-start | bytes 393224 | tf_op jit(solution)/shard_map/ppermute | solution.py:289
  42.0 10.9 %collective-permute-start.8 = (bf16[128,512]{1,0:T(8,128)(2,1)S(1)}, bf16[128,512]{1,0:T(8,128)(2,1)S(1)}, u32[]{:S(2)}, u32[]{:S(2)}) collective-permute-start(bf16[128,512]{1,0:T(8,128)(2,1)S(1)} %copy-done.1), channel_id=1, source_target_pairs={{0,4},{2,6},{4,0},{6,2},{8,12},{10,14},{12,8},{14,10},{1,5},{3,7},... | collective-permute-start | bytes 393224 | tf_op jit(solution)/shard_map/ppermute | solution.py:289
  42.0 12.8 %collective-permute-start.9 = (bf16[128,512]{1,0:T(8,128)(2,1)S(1)}, bf16[128,512]{1,0:T(8,128)(2,1)S(1)}, u32[]{:S(2)}, u32[]{:S(2)}) collective-permute-start(bf16[128,512]{1,0:T(8,128)(2,1)S(1)} %get-tuple-element.36), channel_id=1, source_target_pairs={{0,6},{2,4},{4,2},{6,0},{8,14},{10,12},{12,10},{14,8},{1,7},{3,5},... | collective-permute-start | bytes 393224 | tf_op jit(solution)/shard_map/ppermute | solution.py:289
  44.6 11.0 %collective-permute-start.18 = (bf16[16,1024]{1,0:T(8,128)(2,1)S(1)}, bf16[16,1024]{1,0:T(8,128)(2,1)S(1)}, u32[]{:S(2)}, u32[]{:S(2)}) collective-permute-start(bf16[16,1024]{1,0:T(8,128)(2,1)S(1)} %get-tuple-element.47), channel_id=1, source_target_pairs={{0,6},{1,14},{2,4},{3,12},{4,2},{5,10},{6,0},{7,8},{8,7},{9,15},{1... | collective-permute-start | bytes 98312 | tf_op jit(solution)/shard_map/ppermute | solution.py:319
  47.0 8.7 %collective-permute-start.17 = (bf16[16,1024]{1,0:T(8,128)(2,1)S(1)}, bf16[16,1024]{1,0:T(8,128)(2,1)S(1)}, u32[]{:S(2)}, u32[]{:S(2)}) collective-permute-start(bf16[16,1024]{1,0:T(8,128)(2,1)S(1)} %get-tuple-element.46), channel_id=1, source_target_pairs={{0,4},{1,12},{2,6},{3,14},{4,0},{5,8},{6,2},{7,10},{8,5},{9,13},{1... | collective-permute-start | bytes 98312 | tf_op jit(solution)/shard_map/ppermute | solution.py:319
  47.1 8.6 %collective-permute-start.16 = (bf16[16,1024]{1,0:T(8,128)(2,1)S(1)}, bf16[16,1024]{1,0:T(8,128)(2,1)S(1)}, u32[]{:S(2)}, u32[]{:S(2)}) collective-permute-start(bf16[16,1024]{1,0:T(8,128)(2,1)S(1)} %get-tuple-element.45), channel_id=1, source_target_pairs={{0,2},{1,10},{2,0},{3,8},{4,6},{5,14},{6,4},{7,12},{8,3},{9,11},{1... | collective-permute-start | bytes 98312 | tf_op jit(solution)/shard_map/ppermute | solution.py:319
  52.9 6.1 %collective-permute-start.15 = (bf16[16,1024]{1,0:T(8,128)(2,1)S(1)}, bf16[16,1024]{1,0:T(8,128)(2,1)S(1)}, u32[]{:S(2)}, u32[]{:S(2)}) collective-permute-start(bf16[16,1024]{1,0:T(8,128)(2,1)S(1)} %get-tuple-element.44), channel_id=1, source_target_pairs={{0,0},{1,8},{2,2},{3,10},{4,4},{5,12},{6,6},{7,14},{8,1},{9,9},{10... | collective-permute-start | bytes 98312 | tf_op jit(solution)/shard_map/ppermute | solution.py:319

commit v4 on v3

--- a/solution.py
+++ b/solution.py
@@ -83,18 +83,45 @@
     )(shard_index, weight)
 
 
-def attention(shard_index, slash, tiles, counts, near, far, keep_rows):
+def mask_tiles(shard_index, slash, shards, length):
+    def body(c_ref, slash_ref, out_ref):
+        slot = c_ref[0] % slash_ref.shape[1]
+        difference = lax.broadcasted_iota(jnp.int32, (length, length), 0) - lax.broadcasted_iota(
+            jnp.int32, (length, length), 1
+        )
+        for d in range(shards):
+            distance = difference + d * length
+            allowed = (distance >= 0) & (distance < LOCAL_BAND_KEYS)
+            for i in range(slash_ref.shape[0]):
+                offset = slash_ref[i, slot]
+                allowed |= (distance >= offset) & (distance < offset + SLASH_W)
+            out_ref[d * length : (d + 1) * length, :] = jnp.where(allowed, 0.0, MASKED)
+        out_ref[shards * length : (shards + 1) * length, :] = jnp.where(difference >= 0, 0.0, MASKED)
+        rest = lax.broadcasted_iota(jnp.int32, (2 * length, length), 0)
+        out_ref[(shards + 1) * length :, :] = jnp.where(rest < length, 0.0, MASKED)
+
+    return pl.pallas_call(
+        body,
+        out_shape=pltpu.VMEM(((shards + 3) * length, length), jnp.float32),
+        in_specs=[SMEM, SMEM],
+        out_specs=VMEM,
+        name="mask_tiles",
+    )(shard_index, slash)
+
+
+def attention(shard_index, tiles, counts, masks, near, far, keep_rows):
     heads = len(near)
     length = near[0].shape[0] - PAD_ROWS
     hd = HEAD_SIZE
     width = near[0].shape[1] - 2 * hd
     group = width // hd
+    size = heads + len(far)
     far_keys = len(far) * length
     keys = far_keys + heads * length
     block_rows = heads * keep_rows
     factor = hd ** (-0.5) * math.log2(math.e)
 
-    def body(c_ref, slash_ref, tile_ref, count_ref, *rest):
+    def body(c_ref, tile_ref, count_ref, mask_ref, *rest):
         near_refs, rest = rest[:heads], rest[heads:]
         far_refs, rest = rest[: len(far)], rest[len(far) :]
         out_refs, rows_ref = rest[:heads], rest[heads]
@@ -104,12 +131,13 @@
         first = c - slot
         for k in range(len(far)):
             k_all[k * length : (k + 1) * length, :] = far_refs[k][:, 0:hd]
-            v_all[k * length : (k + 1) * length, :] = far_refs[k][:, hd:]
+            v_all[k * length : (k + 1) * length, 0:hd] = far_refs[k][:, hd:]
+        v_all[:, hd:] = jnp.ones((keys, hd), jnp.bfloat16)
         for k in range(heads):
             to = slot ^ k
             at = pl.ds(pl.multiple_of(far_keys + to * length, length), length)
             k_all[at, :] = near_refs[k][0:length, 0:hd]
-            v_all[at, :] = near_refs[k][0:length, hd : 2 * hd]
+            v_all[at, 0:hd] = near_refs[k][0:length, hd : 2 * hd]
             for g in range(group):
                 q_at = pl.multiple_of((to * group + g) * length, length)
                 q_all[pl.ds(q_at, length), :] = near_refs[k][
@@ -117,28 +145,23 @@
                 ]
             kept_at = pl.ds(pl.multiple_of(to * PAD_ROWS, PAD_ROWS), PAD_ROWS)
             kept_all[kept_at, :] = near_refs[k][length:, 0:hd].astype(jnp.float32)
-        difference = lax.broadcasted_iota(jnp.int32, (length, length), 0) - lax.broadcasted_iota(
-            jnp.int32, (length, length), 1
-        )
-        offsets = [slash_ref[i, slot] for i in range(2)]
         verticals = [tile_ref[i, slot] for i in range(VTILES)]
 
-        def bias_of(q_shard, k_shard):
-            distance = difference + (q_shard - k_shard) * length
-            reach = jnp.int32(LOCAL_BAND_KEYS)
+        def mask_of(q_shard, k_shard):
+            back = q_shard - k_shard
+            entry = back
             for tile in verticals:
-                reach = jnp.where(tile == k_shard, jnp.int32(1 << 30), reach)
-            allowed = (distance >= 0) & (distance < reach)
-            for offset in offsets:
-                allowed |= (distance >= offset) & (distance < offset + SLASH_W)
-            return jnp.where(allowed, 0.0, MASKED)
+                vertical = size + jnp.where(back == 0, 0, 1)
+                entry = jnp.where(tile == k_shard, vertical, entry)
+            entry = jnp.where(back < 0, size + 2, entry)
+            return mask_ref[pl.ds(pl.multiple_of(entry * length, length), length), :]
 
         rows = jnp.zeros((block_rows, width), jnp.float32)
         before = jnp.int32(0)
         for s in range(heads):
             q_shard = first + s
             shards = [c ^ (heads + k) for k in range(len(far))] + [first + t for t in range(s + 1)]
-            bias = jnp.concatenate([bias_of(q_shard, shard) for shard in shards], 1)
+            mask = jnp.concatenate([mask_of(q_shard, shard) for shard in shards], 1)
             seen = len(shards) * length
             rows_at = s * group * length
             scores = lax.dot_general(
@@ -147,14 +170,13 @@
                 (((1,), (1,)), ((), ())),
                 preferred_element_type=jnp.float32,
             )
-            scores = (scores.reshape(group, length, seen) + bias[None]).reshape(group * length, seen)
-            top = jnp.max(scores, axis=1, keepdims=True)
-            weights = jnp.exp2((scores - top) * factor)
-            total = jnp.sum(weights, axis=1, keepdims=True)
+            scores = scores.reshape(group, length, seen) * factor + mask[None]
+            scores = scores.reshape(group * length, seen)
+            weights = jnp.exp2(scores - jnp.max(scores, axis=1, keepdims=True))
             mixed = jnp.dot(
                 weights.astype(jnp.bfloat16), v_all[0:seen, :], preferred_element_type=jnp.float32
             )
-            mixed = (mixed / total).astype(jnp.bfloat16)
+            mixed = (mixed[:, :hd] / mixed[:, hd:]).astype(jnp.bfloat16)
             for g in range(group):
                 mixed_all[s * length : (s + 1) * length, g * hd : (g + 1) * hd] = mixed[
                     g * length : (g + 1) * length
@@ -185,17 +207,17 @@
         body,
         out_shape=[pltpu.VMEM((length, width), jnp.bfloat16)] * heads
         + [pltpu.VMEM((block_rows, width), jnp.bfloat16)],
-        in_specs=[SMEM] * 4 + [VMEM] * (heads + len(far)),
+        in_specs=[SMEM] * 3 + [VMEM] * (1 + heads + len(far)),
         out_specs=[VMEM] * (heads + 1),
         scratch_shapes=[
             pltpu.VMEM((heads * group * length, hd), jnp.bfloat16),
             pltpu.VMEM((keys, hd), jnp.bfloat16),
-            pltpu.VMEM((keys, hd), jnp.bfloat16),
+            pltpu.VMEM((keys, 2 * hd), jnp.bfloat16),
             pltpu.VMEM((heads * PAD_ROWS, hd), jnp.float32),
             pltpu.VMEM((heads * length, width), jnp.bfloat16),
         ],
         name="attention",
-    )(shard_index, slash, tiles, counts, *near, *far)
+    )(shard_index, tiles, counts, masks, *near, *far)
 
 
 def project(shard_index, core_index, own_rows, other_rows, weights):
@@ -300,8 +322,9 @@
     packed_weight = pack_weight(shard_index, out_weight, heads)
     weights = [in_vmem(packed_weight[0])]
     weights += [swap(packed_weight[k], k) for k in range(1, heads)]
+    masks = in_vmem(mask_tiles(shard_index, slash_offsets.T, size, query_tensor.shape[0]))
     *mixed, rows = attention(
-        shard_index, slash_offsets.T, vertical_tiles.T, kept_count, near, far, keep_rows
+        shard_index, vertical_tiles.T, kept_count, masks, near, far, keep_rows
     )
     other_rows = move(rows, "ctx", xor_pairs(size, heads))
     returned = [in_vmem(mixed[0])] + [swap(mixed[k], k) for k in range(1, heads)]

time: 59.9 us -> 65.3 us (1.090)
  the two profiles are of different devices: /device:TPU:11 before, /device:TPU:1 now
where the time goes in v4:
time: 65.3 us; the launch traced here: 64.9 us
  starting transfers between devices  38.5 us (59%)
  Pallas kernels  10.4 us (16%)
  local copies, waits for them, and re-layouts  7.55 us (12%)
  waiting for transfers between devices  7.02 us (11%)
  between operations  0.79 us (1%)
    ppermute x15, starting transfers between devices, move(): return in_vmem(lax.ppermute(x, axis, pairs))  28.6 us
    ppermute x4, starting transfers between devices, local_blocks(): share = lax.ppermute(shares[k], ('ctx', 'head'), pairs)  9.94 us
    unnamed x32, local copies, waits for them, and re-layouts  7.55 us
    ppermute x4, waiting for transfers between devices, local_blocks(): share = lax.ppermute(shares[k], ('ctx', 'head'), pairs)  4.86 us
    pallas_call x1, Pallas kernels, attention(): pl.pallas_call(body, out_shape=[pltpu.VMEM((length, width), jnp.bfloat16)...  4.62 us
    ppermute x15, waiting for transfers between devices, move(): return in_vmem(lax.ppermute(x, axis, pairs))  2.16 us
    pallas_call x1, Pallas kernels, pack_weight(): pl.pallas_call(body, out_shape=[pltpu.VMEM((weight.shape[0], width), jnp....  2.15 us
  transfers between devices with their start and end apart: 19, of which 4 were waited for; matrix products, arithmetic and copies ran while one was open for 0% of the time, Pallas kernels for 13%

profile of v4, /device:TPU:1, one launch (start us, length us, event | category | flops | bytes accessed | tf_op | source)
XLA Modules:
  0.0 64.9 jit_solution(5571529730873967420)
XLA Ops:
  0.6 1.2 %pack_heads.1 = (bf16[136,768]{1,0:T(8,128)(2,1)S(1)}, bf16[136,768]{1,0:T(8,128)(2,1)S(1)}, bf16[136,768]{1,0:T(8,128)(2,1)S(1)}, bf16[136,768]{1,0:T(8,128)(2,...) custom-call(s32[1]{0:T(128)} %bitcast.c_ref, ...), custom_call_target="tpu_custom_call" | custom-call | tf_op jit(solution)/shard_map/pack_heads/pallas_call | solution.py:58
  1.9 2.1 %collective-permute-start = (bf16[136,768]{1,0:T(8,128)(2,1)S(1)}, bf16[136,768]{1,0:T(8,128)(2,1)S(1)}, u32[]{:S(2)}, u32[]{:S(2)}) collective-permute-start(bf16[136,768]{1,0:T(8,128)(2,1)S(1)} %get-tuple-element.26), channel_id=1, source_target_pairs={{0,2},{2,0},{4,6},{6,4},{8,10},{10,8},{12,14},{14,12},{1,3},{3,1},... | collective-permute-start | bytes 626696 | tf_op jit(solution)/shard_map/ppermute | solution.py:311
  4.0 4.2 %collective-permute-start.3 = (bf16[128,256]{1,0:T(8,128)(2,1)S(1)}, bf16[128,256]{1,0:T(8,128)(2,1)S(1)}, u32[]{:S(2)}, u32[]{:S(2)}) collective-permute-start(bf16[128,256]{1,0:T(8,128)(2,1)S(1)} %get-tuple-element.29), channel_id=1, source_target_pairs={{0,8},{2,10},{4,12},{6,14},{1,9},{3,11},{5,13},{7,15},{16,24},{18,... | collective-permute-start | bytes 196616 | tf_op jit(solution)/shard_map/ppermute | solution.py:311
  8.2 1.3 %collective-permute-start.4 = (bf16[128,256]{1,0:T(8,128)(2,1)S(1)}, bf16[128,256]{1,0:T(8,128)(2,1)S(1)}, u32[]{:S(2)}, u32[]{:S(2)}) collective-permute-start(bf16[128,256]{1,0:T(8,128)(2,1)S(1)} %get-tuple-element.30), channel_id=1, source_target_pairs={{0,10},{2,8},{4,14},{6,12},{1,11},{3,9},{5,15},{7,13},{16,26},{18,... | collective-permute-start | bytes 196616 | tf_op jit(solution)/shard_map/ppermute | solution.py:311
  9.5 2.3 %collective-permute-start.5 = (bf16[128,256]{1,0:T(8,128)(2,1)S(1)}, bf16[128,256]{1,0:T(8,128)(2,1)S(1)}, u32[]{:S(2)}, u32[]{:S(2)}) collective-permute-start(bf16[128,256]{1,0:T(8,128)(2,1)S(1)} %get-tuple-element.31), channel_id=1, source_target_pairs={{0,12},{2,14},{4,8},{6,10},{1,13},{3,15},{5,9},{7,11},{16,28},{18,... | collective-permute-start | bytes 196616 | tf_op jit(solution)/shard_map/ppermute | solution.py:311
  11.8 1.3 %collective-permute-start.6 = (bf16[128,256]{1,0:T(8,128)(2,1)S(1)}, bf16[128,256]{1,0:T(8,128)(2,1)S(1)}, u32[]{:S(2)}, u32[]{:S(2)}) collective-permute-start(bf16[128,256]{1,0:T(8,128)(2,1)S(1)} %get-tuple-element.32), channel_id=1, source_target_pairs={{0,14},{2,12},{4,10},{6,8},{1,15},{3,13},{5,11},{7,9},{16,30},{18,... | collective-permute-start | bytes 196616 | tf_op jit(solution)/shard_map/ppermute | solution.py:311
  13.1 0.0 collective-permute-done.3.rest_4_
  13.1 0.4 collective-permute-start.1
  13.5 0.0 collective-permute-done.4.rest_5_
  13.5 0.6 copy-done.8
  14.1 3.5 %collective-permute-start.2 = (bf16[136,768]{1,0:T(8,128)(2,1)S(1)}, bf16[136,768]{1,0:T(8,128)(2,1)S(1)}, u32[]{:S(2)}, u32[]{:S(2)}) collective-permute-start(bf16[136,768]{1,0:T(8,128)(2,1)S(1)} %get-tuple-element.28), channel_id=1, source_target_pairs={{0,6},{2,4},{4,2},{6,0},{8,14},{10,12},{12,10},{14,8},{1,7},{3,5},... | collective-permute-start | bytes 626696 | tf_op jit(solution)/shard_map/ppermute | solution.py:311
  17.6 2.1 %pack_weight.1 = (bf16[256,512]{1,0:T(8,128)(2,1)S(1)}, bf16[256,512]{1,0:T(8,128)(2,1)}, bf16[256,512]{1,0:T(8,128)(2,1)}, bf16[256,512]{1,0:T(8,128)(2,1)}) custom-call(s32[1]{0:T(128)} %bitcast.c_ref, bf16[256,2048]{1,0:T(8,128)(2,1)} %w_ref.1), custom_call_target="tpu_custom_call" | custom-call | tf_op jit(solution)/shard_map/pack_weight/pallas_call | solution.py:77
  19.7 0.0 collective-permute-done.5.rest_6_
  19.7 1.3 %collective-permute-start.11 = (bf16[256,512]{1,0:T(8,128)(2,1)}, bf16[256,512]{1,0:T(8,128)(2,1)S(1)}, u32[]{:S(2)}, u32[]{:S(2)}) collective-permute-start(bf16[256,512]{1,0:T(8,128)(2,1)} %get-tuple-element.39), channel_id=1, source_target_pairs={{0,2},{2,0},{4,6},{6,4},{8,10},{10,8},{12,14},{14,12},{1,3},{3,1},... | collective-permute-start | bytes 786440 | tf_op jit(solution)/shard_map/ppermute | solution.py:311
  21.0 0.0 collective-permute-done.6.rest_7_
  21.0 0.6 copy-done.10
  21.6 1.4 %collective-permute-start.13 = (bf16[256,512]{1,0:T(8,128)(2,1)}, bf16[256,512]{1,0:T(8,128)(2,1)S(1)}, u32[]{:S(2)}, u32[]{:S(2)}) collective-permute-start(bf16[256,512]{1,0:T(8,128)(2,1)} %get-tuple-element.41), channel_id=1, source_target_pairs={{0,6},{2,4},{4,2},{6,0},{8,14},{10,12},{12,10},{14,8},{1,7},{3,5},... | collective-permute-start | bytes 786440 | tf_op jit(solution)/shard_map/ppermute | solution.py:311
  23.0 1.0 %mask_tiles.1.mask_ref = f32[1408,128]{1,0:T(8,128)S(1)} custom-call(s32[1]{0:T(128)} %bitcast.c_ref, s32[2,4]{1,0:T(2,128)} %bitcast.4), custom_call_target="tpu_custom_call" | custom-call | tf_op jit(solution)/shard_map/mask_tiles/pallas_call | solution.py:103
  24.1 0.0 collective-permute-done.1.rest_2_
  24.1 0.7 %copy-done.4 = bf16[136,768]{1,0:T(8,128)(2,1)} copy-done((bf16[136,768]{1,0:T(8,128)(2,1)}, bf16[136,768]{1,0:T(8,128)(2,1)S(1)}, u32[]{:S(2)}) %copy-start.4) | copy-done | bytes 208920
  24.8 0.7 %copy-done.6 = bf16[136,768]{1,0:T(8,128)(2,1)} copy-done((bf16[136,768]{1,0:T(8,128)(2,1)}, bf16[136,768]{1,0:T(8,128)(2,1)S(1)}, u32[]{:S(2)}) %copy-start.6) | copy-done | bytes 208920
  25.5 0.9 %copy-done.3 = bf16[136,768]{1,0:T(8,128)(2,1)S(1)} copy-done((bf16[136,768]{1,0:T(8,128)(2,1)S(1)}, bf16[136,768]{1,0:T(8,128)(2,1)}, u32[]{:S(2)}) %copy-start.3) | copy-done | bytes 208920
  26.4 0.9 %copy-done.5 = bf16[136,768]{1,0:T(8,128)(2,1)S(1)} copy-done((bf16[136,768]{1,0:T(8,128)(2,1)S(1)}, bf16[136,768]{1,0:T(8,128)(2,1)}, u32[]{:S(2)}) %copy-start.5) | copy-done | bytes 208920
  27.3 0.9 %copy-done.7 = bf16[136,768]{1,0:T(8,128)(2,1)S(1)} copy-done((bf16[136,768]{1,0:T(8,128)(2,1)S(1)}, bf16[136,768]{1,0:T(8,128)(2,1)}, u32[]{:S(2)}) %copy-start.7) | copy-done | bytes 208920
  28.3 0.8 %copy-done.9 = bf16[128,256]{1,0:T(8,128)(2,1)S(1)} copy-done((bf16[128,256]{1,0:T(8,128)(2,1)S(1)}, bf16[128,256]{1,0:T(8,128)(2,1)}, u32[]{:S(2)}) %copy-start.9) | copy-done | bytes 65560
  29.1 4.6 %attention.1 = (bf16[128,512]{1,0:T(8,128)(2,1)S(1)}, bf16[128,512]{1,0:T(8,128)(2,1)S(1)}, bf16[128,512]{1,0:T(8,128)(2,1)S(1)}, bf16[128,512]{1,0:T(8,128)(2,1)S(1)}, bf16[64,512]{1,0:T(8,128)(2,1)S(1)}) custom-call(s32[1]{0:T(128)} %bitcast.c_ref, s32[2,4]{1,0:T(2,128)} %bitcast.5, s32[8]{0:T(128)} %count_ref.1, f32[1408,128]{1,0:T(8,128)S(1)} %mask_tiles.1.mask_ref, ...), custom_call_target="tpu_custom_call" | custom-call | tf_op jit(solution)/shard_map/attention/pallas_call | solution.py:206
  33.8 0.6 copy-done.12
  34.4 0.6 copy-done.14
  35.0 4.6 %collective-permute-start.10 = (bf16[64,512]{1,0:T(8,128)(2,1)S(1)}, bf16[64,512]{1,0:T(8,128)(2,1)S(1)}, u32[]{:S(2)}, u32[]{:S(2)}) collective-permute-start(bf16[64,512]{1,0:T(8,128)(2,1)S(1)} %get-tuple-element.37.own_ref), channel_id=1, source_target_pairs={{0,8},{2,10},{4,12},{6,14},{8,0},{10,2},{12,4},{14,6},{1,9},{3,11}... | collective-permute-start | bytes 196616 | tf_op jit(solution)/shard_map/ppermute | solution.py:311
  39.6 0.0 collective-permute-done.11.rest_1_
  39.6 0.0 collective-permute-done.12.rest_2_
  39.6 0.0 collective-permute-done.13.rest_3_
  39.6 2.1 %collective-permute-done.10.other_ref = bf16[64,512]{1,0:T(8,128)(2,1)S(1)} collective-permute-done((bf16[64,512]{1,0:T(8,128)(2,1)S(1)}, bf16[64,512]{1,0:T(8,128)(2,1)S(1)}, u32[]{:S(2)}, u32[]{:S(2)}) %collective-permute-start.10) | collective-permute-done | bytes 65568 | tf_op jit(solution)/shard_map/ppermute | solution.py:311
  41.8 0.5 project.1
  42.2 3.7 %collective-permute-start.14 = (f32[64,1024]{1,0:T(8,128)S(1)}, f32[64,1024]{1,0:T(8,128)S(1)}, u32[]{:S(2)}, u32[]{:S(2)}) collective-permute-start(f32[64,1024]{1,0:T(8,128)S(1)} %get-tuple-element.43), channel_id=1, source_target_pairs={{0,1},{1,0},{2,3},{3,2},{4,5},{5,4},{6,7},{7,6},{8,9},{9,8},{10,11... | collective-permute-start | bytes 786440 | tf_op jit(solution)/shard_map/ppermute | solution.py:311
  45.9 1.6 %collective-permute-start.8 = (bf16[128,512]{1,0:T(8,128)(2,1)S(1)}, bf16[128,512]{1,0:T(8,128)(2,1)S(1)}, u32[]{:S(2)}, u32[]{:S(2)}) collective-permute-start(bf16[128,512]{1,0:T(8,128)(2,1)S(1)} %copy-done.13), channel_id=1, source_target_pairs={{0,4},{2,6},{4,0},{6,2},{8,12},{10,14},{12,8},{14,10},{1,5},{3,7},... | collective-permute-start | bytes 393224 | tf_op jit(solution)/shard_map/ppermute | solution.py:311
  47.5 1.1 %collective-permute-start.9 = (bf16[128,512]{1,0:T(8,128)(2,1)S(1)}, bf16[128,512]{1,0:T(8,128)(2,1)S(1)}, u32[]{:S(2)}, u32[]{:S(2)}) collective-permute-start(bf16[128,512]{1,0:T(8,128)(2,1)S(1)} %get-tuple-element.36), channel_id=1, source_target_pairs={{0,6},{2,4},{4,2},{6,0},{8,14},{10,12},{12,10},{14,8},{1,7},{3,5},... | collective-permute-start | bytes 393224 | tf_op jit(solution)/shard_map/ppermute | solution.py:311
  48.6 0.0 collective-permute-done.14.b_ref
  48.6 5.4 %collective-permute-start.15 = (bf16[16,1024]{1,0:T(8,128)(2,1)S(1)}, bf16[16,1024]{1,0:T(8,128)(2,1)S(1)}, u32[]{:S(2)}, u32[]{:S(2)}) collective-permute-start(bf16[16,1024]{1,0:T(8,128)(2,1)S(1)} %get-tuple-element.44), channel_id=1, source_target_pairs={{0,0},{1,8},{2,2},{3,10},{4,4},{5,12},{6,6},{7,14},{8,1},{9,9},{10... | collective-permute-start | bytes 98312 | tf_op jit(solution)/shard_map/ppermute | solution.py:342
  54.0 0.1 collective-permute-start.16
  54.1 0.0 collective-permute-done.7.rest_1_
  54.1 4.1 %collective-permute-start.17 = (bf16[16,1024]{1,0:T(8,128)(2,1)S(1)}, bf16[16,1024]{1,0:T(8,128)(2,1)S(1)}, u32[]{:S(2)}, u32[]{:S(2)}) collective-permute-start(bf16[16,1024]{1,0:T(8,128)(2,1)S(1)} %get-tuple-element.46), channel_id=1, source_target_pairs={{0,4},{1,12},{2,6},{3,14},{4,0},{5,8},{6,2},{7,10},{8,5},{9,13},{1... | collective-permute-start | bytes 98312 | tf_op jit(solution)/shard_map/ppermute | solution.py:342
  58.2 0.3 collective-permute-start.18
  58.6 0.8 %join_heads.1 = bf16[128,2048]{1,0:T(8,128)(2,1)} custom-call(s32[1]{0:T(128)} %bitcast.c_ref, bf16[128,512]{1,0:T(8,128)(2,1)S(1)} %get-tuple-element.33.rest_0_, bf16[128,512]{1,0:T(8,128)(2,1)S(1)} %collective-permute-done.7.rest_1_, bf16[128,512]{1,0:T(8,128)(2,1)S(1)} %collective-permute-done.8.rest_2_, bf16[128,512]{1,0:T(8,128)(2,1)S(1)} %collective-permute-done.9.rest_3_), custom_call_target="tpu_custom_call" | custom-call | tf_op jit(solution)/shard_map/join_heads/pallas_call | solution.py:283
  59.4 0.2 collective-permute-done.16
  59.6 0.6 collective-permute-done.17
  60.2 4.1 %collective-permute-done.18 = bf16[16,1024]{1,0:T(8,128)(2,1)S(1)} collective-permute-done((bf16[16,1024]{1,0:T(8,128)(2,1)S(1)}, bf16[16,1024]{1,0:T(8,128)(2,1)S(1)}, u32[]{:S(2)}, u32[]{:S(2)}) %collective-permute-start.18) | collective-permute-done | bytes 32800 | tf_op jit(solution)/shard_map/ppermute | solution.py:342
  64.3 0.6 add_convert_fusion
  (30 shorter events, 0.1 us)
Async XLA Ops:
  1.9 17.8 %copy-start = (bf16[136,768]{1,0:T(8,128)(2,1)}, bf16[136,768]{1,0:T(8,128)(2,1)S(1)}, u32[]{:S(2)}) copy-start(bf16[136,768]{1,0:T(8,128)(2,1)S(1)} %get-tuple-element.25.rest_0_) | copy-start | bytes 626692
  1.9 19.7 %collective-permute-start = (bf16[136,768]{1,0:T(8,128)(2,1)S(1)}, bf16[136,768]{1,0:T(8,128)(2,1)S(1)}, u32[]{:S(2)}, u32[]{:S(2)}) collective-permute-start(bf16[136,768]{1,0:T(8,128)(2,1)S(1)} %get-tuple-element.26), channel_id=1, source_target_pairs={{0,2},{2,0},{4,6},{6,4},{8,10},{10,8},{12,14},{14,12},{1,3},{3,1},... | collective-permute-start | bytes 626696 | tf_op jit(solution)/shard_map/ppermute | solution.py:311
  4.0 9.1 %collective-permute-start.3 = (bf16[128,256]{1,0:T(8,128)(2,1)S(1)}, bf16[128,256]{1,0:T(8,128)(2,1)S(1)}, u32[]{:S(2)}, u32[]{:S(2)}) collective-permute-start(bf16[128,256]{1,0:T(8,128)(2,1)S(1)} %get-tuple-element.29), channel_id=1, source_target_pairs={{0,8},{2,10},{4,12},{6,14},{1,9},{3,11},{5,13},{7,15},{16,24},{18,... | collective-permute-start | bytes 196616 | tf_op jit(solution)/shard_map/ppermute | solution.py:311
  8.2 5.3 %collective-permute-start.4 = (bf16[128,256]{1,0:T(8,128)(2,1)S(1)}, bf16[128,256]{1,0:T(8,128)(2,1)S(1)}, u32[]{:S(2)}, u32[]{:S(2)}) collective-permute-start(bf16[128,256]{1,0:T(8,128)(2,1)S(1)} %get-tuple-element.30), channel_id=1, source_target_pairs={{0,10},{2,8},{4,14},{6,12},{1,11},{3,9},{5,15},{7,13},{16,26},{18,... | collective-permute-start | bytes 196616 | tf_op jit(solution)/shard_map/ppermute | solution.py:311
  9.5 10.2 %collective-permute-start.5 = (bf16[128,256]{1,0:T(8,128)(2,1)S(1)}, bf16[128,256]{1,0:T(8,128)(2,1)S(1)}, u32[]{:S(2)}, u32[]{:S(2)}) collective-permute-start(bf16[128,256]{1,0:T(8,128)(2,1)S(1)} %get-tuple-element.31), channel_id=1, source_target_pairs={{0,12},{2,14},{4,8},{6,10},{1,13},{3,15},{5,9},{7,11},{16,28},{18,... | collective-permute-start | bytes 196616 | tf_op jit(solution)/shard_map/ppermute | solution.py:311
  11.8 9.2 %collective-permute-start.6 = (bf16[128,256]{1,0:T(8,128)(2,1)S(1)}, bf16[128,256]{1,0:T(8,128)(2,1)S(1)}, u32[]{:S(2)}, u32[]{:S(2)}) collective-permute-start(bf16[128,256]{1,0:T(8,128)(2,1)S(1)} %get-tuple-element.32), channel_id=1, source_target_pairs={{0,14},{2,12},{4,10},{6,8},{1,15},{3,13},{5,11},{7,9},{16,30},{18,... | collective-permute-start | bytes 196616 | tf_op jit(solution)/shard_map/ppermute | solution.py:311
  13.1 11.0 %collective-permute-start.1 = (bf16[136,768]{1,0:T(8,128)(2,1)S(1)}, bf16[136,768]{1,0:T(8,128)(2,1)S(1)}, u32[]{:S(2)}, u32[]{:S(2)}) collective-permute-start(bf16[136,768]{1,0:T(8,128)(2,1)S(1)} %get-tuple-element.27), channel_id=1, source_target_pairs={{0,4},{2,6},{4,0},{6,2},{8,12},{10,14},{12,8},{14,10},{1,5},{3,7},... | collective-permute-start | bytes 626696 | tf_op jit(solution)/shard_map/ppermute | solution.py:311
  13.5 0.6 copy-start.8
  14.1 10.7 %collective-permute-start.2 = (bf16[136,768]{1,0:T(8,128)(2,1)S(1)}, bf16[136,768]{1,0:T(8,128)(2,1)S(1)}, u32[]{:S(2)}, u32[]{:S(2)}) collective-permute-start(bf16[136,768]{1,0:T(8,128)(2,1)S(1)} %get-tuple-element.28), channel_id=1, source_target_pairs={{0,6},{2,4},{4,2},{6,0},{8,14},{10,12},{12,10},{14,8},{1,7},{3,5},... | collective-permute-start | bytes 626696 | tf_op jit(solution)/shard_map/ppermute | solution.py:311
  19.7 19.9 %collective-permute-start.11 = (bf16[256,512]{1,0:T(8,128)(2,1)}, bf16[256,512]{1,0:T(8,128)(2,1)S(1)}, u32[]{:S(2)}, u32[]{:S(2)}) collective-permute-start(bf16[256,512]{1,0:T(8,128)(2,1)} %get-tuple-element.39), channel_id=1, source_target_pairs={{0,2},{2,0},{4,6},{6,4},{8,10},{10,8},{12,14},{14,12},{1,3},{3,1},... | collective-permute-start | bytes 786440 | tf_op jit(solution)/shard_map/ppermute | solution.py:311
  21.0 0.6 copy-start.10
  21.6 18.0 %collective-permute-start.12 = (bf16[256,512]{1,0:T(8,128)(2,1)}, bf16[256,512]{1,0:T(8,128)(2,1)S(1)}, u32[]{:S(2)}, u32[]{:S(2)}) collective-permute-start(bf16[256,512]{1,0:T(8,128)(2,1)} %get-tuple-element.40), channel_id=1, source_target_pairs={{0,4},{2,6},{4,0},{6,2},{8,12},{10,14},{12,8},{14,10},{1,5},{3,7},... | collective-permute-start | bytes 786440 | tf_op jit(solution)/shard_map/ppermute | solution.py:311
  21.6 2.4 %copy-start.2 = (bf16[136,768]{1,0:T(8,128)(2,1)}, bf16[136,768]{1,0:T(8,128)(2,1)S(1)}, u32[]{:S(2)}) copy-start(bf16[136,768]{1,0:T(8,128)(2,1)S(1)} %collective-permute-done.rest_1_) | copy-start | bytes 626692
  21.6 18.0 %collective-permute-start.13 = (bf16[256,512]{1,0:T(8,128)(2,1)}, bf16[256,512]{1,0:T(8,128)(2,1)S(1)}, u32[]{:S(2)}, u32[]{:S(2)}) collective-permute-start(bf16[256,512]{1,0:T(8,128)(2,1)} %get-tuple-element.41), channel_id=1, source_target_pairs={{0,6},{2,4},{4,2},{6,0},{8,14},{10,12},{12,10},{14,8},{1,7},{3,5},... | collective-permute-start | bytes 786440 | tf_op jit(solution)/shard_map/ppermute | solution.py:311
  23.0 2.4 %copy-start.1 = (bf16[136,768]{1,0:T(8,128)(2,1)S(1)}, bf16[136,768]{1,0:T(8,128)(2,1)}, u32[]{:S(2)}) copy-start(bf16[136,768]{1,0:T(8,128)(2,1)} %copy-done) | copy-start | bytes 626692
  23.0 2.4 %copy-start.11 = (bf16[128,256]{1,0:T(8,128)(2,1)S(1)}, bf16[128,256]{1,0:T(8,128)(2,1)}, u32[]{:S(2)}) copy-start(bf16[128,256]{1,0:T(8,128)(2,1)} %copy-done.10) | copy-start | bytes 196612
  24.1 0.7 %copy-start.4 = (bf16[136,768]{1,0:T(8,128)(2,1)}, bf16[136,768]{1,0:T(8,128)(2,1)S(1)}, u32[]{:S(2)}) copy-start(bf16[136,768]{1,0:T(8,128)(2,1)S(1)} %collective-permute-done.1.rest_2_) | copy-start | bytes 626692
  24.8 0.7 %copy-start.6 = (bf16[136,768]{1,0:T(8,128)(2,1)}, bf16[136,768]{1,0:T(8,128)(2,1)S(1)}, u32[]{:S(2)}) copy-start(bf16[136,768]{1,0:T(8,128)(2,1)S(1)} %collective-permute-done.2.rest_3_) | copy-start | bytes 626692
  25.5 0.9 %copy-start.3 = (bf16[136,768]{1,0:T(8,128)(2,1)S(1)}, bf16[136,768]{1,0:T(8,128)(2,1)}, u32[]{:S(2)}) copy-start(bf16[136,768]{1,0:T(8,128)(2,1)} %copy-done.2) | copy-start | bytes 626692
  26.4 0.9 %copy-start.5 = (bf16[136,768]{1,0:T(8,128)(2,1)S(1)}, bf16[136,768]{1,0:T(8,128)(2,1)}, u32[]{:S(2)}) copy-start(bf16[136,768]{1,0:T(8,128)(2,1)} %copy-done.4) | copy-start | bytes 626692
  27.3 0.9 %copy-start.7 = (bf16[136,768]{1,0:T(8,128)(2,1)S(1)}, bf16[136,768]{1,0:T(8,128)(2,1)}, u32[]{:S(2)}) copy-start(bf16[136,768]{1,0:T(8,128)(2,1)} %copy-done.6) | copy-start | bytes 626692
  28.3 0.8 %copy-start.9 = (bf16[128,256]{1,0:T(8,128)(2,1)S(1)}, bf16[128,256]{1,0:T(8,128)(2,1)}, u32[]{:S(2)}) copy-start(bf16[128,256]{1,0:T(8,128)(2,1)} %copy-done.8) | copy-start | bytes 196612
  33.7 0.7 %copy-start.12 = (bf16[128,512]{1,0:T(8,128)(2,1)}, bf16[128,512]{1,0:T(8,128)(2,1)S(1)}, u32[]{:S(2)}) copy-start(bf16[128,512]{1,0:T(8,128)(2,1)S(1)} %get-tuple-element.35) | copy-start | bytes 393220
  34.4 0.6 copy-start.14
  35.0 6.7 %collective-permute-start.10 = (bf16[64,512]{1,0:T(8,128)(2,1)S(1)}, bf16[64,512]{1,0:T(8,128)(2,1)S(1)}, u32[]{:S(2)}, u32[]{:S(2)}) collective-permute-start(bf16[64,512]{1,0:T(8,128)(2,1)S(1)} %get-tuple-element.37.own_ref), channel_id=1, source_target_pairs={{0,8},{2,10},{4,12},{6,14},{8,0},{10,2},{12,4},{14,6},{1,9},{3,11}... | collective-permute-start | bytes 196616 | tf_op jit(solution)/shard_map/ppermute | solution.py:311
  41.7 4.2 %copy-start.15 = (bf16[128,512]{1,0:T(8,128)(2,1)S(1)}, bf16[128,512]{1,0:T(8,128)(2,1)}, u32[]{:S(2)}) copy-start(bf16[128,512]{1,0:T(8,128)(2,1)} %copy-done.14) | copy-start | bytes 393220
  41.7 4.2 %copy-start.13 = (bf16[128,512]{1,0:T(8,128)(2,1)S(1)}, bf16[128,512]{1,0:T(8,128)(2,1)}, u32[]{:S(2)}) copy-start(bf16[128,512]{1,0:T(8,128)(2,1)} %copy-done.12) | copy-start | bytes 393220
  42.2 6.3 %collective-permute-start.14 = (f32[64,1024]{1,0:T(8,128)S(1)}, f32[64,1024]{1,0:T(8,128)S(1)}, u32[]{:S(2)}, u32[]{:S(2)}) collective-permute-start(f32[64,1024]{1,0:T(8,128)S(1)} %get-tuple-element.43), channel_id=1, source_target_pairs={{0,1},{1,0},{2,3},{3,2},{4,5},{5,4},{6,7},{7,6},{8,9},{9,8},{10,11... | collective-permute-start | bytes 786440 | tf_op jit(solution)/shard_map/ppermute | solution.py:311
  45.9 8.2 %collective-permute-start.7 = (bf16[128,512]{1,0:T(8,128)(2,1)S(1)}, bf16[128,512]{1,0:T(8,128)(2,1)S(1)}, u32[]{:S(2)}, u32[]{:S(2)}) collective-permute-start(bf16[128,512]{1,0:T(8,128)(2,1)S(1)} %copy-done.15), channel_id=1, source_target_pairs={{0,2},{2,0},{4,6},{6,4},{8,10},{10,8},{12,14},{14,12},{1,3},{3,1},... | collective-permute-start | bytes 393224 | tf_op jit(solution)/shard_map/ppermute | solution.py:311
  45.9 12.3 %collective-permute-start.8 = (bf16[128,512]{1,0:T(8,128)(2,1)S(1)}, bf16[128,512]{1,0:T(8,128)(2,1)S(1)}, u32[]{:S(2)}, u32[]{:S(2)}) collective-permute-start(bf16[128,512]{1,0:T(8,128)(2,1)S(1)} %copy-done.13), channel_id=1, source_target_pairs={{0,4},{2,6},{4,0},{6,2},{8,12},{10,14},{12,8},{14,10},{1,5},{3,7},... | collective-permute-start | bytes 393224 | tf_op jit(solution)/shard_map/ppermute | solution.py:311
  47.5 11.1 %collective-permute-start.9 = (bf16[128,512]{1,0:T(8,128)(2,1)S(1)}, bf16[128,512]{1,0:T(8,128)(2,1)S(1)}, u32[]{:S(2)}, u32[]{:S(2)}) collective-permute-start(bf16[128,512]{1,0:T(8,128)(2,1)S(1)} %get-tuple-element.36), channel_id=1, source_target_pairs={{0,6},{2,4},{4,2},{6,0},{8,14},{10,12},{12,10},{14,8},{1,7},{3,5},... | collective-permute-start | bytes 393224 | tf_op jit(solution)/shard_map/ppermute | solution.py:311
  48.6 10.8 %collective-permute-start.15 = (bf16[16,1024]{1,0:T(8,128)(2,1)S(1)}, bf16[16,1024]{1,0:T(8,128)(2,1)S(1)}, u32[]{:S(2)}, u32[]{:S(2)}) collective-permute-start(bf16[16,1024]{1,0:T(8,128)(2,1)S(1)} %get-tuple-element.44), channel_id=1, source_target_pairs={{0,0},{1,8},{2,2},{3,10},{4,4},{5,12},{6,6},{7,14},{8,1},{9,9},{10... | collective-permute-start | bytes 98312 | tf_op jit(solution)/shard_map/ppermute | solution.py:342
  54.0 5.6 %collective-permute-start.16 = (bf16[16,1024]{1,0:T(8,128)(2,1)S(1)}, bf16[16,1024]{1,0:T(8,128)(2,1)S(1)}, u32[]{:S(2)}, u32[]{:S(2)}) collective-permute-start(bf16[16,1024]{1,0:T(8,128)(2,1)S(1)} %get-tuple-element.45), channel_id=1, source_target_pairs={{0,2},{1,10},{2,0},{3,8},{4,6},{5,14},{6,4},{7,12},{8,3},{9,11},{1... | collective-permute-start | bytes 98312 | tf_op jit(solution)/shard_map/ppermute | solution.py:342
  54.1 6.0 %collective-permute-start.17 = (bf16[16,1024]{1,0:T(8,128)(2,1)S(1)}, bf16[16,1024]{1,0:T(8,128)(2,1)S(1)}, u32[]{:S(2)}, u32[]{:S(2)}) collective-permute-start(bf16[16,1024]{1,0:T(8,128)(2,1)S(1)} %get-tuple-element.46), channel_id=1, source_target_pairs={{0,4},{1,12},{2,6},{3,14},{4,0},{5,8},{6,2},{7,10},{8,5},{9,13},{1... | collective-permute-start | bytes 98312 | tf_op jit(solution)/shard_map/ppermute | solution.py:342
  58.2 6.0 %collective-permute-start.18 = (bf16[16,1024]{1,0:T(8,128)(2,1)S(1)}, bf16[16,1024]{1,0:T(8,128)(2,1)S(1)}, u32[]{:S(2)}, u32[]{:S(2)}) collective-permute-start(bf16[16,1024]{1,0:T(8,128)(2,1)S(1)} %get-tuple-element.47), channel_id=1, source_target_pairs={{0,6},{1,14},{2,4},{3,12},{4,2},{5,10},{6,0},{7,8},{8,7},{9,15},{1... | collective-permute-start | bytes 98312 | tf_op jit(solution)/shard_map/ppermute | solution.py:342

commit v5 on v4

--- a/solution.py
+++ b/solution.py
@@ -18,8 +18,10 @@
 MASKED = -1e30
 
 
+ANY = pl.BlockSpec(memory_space=pl.ANY)
 SMEM = pl.BlockSpec(memory_space=pltpu.SMEM)
 VMEM = pl.BlockSpec(memory_space=pltpu.VMEM)
+GRANT = pltpu.CompilerParams(vmem_limit_bytes=16 << 20)
 
 
 def xor_pairs(size, k):
@@ -28,6 +30,20 @@
 
 def in_vmem(x):
     return pltpu.with_memory_space_constraint(x, pltpu.VMEM)
+
+
+def in_hbm(x):
+    return pltpu.with_memory_space_constraint(x, pltpu.HBM)
+
+
+def start_all(copies, sems):
+    started = [
+        pltpu.make_async_copy(source, target, sems.at[number])
+        for number, (source, target) in enumerate(copies)
+    ]
+    for copy in started:
+        copy.start()
+    return started
 
 
 def pack_heads(shard_index, query, key, value, kept_rows, heads):
@@ -37,98 +53,144 @@
     capacity = kept_rows.shape[1]
     total = 2 * hd + width
 
-    def body(c_ref, q_ref, k_ref, v_ref, kept_ref, *out):
+    def body(c_ref, q_ref, k_ref, v_ref, kept_ref, *rest):
+        out, (kept_buf, sems) = rest[: 2 * heads], rest[2 * heads :]
         slot = c_ref[0] % heads
-        kept = jnp.zeros((PAD_ROWS, total), jnp.bfloat16)
+        copies = [(kept_ref, kept_buf)]
         for j in range(heads):
             head = slot ^ j
-            q_at = pl.multiple_of(head * width, hd)
-            k_at = pl.multiple_of(head * hd, hd)
-            k, v = k_ref[:, pl.ds(k_at, hd)], v_ref[:, pl.ds(k_at, hd)]
-            out[j][0:length, 0:hd] = k
-            out[j][0:length, hd : 2 * hd] = v
-            out[j][0:length, 2 * hd :] = q_ref[:, pl.ds(q_at, width)]
-            out[j][length:, :] = kept
-            out[j][length : length + 1, 0:capacity] = (
-                kept_ref[...].astype(jnp.float32).astype(jnp.bfloat16)
-            )
-            out[heads + j][:, 0:hd] = k
-            out[heads + j][:, hd:] = v
+            q_from = q_ref.at[:, pl.ds(pl.multiple_of(head * width, hd), width)]
+            k_from = k_ref.at[:, pl.ds(pl.multiple_of(head * hd, hd), hd)]
+            v_from = v_ref.at[:, pl.ds(pl.multiple_of(head * hd, hd), hd)]
+            rows = pl.ds(0, length)
+            copies += [
+                (q_from, out[j].at[rows, pl.ds(2 * hd, width)]),
+                (k_from, out[j].at[rows, pl.ds(0, hd)]),
+                (v_from, out[j].at[rows, pl.ds(hd, hd)]),
+                (k_from, out[heads + j].at[:, pl.ds(0, hd)]),
+                (v_from, out[heads + j].at[:, pl.ds(hd, hd)]),
+            ]
+        started = start_all(copies, sems)
+        for j in range(heads):
+            out[j][length:, :] = jnp.zeros((PAD_ROWS, total), jnp.bfloat16)
+        started[0].wait()
+        kept = kept_buf[...].astype(jnp.float32).astype(jnp.bfloat16)
+        for j in range(heads):
+            out[j][length : length + 1, 0:capacity] = kept
+        for copy in started[1:]:
+            copy.wait()
 
     return pl.pallas_call(
         body,
         out_shape=[pltpu.VMEM((length + PAD_ROWS, total), jnp.bfloat16)] * heads
         + [pltpu.VMEM((length, 2 * hd), jnp.bfloat16)] * heads,
-        in_specs=[SMEM] + [VMEM] * 4,
+        in_specs=[SMEM] + [ANY] * 4,
         out_specs=[VMEM] * (2 * heads),
+        scratch_shapes=[
+            pltpu.VMEM((1, capacity), jnp.int32),
+            pltpu.SemaphoreType.DMA((1 + 5 * heads,)),
+        ],
+        compiler_params=GRANT,
         name="pack_heads",
-    )(shard_index, query, key, value, kept_rows)
-
-
-def pack_weight(shard_index, weight, heads):
+    )(shard_index, in_hbm(query), in_hbm(key), in_hbm(value), in_hbm(kept_rows))
+
+
+def pack_weight(shard_index, group_index, weight, heads):
     width = weight.shape[1] // heads
-
-    def body(c_ref, w_ref, *out):
+    outs = weight.shape[0]
+    counts = [outs] * (heads - 1) + [outs // 2]
+
+    def body(c_ref, g_ref, w_ref, *rest):
+        out, sems = rest[:heads], rest[heads]
         slot = c_ref[0] % heads
+        copies = []
         for j in range(heads):
             at = pl.multiple_of((slot ^ j) * width, HEAD_SIZE)
-            out[j][...] = w_ref[:, pl.ds(at, width)]
-
-    return pl.pallas_call(
-        body,
-        out_shape=[pltpu.VMEM((weight.shape[0], width), jnp.bfloat16)] * heads,
-        in_specs=[SMEM, VMEM],
+            first = pl.multiple_of(g_ref[0] * counts[j], counts[j]) if counts[j] < outs else 0
+            copies.append((w_ref.at[pl.ds(first, counts[j]), pl.ds(at, width)], out[j]))
+        for copy in start_all(copies, sems):
+            copy.wait()
+
+    return pl.pallas_call(
+        body,
+        out_shape=[pltpu.VMEM((count, width), jnp.bfloat16) for count in counts],
+        in_specs=[SMEM, SMEM, ANY],
         out_specs=[VMEM] * heads,
+        scratch_shapes=[pltpu.SemaphoreType.DMA((heads,))],
+        compiler_params=GRANT,
         name="pack_weight",
-    )(shard_index, weight)
-
-
-def mask_tiles(shard_index, slash, shards, length):
-    def body(c_ref, slash_ref, out_ref):
-        slot = c_ref[0] % slash_ref.shape[1]
+    )(shard_index, group_index, in_hbm(weight))
+
+
+def mask_tiles(shard_index, slash, tiles, counts, length):
+    heads = slash.shape[1]
+    size = counts.shape[0]
+    lanes = HEAD_SIZE
+
+    def body(c_ref, slash_ref, tile_ref, count_ref, out_ref, table_ref, tile_buf):
+        c = c_ref[0]
+        slot = c % heads
+        first = c - slot
         difference = lax.broadcasted_iota(jnp.int32, (length, length), 0) - lax.broadcasted_iota(
             jnp.int32, (length, length), 1
         )
-        for d in range(shards):
+        for d in range(size):
             distance = difference + d * length
             allowed = (distance >= 0) & (distance < LOCAL_BAND_KEYS)
             for i in range(slash_ref.shape[0]):
                 offset = slash_ref[i, slot]
                 allowed |= (distance >= offset) & (distance < offset + SLASH_W)
-            out_ref[d * length : (d + 1) * length, :] = jnp.where(allowed, 0.0, MASKED)
-        out_ref[shards * length : (shards + 1) * length, :] = jnp.where(difference >= 0, 0.0, MASKED)
-        rest = lax.broadcasted_iota(jnp.int32, (2 * length, length), 0)
-        out_ref[(shards + 1) * length :, :] = jnp.where(rest < length, 0.0, MASKED)
-
-    return pl.pallas_call(
-        body,
-        out_shape=pltpu.VMEM(((shards + 3) * length, length), jnp.float32),
-        in_specs=[SMEM, SMEM],
-        out_specs=VMEM,
+            tile_buf[d] = jnp.where(allowed, 0.0, MASKED)
+        tile_buf[size] = jnp.where(difference >= 0, 0.0, MASKED)
+        tile_buf[size + 1] = jnp.zeros((length, length), jnp.float32)
+        tile_buf[size + 2] = jnp.full((length, length), MASKED, jnp.float32)
+        before = jnp.int32(0)
+        for s in range(heads):
+            shards = [c ^ k for k in range(heads, size)] + [first + t for t in range(s + 1)]
+            for number, k_shard in enumerate(shards):
+                back = first + s - k_shard
+                entry = back
+                for i in range(tile_ref.shape[0]):
+                    vertical = size + jnp.where(back == 0, 0, 1)
+                    entry = jnp.where(tile_ref[i, slot] == k_shard, vertical, entry)
+                entry = jnp.where(back < 0, size + 2, entry)
+                out_ref[s, :, number * length : (number + 1) * length] = tile_buf[entry]
+            count = count_ref[first + s]
+            table_ref[s, 0:1, :] = jnp.full((1, lanes), count, jnp.int32)
+            table_ref[s, 1:2, :] = jnp.full((1, lanes), before, jnp.int32)
+            before = before + count
+
+    return pl.pallas_call(
+        body,
+        out_shape=[
+            pltpu.VMEM((heads, length, size * length), jnp.float32),
+            pltpu.VMEM((heads, 8, lanes), jnp.int32),
+        ],
+        in_specs=[SMEM] * 4,
+        out_specs=[VMEM] * 2,
+        scratch_shapes=[pltpu.VMEM((size + 3, length, length), jnp.float32)],
+        compiler_params=GRANT,
         name="mask_tiles",
-    )(shard_index, slash)
-
-
-def attention(shard_index, tiles, counts, masks, near, far, keep_rows):
+    )(shard_index, in_hbm(slash), in_hbm(tiles), in_hbm(counts))
+
+
+def attention(shard_index, masks, table, near, far, keep_rows):
     heads = len(near)
     length = near[0].shape[0] - PAD_ROWS
     hd = HEAD_SIZE
     width = near[0].shape[1] - 2 * hd
     group = width // hd
-    size = heads + len(far)
     far_keys = len(far) * length
     keys = far_keys + heads * length
     block_rows = heads * keep_rows
     factor = hd ** (-0.5) * math.log2(math.e)
 
-    def body(c_ref, tile_ref, count_ref, mask_ref, *rest):
+    def body(c_ref, mask_ref, table_ref, *rest):
         near_refs, rest = rest[:heads], rest[heads:]
         far_refs, rest = rest[: len(far)], rest[len(far) :]
         out_refs, rows_ref = rest[:heads], rest[heads]
         q_all, k_all, v_all, kept_all, mixed_all = rest[heads + 1 :]
-        c = c_ref[0]
-        slot = c % heads
-        first = c - slot
+        slot = c_ref[0] % heads
         for k in range(len(far)):
             k_all[k * length : (k + 1) * length, :] = far_refs[k][:, 0:hd]
             v_all[k * length : (k + 1) * length, 0:hd] = far_refs[k][:, hd:]
@@ -145,24 +207,9 @@
                 ]
             kept_at = pl.ds(pl.multiple_of(to * PAD_ROWS, PAD_ROWS), PAD_ROWS)
             kept_all[kept_at, :] = near_refs[k][length:, 0:hd].astype(jnp.float32)
-        verticals = [tile_ref[i, slot] for i in range(VTILES)]
-
-        def mask_of(q_shard, k_shard):
-            back = q_shard - k_shard
-            entry = back
-            for tile in verticals:
-                vertical = size + jnp.where(back == 0, 0, 1)
-                entry = jnp.where(tile == k_shard, vertical, entry)
-            entry = jnp.where(back < 0, size + 2, entry)
-            return mask_ref[pl.ds(pl.multiple_of(entry * length, length), length), :]
-
         rows = jnp.zeros((block_rows, width), jnp.float32)
-        before = jnp.int32(0)
         for s in range(heads):
-            q_shard = first + s
-            shards = [c ^ (heads + k) for k in range(len(far))] + [first + t for t in range(s + 1)]
-            mask = jnp.concatenate([mask_of(q_shard, shard) for shard in shards], 1)
-            seen = len(shards) * length
+            seen = far_keys + (s + 1) * length
             rows_at = s * group * length
             scores = lax.dot_general(
                 q_all[rows_at : rows_at + group * length, :],
@@ -170,7 +217,7 @@
                 (((1,), (1,)), ((), ())),
                 preferred_element_type=jnp.float32,
             )
-            scores = scores.reshape(group, length, seen) * factor + mask[None]
+            scores = scores.reshape(group, length, seen) * factor + mask_ref[s, :, 0:seen][None]
             scores = scores.reshape(group * length, seen)
             weights = jnp.exp2(scores - jnp.max(scores, axis=1, keepdims=True))
             mixed = jnp.dot(
@@ -181,12 +228,12 @@
                 mixed_all[s * length : (s + 1) * length, g * hd : (g + 1) * hd] = mixed[
                     g * length : (g + 1) * length
                 ]
-            count = count_ref[q_shard]
             kept = kept_all[s * PAD_ROWS : s * PAD_ROWS + 1, :].astype(jnp.int32)
             token = lax.broadcasted_iota(jnp.int32, (length, hd), 0)
             is_token = (token == kept).astype(jnp.float32).astype(jnp.bfloat16)
             index = lax.broadcasted_iota(jnp.int32, (hd, block_rows), 0)
             place = lax.broadcasted_iota(jnp.int32, (hd, block_rows), 1)
+            count, before = table_ref[s, 0:1, 0:block_rows], table_ref[s, 1:2, 0:block_rows]
             is_place = ((place - index == before) & (index < count)).astype(jnp.float32)
             chooser = jnp.dot(
                 is_token, is_place.astype(jnp.bfloat16), preferred_element_type=jnp.float32
@@ -197,7 +244,6 @@
                 (((0,), (0,)), ((), ())),
                 preferred_element_type=jnp.float32,
             )
-            before = before + count
         rows_ref[...] = rows.astype(jnp.bfloat16)
         for k in range(heads):
             at = pl.multiple_of((slot ^ k) * length, length)
@@ -207,7 +253,7 @@
         body,
         out_shape=[pltpu.VMEM((length, width), jnp.bfloat16)] * heads
         + [pltpu.VMEM((block_rows, width), jnp.bfloat16)],
-        in_specs=[SMEM] * 3 + [VMEM] * (1 + heads + len(far)),
+        in_specs=[SMEM] + [VMEM] * (2 + heads + len(far)),
         out_specs=[VMEM] * (heads + 1),
         scratch_shapes=[
             pltpu.VMEM((heads * group * length, hd), jnp.bfloat16),
@@ -216,38 +262,44 @@
             pltpu.VMEM((heads * PAD_ROWS, hd), jnp.float32),
             pltpu.VMEM((heads * length, width), jnp.bfloat16),
         ],
+        compiler_params=GRANT,
         name="attention",
-    )(shard_index, tiles, counts, masks, *near, *far)
-
-
-def project(shard_index, core_index, own_rows, other_rows, weights):
-    heads = len(weights)
+    )(shard_index, masks, table, *near, *far)
+
+
+def project(shard_index, core_index, group_index, own_rows, other_rows, weights):
+    heads = len(weights) - 1
     count = own_rows.shape[0]
     outs = weights[0].shape[0]
 
-    def body(c_ref, h_ref, own_ref, other_ref, *rest):
-        w_refs, (keep_ref, send_ref) = rest[:heads], rest[heads:]
+    def body(c_ref, h_ref, g_ref, own_ref, other_ref, *rest):
+        w_refs, (keep_ref, send_ref) = rest[: heads + 1], rest[heads + 1 :]
         slot = c_ref[0] % heads
         keeps_own = c_ref[0] // heads == h_ref[0]
         own, other = own_ref[...], other_ref[...]
         both = jnp.concatenate(
             [jnp.where(keeps_own, own, other), jnp.where(keeps_own, other, own)], 0
         )
-        for j in range(heads):
-            at = pl.multiple_of((slot ^ j) * outs, HEAD_SIZE)
+        half = outs // 2
+        last = (slot ^ (heads - 1)) * outs
+        starts = [(slot ^ j) * outs for j in range(heads - 1)]
+        starts += [last + g_ref[0] * half, last + (1 - g_ref[0]) * half]
+        for w_ref, start in zip(w_refs, starts):
+            at = pl.ds(pl.multiple_of(start, HEAD_SIZE), w_ref.shape[0])
             share = lax.dot_general(
-                both, w_refs[j][...], (((1,), (1,)), ((), ())), preferred_element_type=jnp.float32
+                both, w_ref[...], (((1,), (1,)), ((), ())), preferred_element_type=jnp.float32
             )
-            keep_ref[:, pl.ds(at, outs)] = share[:count]
-            send_ref[:, pl.ds(at, outs)] = share[count:]
+            keep_ref[:, at] = share[:count]
+            send_ref[:, at] = share[count:]
 
     return pl.pallas_call(
         body,
         out_shape=[pltpu.VMEM((count, heads * outs), jnp.float32)] * 2,
-        in_specs=[SMEM] * 2 + [VMEM] * (2 + heads),
+        in_specs=[SMEM] * 3 + [VMEM] * (3 + heads),
         out_specs=[VMEM] * 2,
+        compiler_params=GRANT,
         name="project",
-    )(shard_index, core_index, own_rows, other_rows, *weights)
+    )(shard_index, core_index, group_index, own_rows, other_rows, *weights)
 
 
 def split_rows(shard_index, kept, received, heads):
@@ -266,8 +318,26 @@
         out_shape=[pltpu.VMEM((keep_rows, kept.shape[1]), jnp.bfloat16)] * heads,
         in_specs=[SMEM, VMEM, VMEM],
         out_specs=[VMEM] * heads,
+        compiler_params=GRANT,
         name="split_rows",
     )(shard_index, kept, received)
+
+
+def add_shares(shares):
+    def body(*rest):
+        total = rest[0][...].astype(jnp.float32)
+        for share in rest[1:-1]:
+            total = total + share[...].astype(jnp.float32)
+        rest[-1][...] = total.astype(jnp.bfloat16)
+
+    return pl.pallas_call(
+        body,
+        out_shape=pltpu.VMEM(shares[0].shape, jnp.bfloat16),
+        in_specs=[VMEM] * len(shares),
+        out_specs=VMEM,
+        compiler_params=GRANT,
+        name="add_shares",
+    )(*shares)
 
 
 def join_heads(shard_index, pieces):
@@ -275,16 +345,22 @@
     length, width = pieces[0].shape
 
     def body(c_ref, *rest):
+        ins, (out_ref, sems) = rest[:heads], rest[heads:]
         slot = c_ref[0] % heads
+        copies = []
         for j in range(heads):
             at = pl.multiple_of((slot ^ j) * width, HEAD_SIZE)
-            rest[heads][:, pl.ds(at, width)] = rest[j][...]
-
-    return pl.pallas_call(
-        body,
-        out_shape=jax.ShapeDtypeStruct((length, heads * width), jnp.bfloat16),
+            copies.append((ins[j], out_ref.at[:, pl.ds(at, width)]))
+        for copy in start_all(copies, sems):
+            copy.wait()
+
+    return pl.pallas_call(
+        body,
+        out_shape=pltpu.HBM((length, heads * width), jnp.bfloat16),
         in_specs=[SMEM] + [VMEM] * heads,
-        out_specs=VMEM,
+        out_specs=ANY,
+        scratch_shapes=[pltpu.SemaphoreType.DMA((heads,))],
+        compiler_params=GRANT,
         name="join_heads",
     )(shard_index, *pieces)
 
@@ -305,6 +381,7 @@
     keep_rows = query_tensor.shape[0] // 8
     c = lax.axis_index("ctx").astype(jnp.int32)
     shard_index = c.reshape(1)
+    group_index = lax.axis_index("groups").astype(jnp.int32).reshape(1)
     core_index = lax.axis_index("head").astype(jnp.int32).reshape(1)
 
     def move(x, axis, pairs):
@@ -319,29 +396,27 @@
     for k in range(heads, size):
         pairs = [(i, i ^ k) for i in range(size) if i // heads < (i ^ k) // heads]
         far.append(move(packed[heads + k % heads], "ctx", pairs))
-    packed_weight = pack_weight(shard_index, out_weight, heads)
+    packed_weight = pack_weight(shard_index, group_index, out_weight, heads)
     weights = [in_vmem(packed_weight[0])]
     weights += [swap(packed_weight[k], k) for k in range(1, heads)]
-    masks = in_vmem(mask_tiles(shard_index, slash_offsets.T, size, query_tensor.shape[0]))
-    *mixed, rows = attention(
-        shard_index, vertical_tiles.T, kept_count, masks, near, far, keep_rows
-    )
+    weights.append(move(weights[-1], "groups", [(0, 1), (1, 0)]))
+    masks, table = mask_tiles(
+        shard_index, slash_offsets.T, vertical_tiles.T, kept_count, query_tensor.shape[0]
+    )
+    *mixed, rows = attention(shard_index, in_vmem(masks), in_vmem(table), near, far, keep_rows)
     other_rows = move(rows, "ctx", xor_pairs(size, heads))
     returned = [in_vmem(mixed[0])] + [swap(mixed[k], k) for k in range(1, heads)]
-    attended = join_heads(shard_index, returned)
-    kept, sent = project(shard_index, core_index, in_vmem(rows), other_rows, weights)
+    kept, sent = project(shard_index, core_index, group_index, in_vmem(rows), other_rows, weights)
     received = move(sent, "head", [(i, cores - 1 - i) for i in range(cores)])
     shares = split_rows(shard_index, in_vmem(kept), received, heads)
-    total = jnp.zeros(shares[0].shape, jnp.float32)
-    for k in range(heads):
-        pairs = []
-        for i in range(size):
-            for h in range(cores):
-                target = heads * h + ((i % heads) ^ k)
-                pairs.append((i * cores + h, target * cores + i // heads))
-        share = lax.ppermute(shares[k], ("ctx", "head"), pairs)
-        total = total + share.astype(jnp.float32)
-    return (attended, total.astype(jnp.bfloat16))
+    parts = [in_vmem(shares[0])] + [swap(shares[k], k) for k in range(1, heads)]
+    summed = add_shares(parts)
+    pairs = []
+    for i in range(size):
+        for h in range(cores):
+            pairs.append((i * cores + h, (heads * h + i % heads) * cores + i // heads))
+    projected = in_hbm(lax.ppermute(summed, ("ctx", "head"), pairs))
+    return (join_heads(shard_index, returned), projected)
 
 
 def shifted_2(x, axis, by):
@@ -578,7 +653,8 @@
         length = args[0].shape[0] // size // mesh.shape["groups"]
         power = size & (size - 1) == 0 and heads & (heads - 1) == 0
         whole_tiles = length == VTILE and args[5].shape[1] <= HEAD_SIZE
-        return power and whole_tiles and cores == 2 and size == heads * cores
+        pairs = cores == 2 and mesh.shape["groups"] == 2 and args[7].shape[0] // size % 256 == 0
+        return power and whole_tiles and pairs and size == heads * cores
 
     def sharded(body):
         return jax.shard_map(

time: 65.3 us -> 60.5 us (0.926)
  local copies, waits for them, and re-layouts: 7.55 us -> 0.61 us
  waiting for transfers between devices: 7.02 us -> 11.5 us
  Pallas kernels: 10.4 us -> 9.27 us
    ppermute x15 -> x19, waiting for transfers between devices: 2.16 us -> 10.8 us  [move(): return in_vmem(lax.ppermute(x, axis, pairs))]
    unnamed x32 -> x1, local copies, waits for them, and re-layouts: 7.55 us -> 0.61 us
    ppermute x4 -> x1, waiting for transfers between devices: 4.86 us -> 0.72 us  [local_blocks(): projected = in_hbm(lax.ppermute(summed, ('ctx', 'head'), pairs))]
    ppermute x4 -> x1, starting transfers between devices: 9.94 us -> 6.37 us  [local_blocks(): projected = in_hbm(lax.ppermute(summed, ('ctx', 'head'), pairs))]
    ppermute x15 -> x19, starting transfers between devices: 28.6 us -> 31.6 us  [move(): return in_vmem(lax.ppermute(x, axis, pairs))]
    pallas_call x3 -> x4, Pallas kernels: 4.01 us -> 3.25 us  [the longest x1 1.21 us: mask_tiles(): pl.pallas_call(body, out_shape=[pltpu.VMEM((heads, length, size * length)...]
  transfers between devices with their start and end apart: 19 -> 20, of which waited for: 4 -> 7; matrix products, arithmetic and copies ran while one was open for 0% -> 0% of each run, Pallas kernels for 13% -> 12%
where the time goes in v5:
time: 60.5 us; the launch traced here: 60.2 us
  starting transfers between devices  38 us (63%)
  waiting for transfers between devices  11.5 us (19%)
  Pallas kernels  9.27 us (15%)
  between operations  0.8 us (1%)
  local copies, waits for them, and re-layouts  0.61 us (1%)
    ppermute x19, starting transfers between devices, move(): return in_vmem(lax.ppermute(x, axis, pairs))  31.6 us
    ppermute x19, waiting for transfers between devices, move(): return in_vmem(lax.ppermute(x, axis, pairs))  10.8 us
    ppermute x1, starting transfers between devices, local_blocks(): projected = in_hbm(lax.ppermute(summed, ('ctx', 'head'), pairs))  6.37 us
    pallas_call x1, Pallas kernels, attention(): pl.pallas_call(body, out_shape=[pltpu.VMEM((length, width), jnp.bfloat16)...  4.05 us
    pallas_call x1, Pallas kernels, pack_heads(): pl.pallas_call(body, out_shape=[pltpu.VMEM((length + PAD_ROWS, total), jn...  1.48 us
  transfers between devices with their start and end apart: 20, of which 7 were waited for; matrix products, arithmetic and copies ran while one was open for 0% of the time, Pallas kernels for 12%

profile of v5, /device:TPU:1, one launch (start us, length us, event | category | flops | bytes accessed | tf_op | source)
XLA Modules:
  0.0 60.2 jit_solution(17732480229330792192)
XLA Ops:
  0.6 1.5 %pack_heads.1 = (bf16[136,768]{1,0:T(8,128)(2,1)S(1)}, bf16[136,768]{1,0:T(8,128)(2,1)S(1)}, bf16[136,768]{1,0:T(8,128)(2,1)S(1)}, bf16[136,768]{1,0:T(8,128)(2,...) custom-call(s32[1]{0:T(128)} %bitcast.c_ref, ...), custom_call_target="tpu_custom_call" | custom-call | tf_op jit(solution)/shard_map/pack_heads/pallas_call | solution.py:83
  2.1 5.0 %collective-permute-start.3 = (bf16[128,256]{1,0:T(8,128)(2,1)S(1)}, bf16[128,256]{1,0:T(8,128)(2,1)S(1)}, u32[]{:S(2)}, u32[]{:S(2)}) collective-permute-start(bf16[128,256]{1,0:T(8,128)(2,1)S(1)} %get-tuple-element.33), channel_id=1, source_target_pairs={{0,8},{2,10},{4,12},{6,14},{1,9},{3,11},{5,13},{7,15},{16,24},{18,... | collective-permute-start | bytes 196616 | tf_op jit(solution)/shard_map/ppermute | solution.py:388
  7.2 1.2 %pack_weight.1 = (bf16[256,512]{1,0:T(8,128)(2,1)S(1)}, bf16[256,512]{1,0:T(8,128)(2,1)S(1)}, bf16[256,512]{1,0:T(8,128)(2,1)S(1)}, bf16[128,512]{1,0:T(8,128)(2,1)S(1)}) custom-call(s32[1]{0:T(128)} %bitcast.c_ref, s32[1]{0:T(128)} %bitcast.4.g_ref, bf16[256,2048]{1,0:T(8,128)(2,1)} %w_ref.1), custom_call_target="tpu_custom_call" | custom-call | tf_op jit(solution)/shard_map/pack_weight/pallas_call | solution.py:114
  8.4 2.3 %collective-permute-start.13 = (bf16[128,512]{1,0:T(8,128)(2,1)S(1)}, bf16[128,512]{1,0:T(8,128)(2,1)S(1)}, u32[]{:S(2)}, u32[]{:S(2)}) collective-permute-start(bf16[128,512]{1,0:T(8,128)(2,1)S(1)} %get-tuple-element.45), channel_id=1, source_target_pairs={{0,6},{2,4},{4,2},{6,0},{8,14},{10,12},{12,10},{14,8},{1,7},{3,5},... | collective-permute-start | bytes 393224 | tf_op jit(solution)/shard_map/ppermute | solution.py:388
  10.7 1.3 %collective-permute-start.4 = (bf16[128,256]{1,0:T(8,128)(2,1)S(1)}, bf16[128,256]{1,0:T(8,128)(2,1)S(1)}, u32[]{:S(2)}, u32[]{:S(2)}) collective-permute-start(bf16[128,256]{1,0:T(8,128)(2,1)S(1)} %get-tuple-element.34), channel_id=1, source_target_pairs={{0,10},{2,8},{4,14},{6,12},{1,11},{3,9},{5,15},{7,13},{16,26},{18,... | collective-permute-start | bytes 196616 | tf_op jit(solution)/shard_map/ppermute | solution.py:388
  11.9 1.3 %collective-permute-start.5 = (bf16[128,256]{1,0:T(8,128)(2,1)S(1)}, bf16[128,256]{1,0:T(8,128)(2,1)S(1)}, u32[]{:S(2)}, u32[]{:S(2)}) collective-permute-start(bf16[128,256]{1,0:T(8,128)(2,1)S(1)} %get-tuple-element.35), channel_id=1, source_target_pairs={{0,12},{2,14},{4,8},{6,10},{1,13},{3,15},{5,9},{7,11},{16,28},{18,... | collective-permute-start | bytes 196616 | tf_op jit(solution)/shard_map/ppermute | solution.py:388
  13.3 1.2 %collective-permute-start = (bf16[136,768]{1,0:T(8,128)(2,1)S(1)}, bf16[136,768]{1,0:T(8,128)(2,1)S(1)}, u32[]{:S(2)}, u32[]{:S(2)}) collective-permute-start(bf16[136,768]{1,0:T(8,128)(2,1)S(1)} %get-tuple-element.30), channel_id=1, source_target_pairs={{0,2},{2,0},{4,6},{6,4},{8,10},{10,8},{12,14},{14,12},{1,3},{3,1},... | collective-permute-start | bytes 626696 | tf_op jit(solution)/shard_map/ppermute | solution.py:388
  14.5 0.0 collective-permute-done.3.rest_4_
  14.5 2.4 %collective-permute-start.6 = (bf16[128,256]{1,0:T(8,128)(2,1)S(1)}, bf16[128,256]{1,0:T(8,128)(2,1)S(1)}, u32[]{:S(2)}, u32[]{:S(2)}) collective-permute-start(bf16[128,256]{1,0:T(8,128)(2,1)S(1)} %get-tuple-element.36), channel_id=1, source_target_pairs={{0,14},{2,12},{4,10},{6,8},{1,15},{3,13},{5,11},{7,9},{16,30},{18,... | collective-permute-start | bytes 196616 | tf_op jit(solution)/shard_map/ppermute | solution.py:388
  16.9 0.0 collective-permute-done.4.rest_5_
  16.9 0.1 collective-permute-start.1
  16.9 0.0 collective-permute-done.5.rest_6_
  17.0 1.7 %collective-permute-start.2 = (bf16[136,768]{1,0:T(8,128)(2,1)S(1)}, bf16[136,768]{1,0:T(8,128)(2,1)S(1)}, u32[]{:S(2)}, u32[]{:S(2)}) collective-permute-start(bf16[136,768]{1,0:T(8,128)(2,1)S(1)} %get-tuple-element.32), channel_id=1, source_target_pairs={{0,6},{2,4},{4,2},{6,0},{8,14},{10,12},{12,10},{14,8},{1,7},{3,5},... | collective-permute-start | bytes 626696 | tf_op jit(solution)/shard_map/ppermute | solution.py:388
  18.7 0.0 collective-permute-done.6.rest_7_
  18.7 0.9 %collective-permute-start.11 = (bf16[256,512]{1,0:T(8,128)(2,1)S(1)}, bf16[256,512]{1,0:T(8,128)(2,1)S(1)}, u32[]{:S(2)}, u32[]{:S(2)}) collective-permute-start(bf16[256,512]{1,0:T(8,128)(2,1)S(1)} %get-tuple-element.43), channel_id=1, source_target_pairs={{0,2},{2,0},{4,6},{6,4},{8,10},{10,8},{12,14},{14,12},{1,3},{3,1},... | collective-permute-start | bytes 786440 | tf_op jit(solution)/shard_map/ppermute | solution.py:388
  19.6 0.0 collective-permute-done.13.rest_3_
  19.6 2.1 %collective-permute-start.12 = (bf16[256,512]{1,0:T(8,128)(2,1)S(1)}, bf16[256,512]{1,0:T(8,128)(2,1)S(1)}, u32[]{:S(2)}, u32[]{:S(2)}) collective-permute-start(bf16[256,512]{1,0:T(8,128)(2,1)S(1)} %get-tuple-element.44), channel_id=1, source_target_pairs={{0,4},{2,6},{4,0},{6,2},{8,12},{10,14},{12,8},{14,10},{1,5},{3,7},... | collective-permute-start | bytes 786440 | tf_op jit(solution)/shard_map/ppermute | solution.py:388
  21.7 0.0 collective-permute-done.rest_1_
  21.7 1.2 %collective-permute-start.14 = (bf16[128,512]{1,0:T(8,128)(2,1)S(1)}, bf16[128,512]{1,0:T(8,128)(2,1)S(1)}, u32[]{:S(2)}, u32[]{:S(2)}) collective-permute-start(bf16[128,512]{1,0:T(8,128)(2,1)S(1)} %collective-permute-done.13.rest_3_), channel_id=1, source_target_pairs={{0,16},{16,0},{1,17},{17,1},{2,18},{18,2},{3,19},{19,3},{4,20},{20... | collective-permute-start | bytes 393224 | tf_op jit(solution)/shard_map/ppermute | solution.py:388
  23.0 1.2 %mask_tiles.1 = (f32[4,128,1024]{2,1,0:T(8,128)S(1)}, s32[4,8,128]{2,1,0:T(8,128)S(1)}) custom-call(s32[1]{0:T(128)} %bitcast.c_ref, s32[2,4]{1,0:T(2,128)} %bitcast.5, s32[2,4]{1,0:T(2,128)} %bitcast.6, s32[8]{0:T(128)} %count_ref.1), custom_call_target="tpu_custom_call" | custom-call | tf_op jit(solution)/shard_map/mask_tiles/pallas_call | solution.py:163
  24.2 0.0 collective-permute-done.1.rest_2_
  24.2 2.5 %collective-permute-done.2.rest_3_ = bf16[136,768]{1,0:T(8,128)(2,1)S(1)} collective-permute-done((bf16[136,768]{1,0:T(8,128)(2,1)S(1)}, bf16[136,768]{1,0:T(8,128)(2,1)S(1)}, u32[]{:S(2)}, u32[]{:S(2)}) %collective-permute-start.2) | collective-permute-done | bytes 208928 | tf_op jit(solution)/shard_map/ppermute | solution.py:388
  26.8 4.0 %attention.1 = (bf16[128,512]{1,0:T(8,128)(2,1)S(1)}, bf16[128,512]{1,0:T(8,128)(2,1)S(1)}, bf16[128,512]{1,0:T(8,128)(2,1)S(1)}, bf16[128,512]{1,0:T(8,128)(2,1)S(1)}, bf16[64,512]{1,0:T(8,128)(2,1)S(1)}) custom-call(s32[1]{0:T(128)} %bitcast.c_ref, f32[4,128,1024]{2,1,0:T(8,128)S(1)} %get-tuple-element.27.mask_ref, ...), custom_call_target="tpu_custom_call" | custom-call | tf_op jit(solution)/shard_map/attention/pallas_call | solution.py:252
  30.8 0.6 %collective-permute-start.10 = (bf16[64,512]{1,0:T(8,128)(2,1)S(1)}, bf16[64,512]{1,0:T(8,128)(2,1)S(1)}, u32[]{:S(2)}, u32[]{:S(2)}) collective-permute-start(bf16[64,512]{1,0:T(8,128)(2,1)S(1)} %get-tuple-element.41.own_ref), channel_id=1, source_target_pairs={{0,8},{2,10},{4,12},{6,14},{8,0},{10,2},{12,4},{14,6},{1,9},{3,11}... | collective-permute-start | bytes 196616 | tf_op jit(solution)/shard_map/ppermute | solution.py:388
  31.4 0.0 collective-permute-done.14.rest_4_
  31.4 0.0 collective-permute-done.11.rest_1_
  31.4 1.2 %collective-permute-done.12.rest_2_ = bf16[256,512]{1,0:T(8,128)(2,1)S(1)} collective-permute-done((bf16[256,512]{1,0:T(8,128)(2,1)S(1)}, bf16[256,512]{1,0:T(8,128)(2,1)S(1)}, u32[]{:S(2)}, u32[]{:S(2)}) %collective-permute-start.12) | collective-permute-done | bytes 262176 | tf_op jit(solution)/shard_map/ppermute | solution.py:388
  32.6 2.7 %collective-permute-done.10.other_ref = bf16[64,512]{1,0:T(8,128)(2,1)S(1)} collective-permute-done((bf16[64,512]{1,0:T(8,128)(2,1)S(1)}, bf16[64,512]{1,0:T(8,128)(2,1)S(1)}, u32[]{:S(2)}, u32[]{:S(2)}) %collective-permute-start.10) | collective-permute-done | bytes 65568 | tf_op jit(solution)/shard_map/ppermute | solution.py:388
  35.3 0.4 project.1
  35.7 4.9 %collective-permute-start.15 = (f32[64,1024]{1,0:T(8,128)S(1)}, f32[64,1024]{1,0:T(8,128)S(1)}, u32[]{:S(2)}, u32[]{:S(2)}) collective-permute-start(f32[64,1024]{1,0:T(8,128)S(1)} %get-tuple-element.47), channel_id=1, source_target_pairs={{0,1},{1,0},{2,3},{3,2},{4,5},{5,4},{6,7},{7,6},{8,9},{9,8},{10,11... | collective-permute-start | bytes 786440 | tf_op jit(solution)/shard_map/ppermute | solution.py:388
  40.6 2.3 %collective-permute-start.7 = (bf16[128,512]{1,0:T(8,128)(2,1)S(1)}, bf16[128,512]{1,0:T(8,128)(2,1)S(1)}, u32[]{:S(2)}, u32[]{:S(2)}) collective-permute-start(bf16[128,512]{1,0:T(8,128)(2,1)S(1)} %get-tuple-element.38), channel_id=1, source_target_pairs={{0,2},{2,0},{4,6},{6,4},{8,10},{10,8},{12,14},{14,12},{1,3},{3,1},... | collective-permute-start | bytes 393224 | tf_op jit(solution)/shard_map/ppermute | solution.py:388
  43.0 0.2 collective-permute-start.8
  43.1 1.0 %collective-permute-start.9 = (bf16[128,512]{1,0:T(8,128)(2,1)S(1)}, bf16[128,512]{1,0:T(8,128)(2,1)S(1)}, u32[]{:S(2)}, u32[]{:S(2)}) collective-permute-start(bf16[128,512]{1,0:T(8,128)(2,1)S(1)} %get-tuple-element.40), channel_id=1, source_target_pairs={{0,6},{2,4},{4,2},{6,0},{8,14},{10,12},{12,10},{14,8},{1,7},{3,5},... | collective-permute-start | bytes 393224 | tf_op jit(solution)/shard_map/ppermute | solution.py:388
  44.1 0.0 collective-permute-done.15.b_ref
  44.2 1.5 %collective-permute-start.16 = (bf16[16,1024]{1,0:T(8,128)(2,1)S(1)}, bf16[16,1024]{1,0:T(8,128)(2,1)S(1)}, u32[]{:S(2)}, u32[]{:S(2)}) collective-permute-start(bf16[16,1024]{1,0:T(8,128)(2,1)S(1)} %get-tuple-element.49), channel_id=1, source_target_pairs={{0,2},{2,0},{4,6},{6,4},{8,10},{10,8},{12,14},{14,12},{1,3},{3,1},... | collective-permute-start | bytes 98312 | tf_op jit(solution)/shard_map/ppermute | solution.py:388
  45.7 0.2 collective-permute-start.17
  45.9 1.5 %collective-permute-done.16.rest_1_ = bf16[16,1024]{1,0:T(8,128)(2,1)S(1)} collective-permute-done((bf16[16,1024]{1,0:T(8,128)(2,1)S(1)}, bf16[16,1024]{1,0:T(8,128)(2,1)S(1)}, u32[]{:S(2)}, u32[]{:S(2)}) %collective-permute-start.16) | collective-permute-done | bytes 32800 | tf_op jit(solution)/shard_map/ppermute | solution.py:388
  47.4 1.3 %collective-permute-start.18 = (bf16[16,1024]{1,0:T(8,128)(2,1)S(1)}, bf16[16,1024]{1,0:T(8,128)(2,1)S(1)}, u32[]{:S(2)}, u32[]{:S(2)}) collective-permute-start(bf16[16,1024]{1,0:T(8,128)(2,1)S(1)} %get-tuple-element.51), channel_id=1, source_target_pairs={{0,6},{2,4},{4,2},{6,0},{8,14},{10,12},{12,10},{14,8},{1,7},{3,5},... | collective-permute-start | bytes 98312 | tf_op jit(solution)/shard_map/ppermute | solution.py:388
  48.7 2.5 %collective-permute-done.17.rest_2_ = bf16[16,1024]{1,0:T(8,128)(2,1)S(1)} collective-permute-done((bf16[16,1024]{1,0:T(8,128)(2,1)S(1)}, bf16[16,1024]{1,0:T(8,128)(2,1)S(1)}, u32[]{:S(2)}, u32[]{:S(2)}) %collective-permute-start.17) | collective-permute-done | bytes 32800 | tf_op jit(solution)/shard_map/ppermute | solution.py:388
  51.2 0.4 collective-permute-done.18.rest_3_
  51.6 6.4 %collective-permute-start.19 = (bf16[16,1024]{1,0:T(8,128)(2,1)S(1)}, bf16[16,1024]{1,0:T(8,128)(2,1)S(1)}, u32[]{:S(2)}, u32[]{:S(2)}) collective-permute-start(bf16[16,1024]{1,0:T(8,128)(2,1)S(1)} %add_shares.1), channel_id=1, source_target_pairs={{0,0},{1,8},{2,2},{3,10},{4,4},{5,12},{6,6},{7,14},{8,1},{9,9},{10... | collective-permute-start | bytes 98312 | tf_op jit(solution)/shard_map/ppermute | solution.py:418
  58.0 0.0 collective-permute-done.7.rest_1_
  58.0 0.0 collective-permute-done.8.rest_2_
  58.0 0.0 collective-permute-done.9.rest_3_
  58.0 0.8 %join_heads.1 = bf16[128,2048]{1,0:T(8,128)(2,1)} custom-call(s32[1]{0:T(128)} %bitcast.c_ref, bf16[128,512]{1,0:T(8,128)(2,1)S(1)} %get-tuple-element.37.rest_0_, bf16[128,512]{1,0:T(8,128)(2,1)S(1)} %collective-permute-done.7.rest_1_, bf16[128,512]{1,0:T(8,128)(2,1)S(1)} %collective-permute-done.8.rest_2_, bf16[128,512]{1,0:T(8,128)(2,1)S(1)} %collective-permute-done.9.rest_3_), custom_call_target="tpu_custom_call" | custom-call | tf_op jit(solution)/shard_map/join_heads/pallas_call | solution.py:357
  58.9 0.7 %collective-permute-done.19 = bf16[16,1024]{1,0:T(8,128)(2,1)S(1)} collective-permute-done((bf16[16,1024]{1,0:T(8,128)(2,1)S(1)}, bf16[16,1024]{1,0:T(8,128)(2,1)S(1)}, u32[]{:S(2)}, u32[]{:S(2)}) %collective-permute-start.19) | collective-permute-done | bytes 32800 | tf_op jit(solution)/shard_map/ppermute | solution.py:418
  59.6 0.6 %copy.11 = bf16[16,1024]{1,0:T(8,128)(2,1)} copy(bf16[16,1024]{1,0:T(8,128)(2,1)S(1)} %collective-permute-done.19) | data formatting | bytes 65536
  (2 shorter events, 0.1 us)
Async XLA Ops:
  2.1 12.4 %collective-permute-start.3 = (bf16[128,256]{1,0:T(8,128)(2,1)S(1)}, bf16[128,256]{1,0:T(8,128)(2,1)S(1)}, u32[]{:S(2)}, u32[]{:S(2)}) collective-permute-start(bf16[128,256]{1,0:T(8,128)(2,1)S(1)} %get-tuple-element.33), channel_id=1, source_target_pairs={{0,8},{2,10},{4,12},{6,14},{1,9},{3,11},{5,13},{7,15},{16,24},{18,... | collective-permute-start | bytes 196616 | tf_op jit(solution)/shard_map/ppermute | solution.py:388
  8.4 11.2 %collective-permute-start.13 = (bf16[128,512]{1,0:T(8,128)(2,1)S(1)}, bf16[128,512]{1,0:T(8,128)(2,1)S(1)}, u32[]{:S(2)}, u32[]{:S(2)}) collective-permute-start(bf16[128,512]{1,0:T(8,128)(2,1)S(1)} %get-tuple-element.45), channel_id=1, source_target_pairs={{0,6},{2,4},{4,2},{6,0},{8,14},{10,12},{12,10},{14,8},{1,7},{3,5},... | collective-permute-start | bytes 393224 | tf_op jit(solution)/shard_map/ppermute | solution.py:388
  10.7 6.2 %collective-permute-start.4 = (bf16[128,256]{1,0:T(8,128)(2,1)S(1)}, bf16[128,256]{1,0:T(8,128)(2,1)S(1)}, u32[]{:S(2)}, u32[]{:S(2)}) collective-permute-start(bf16[128,256]{1,0:T(8,128)(2,1)S(1)} %get-tuple-element.34), channel_id=1, source_target_pairs={{0,10},{2,8},{4,14},{6,12},{1,11},{3,9},{5,15},{7,13},{16,26},{18,... | collective-permute-start | bytes 196616 | tf_op jit(solution)/shard_map/ppermute | solution.py:388
  11.9 5.0 %collective-permute-start.5 = (bf16[128,256]{1,0:T(8,128)(2,1)S(1)}, bf16[128,256]{1,0:T(8,128)(2,1)S(1)}, u32[]{:S(2)}, u32[]{:S(2)}) collective-permute-start(bf16[128,256]{1,0:T(8,128)(2,1)S(1)} %get-tuple-element.35), channel_id=1, source_target_pairs={{0,12},{2,14},{4,8},{6,10},{1,13},{3,15},{5,9},{7,11},{16,28},{18,... | collective-permute-start | bytes 196616 | tf_op jit(solution)/shard_map/ppermute | solution.py:388
  13.3 8.5 %collective-permute-start = (bf16[136,768]{1,0:T(8,128)(2,1)S(1)}, bf16[136,768]{1,0:T(8,128)(2,1)S(1)}, u32[]{:S(2)}, u32[]{:S(2)}) collective-permute-start(bf16[136,768]{1,0:T(8,128)(2,1)S(1)} %get-tuple-element.30), channel_id=1, source_target_pairs={{0,2},{2,0},{4,6},{6,4},{8,10},{10,8},{12,14},{14,12},{1,3},{3,1},... | collective-permute-start | bytes 626696 | tf_op jit(solution)/shard_map/ppermute | solution.py:388
  14.5 4.2 %collective-permute-start.6 = (bf16[128,256]{1,0:T(8,128)(2,1)S(1)}, bf16[128,256]{1,0:T(8,128)(2,1)S(1)}, u32[]{:S(2)}, u32[]{:S(2)}) collective-permute-start(bf16[128,256]{1,0:T(8,128)(2,1)S(1)} %get-tuple-element.36), channel_id=1, source_target_pairs={{0,14},{2,12},{4,10},{6,8},{1,15},{3,13},{5,11},{7,9},{16,30},{18,... | collective-permute-start | bytes 196616 | tf_op jit(solution)/shard_map/ppermute | solution.py:388
  16.9 7.3 %collective-permute-start.1 = (bf16[136,768]{1,0:T(8,128)(2,1)S(1)}, bf16[136,768]{1,0:T(8,128)(2,1)S(1)}, u32[]{:S(2)}, u32[]{:S(2)}) collective-permute-start(bf16[136,768]{1,0:T(8,128)(2,1)S(1)} %get-tuple-element.31), channel_id=1, source_target_pairs={{0,4},{2,6},{4,0},{6,2},{8,12},{10,14},{12,8},{14,10},{1,5},{3,7},... | collective-permute-start | bytes 626696 | tf_op jit(solution)/shard_map/ppermute | solution.py:388
  17.0 9.8 %collective-permute-start.2 = (bf16[136,768]{1,0:T(8,128)(2,1)S(1)}, bf16[136,768]{1,0:T(8,128)(2,1)S(1)}, u32[]{:S(2)}, u32[]{:S(2)}) collective-permute-start(bf16[136,768]{1,0:T(8,128)(2,1)S(1)} %get-tuple-element.32), channel_id=1, source_target_pairs={{0,6},{2,4},{4,2},{6,0},{8,14},{10,12},{12,10},{14,8},{1,7},{3,5},... | collective-permute-start | bytes 626696 | tf_op jit(solution)/shard_map/ppermute | solution.py:388
  18.7 12.8 %collective-permute-start.11 = (bf16[256,512]{1,0:T(8,128)(2,1)S(1)}, bf16[256,512]{1,0:T(8,128)(2,1)S(1)}, u32[]{:S(2)}, u32[]{:S(2)}) collective-permute-start(bf16[256,512]{1,0:T(8,128)(2,1)S(1)} %get-tuple-element.43), channel_id=1, source_target_pairs={{0,2},{2,0},{4,6},{6,4},{8,10},{10,8},{12,14},{14,12},{1,3},{3,1},... | collective-permute-start | bytes 786440 | tf_op jit(solution)/shard_map/ppermute | solution.py:388
  19.6 13.0 %collective-permute-start.12 = (bf16[256,512]{1,0:T(8,128)(2,1)S(1)}, bf16[256,512]{1,0:T(8,128)(2,1)S(1)}, u32[]{:S(2)}, u32[]{:S(2)}) collective-permute-start(bf16[256,512]{1,0:T(8,128)(2,1)S(1)} %get-tuple-element.44), channel_id=1, source_target_pairs={{0,4},{2,6},{4,0},{6,2},{8,12},{10,14},{12,8},{14,10},{1,5},{3,7},... | collective-permute-start | bytes 786440 | tf_op jit(solution)/shard_map/ppermute | solution.py:388
  21.7 9.7 %collective-permute-start.14 = (bf16[128,512]{1,0:T(8,128)(2,1)S(1)}, bf16[128,512]{1,0:T(8,128)(2,1)S(1)}, u32[]{:S(2)}, u32[]{:S(2)}) collective-permute-start(bf16[128,512]{1,0:T(8,128)(2,1)S(1)} %collective-permute-done.13.rest_3_), channel_id=1, source_target_pairs={{0,16},{16,0},{1,17},{17,1},{2,18},{18,2},{3,19},{19,3},{4,20},{20... | collective-permute-start | bytes 393224 | tf_op jit(solution)/shard_map/ppermute | solution.py:388
  30.8 4.5 %collective-permute-start.10 = (bf16[64,512]{1,0:T(8,128)(2,1)S(1)}, bf16[64,512]{1,0:T(8,128)(2,1)S(1)}, u32[]{:S(2)}, u32[]{:S(2)}) collective-permute-start(bf16[64,512]{1,0:T(8,128)(2,1)S(1)} %get-tuple-element.41.own_ref), channel_id=1, source_target_pairs={{0,8},{2,10},{4,12},{6,14},{8,0},{10,2},{12,4},{14,6},{1,9},{3,11}... | collective-permute-start | bytes 196616 | tf_op jit(solution)/shard_map/ppermute | solution.py:388
  35.7 8.4 %collective-permute-start.15 = (f32[64,1024]{1,0:T(8,128)S(1)}, f32[64,1024]{1,0:T(8,128)S(1)}, u32[]{:S(2)}, u32[]{:S(2)}) collective-permute-start(f32[64,1024]{1,0:T(8,128)S(1)} %get-tuple-element.47), channel_id=1, source_target_pairs={{0,1},{1,0},{2,3},{3,2},{4,5},{5,4},{6,7},{7,6},{8,9},{9,8},{10,11... | collective-permute-start | bytes 786440 | tf_op jit(solution)/shard_map/ppermute | solution.py:388
  40.6 17.4 %collective-permute-start.7 = (bf16[128,512]{1,0:T(8,128)(2,1)S(1)}, bf16[128,512]{1,0:T(8,128)(2,1)S(1)}, u32[]{:S(2)}, u32[]{:S(2)}) collective-permute-start(bf16[128,512]{1,0:T(8,128)(2,1)S(1)} %get-tuple-element.38), channel_id=1, source_target_pairs={{0,2},{2,0},{4,6},{6,4},{8,10},{10,8},{12,14},{14,12},{1,3},{3,1},... | collective-permute-start | bytes 393224 | tf_op jit(solution)/shard_map/ppermute | solution.py:388
  43.0 15.1 %collective-permute-start.8 = (bf16[128,512]{1,0:T(8,128)(2,1)S(1)}, bf16[128,512]{1,0:T(8,128)(2,1)S(1)}, u32[]{:S(2)}, u32[]{:S(2)}) collective-permute-start(bf16[128,512]{1,0:T(8,128)(2,1)S(1)} %get-tuple-element.39), channel_id=1, source_target_pairs={{0,4},{2,6},{4,0},{6,2},{8,12},{10,14},{12,8},{14,10},{1,5},{3,7},... | collective-permute-start | bytes 393224 | tf_op jit(solution)/shard_map/ppermute | solution.py:388
  43.1 14.9 %collective-permute-start.9 = (bf16[128,512]{1,0:T(8,128)(2,1)S(1)}, bf16[128,512]{1,0:T(8,128)(2,1)S(1)}, u32[]{:S(2)}, u32[]{:S(2)}) collective-permute-start(bf16[128,512]{1,0:T(8,128)(2,1)S(1)} %get-tuple-element.40), channel_id=1, source_target_pairs={{0,6},{2,4},{4,2},{6,0},{8,14},{10,12},{12,10},{14,8},{1,7},{3,5},... | collective-permute-start | bytes 393224 | tf_op jit(solution)/shard_map/ppermute | solution.py:388
  44.2 3.2 %collective-permute-start.16 = (bf16[16,1024]{1,0:T(8,128)(2,1)S(1)}, bf16[16,1024]{1,0:T(8,128)(2,1)S(1)}, u32[]{:S(2)}, u32[]{:S(2)}) collective-permute-start(bf16[16,1024]{1,0:T(8,128)(2,1)S(1)} %get-tuple-element.49), channel_id=1, source_target_pairs={{0,2},{2,0},{4,6},{6,4},{8,10},{10,8},{12,14},{14,12},{1,3},{3,1},... | collective-permute-start | bytes 98312 | tf_op jit(solution)/shard_map/ppermute | solution.py:388
  45.7 5.4 %collective-permute-start.17 = (bf16[16,1024]{1,0:T(8,128)(2,1)S(1)}, bf16[16,1024]{1,0:T(8,128)(2,1)S(1)}, u32[]{:S(2)}, u32[]{:S(2)}) collective-permute-start(bf16[16,1024]{1,0:T(8,128)(2,1)S(1)} %get-tuple-element.50), channel_id=1, source_target_pairs={{0,4},{2,6},{4,0},{6,2},{8,12},{10,14},{12,8},{14,10},{1,5},{3,7},... | collective-permute-start | bytes 98312 | tf_op jit(solution)/shard_map/ppermute | solution.py:388
  47.4 4.2 %collective-permute-start.18 = (bf16[16,1024]{1,0:T(8,128)(2,1)S(1)}, bf16[16,1024]{1,0:T(8,128)(2,1)S(1)}, u32[]{:S(2)}, u32[]{:S(2)}) collective-permute-start(bf16[16,1024]{1,0:T(8,128)(2,1)S(1)} %get-tuple-element.51), channel_id=1, source_target_pairs={{0,6},{2,4},{4,2},{6,0},{8,14},{10,12},{12,10},{14,8},{1,7},{3,5},... | collective-permute-start | bytes 98312 | tf_op jit(solution)/shard_map/ppermute | solution.py:388
  51.6 8.0 %collective-permute-start.19 = (bf16[16,1024]{1,0:T(8,128)(2,1)S(1)}, bf16[16,1024]{1,0:T(8,128)(2,1)S(1)}, u32[]{:S(2)}, u32[]{:S(2)}) collective-permute-start(bf16[16,1024]{1,0:T(8,128)(2,1)S(1)} %add_shares.1), channel_id=1, source_target_pairs={{0,0},{1,8},{2,2},{3,10},{4,4},{5,12},{6,6},{7,14},{8,1},{9,9},{10... | collective-permute-start | bytes 98312 | tf_op jit(solution)/shard_map/ppermute | solution.py:418

commit v6 on v5

--- a/solution.py
+++ b/solution.py
@@ -95,42 +95,25 @@
     )(shard_index, in_hbm(query), in_hbm(key), in_hbm(value), in_hbm(kept_rows))
 
 
-def pack_weight(shard_index, group_index, weight, heads):
+def pack_weight(shard_index, group_index, slash, tiles, counts, weight, length):
+    heads = slash.shape[1]
+    size = counts.shape[0]
+    lanes = HEAD_SIZE
     width = weight.shape[1] // heads
     outs = weight.shape[0]
-    counts = [outs] * (heads - 1) + [outs // 2]
-
-    def body(c_ref, g_ref, w_ref, *rest):
-        out, sems = rest[:heads], rest[heads]
-        slot = c_ref[0] % heads
+    sent = [outs] * (heads - 1) + [outs // 2]
+
+    def body(c_ref, g_ref, slash_ref, tile_ref, count_ref, w_ref, *rest):
+        out, (mask_ref, table_ref, tile_buf, sems) = rest[:heads], rest[heads:]
+        c = c_ref[0]
+        slot = c % heads
+        first = c - slot
         copies = []
         for j in range(heads):
             at = pl.multiple_of((slot ^ j) * width, HEAD_SIZE)
-            first = pl.multiple_of(g_ref[0] * counts[j], counts[j]) if counts[j] < outs else 0
-            copies.append((w_ref.at[pl.ds(first, counts[j]), pl.ds(at, width)], out[j]))
-        for copy in start_all(copies, sems):
-            copy.wait()
-
-    return pl.pallas_call(
-        body,
-        out_shape=[pltpu.VMEM((count, width), jnp.bfloat16) for count in counts],
-        in_specs=[SMEM, SMEM, ANY],
-        out_specs=[VMEM] * heads,
-        scratch_shapes=[pltpu.SemaphoreType.DMA((heads,))],
-        compiler_params=GRANT,
-        name="pack_weight",
-    )(shard_index, group_index, in_hbm(weight))
-
-
-def mask_tiles(shard_index, slash, tiles, counts, length):
-    heads = slash.shape[1]
-    size = counts.shape[0]
-    lanes = HEAD_SIZE
-
-    def body(c_ref, slash_ref, tile_ref, count_ref, out_ref, table_ref, tile_buf):
-        c = c_ref[0]
-        slot = c % heads
-        first = c - slot
+            row = pl.multiple_of(g_ref[0] * sent[j], sent[j]) if sent[j] < outs else 0
+            copies.append((w_ref.at[pl.ds(row, sent[j]), pl.ds(at, width)], out[j]))
+        started = start_all(copies, sems)
         difference = lax.broadcasted_iota(jnp.int32, (length, length), 0) - lax.broadcasted_iota(
             jnp.int32, (length, length), 1
         )
@@ -154,24 +137,30 @@
                     vertical = size + jnp.where(back == 0, 0, 1)
                     entry = jnp.where(tile_ref[i, slot] == k_shard, vertical, entry)
                 entry = jnp.where(back < 0, size + 2, entry)
-                out_ref[s, :, number * length : (number + 1) * length] = tile_buf[entry]
+                mask_ref[s, :, number * length : (number + 1) * length] = tile_buf[entry]
             count = count_ref[first + s]
             table_ref[s, 0:1, :] = jnp.full((1, lanes), count, jnp.int32)
             table_ref[s, 1:2, :] = jnp.full((1, lanes), before, jnp.int32)
             before = before + count
+        for copy in started:
+            copy.wait()
 
     return pl.pallas_call(
         body,
-        out_shape=[
+        out_shape=[pltpu.VMEM((count, width), jnp.bfloat16) for count in sent]
+        + [
             pltpu.VMEM((heads, length, size * length), jnp.float32),
             pltpu.VMEM((heads, 8, lanes), jnp.int32),
         ],
-        in_specs=[SMEM] * 4,
-        out_specs=[VMEM] * 2,
-        scratch_shapes=[pltpu.VMEM((size + 3, length, length), jnp.float32)],
+        in_specs=[SMEM] * 5 + [ANY],
+        out_specs=[VMEM] * (heads + 2),
+        scratch_shapes=[
+            pltpu.VMEM((size + 3, length, length), jnp.float32),
+            pltpu.SemaphoreType.DMA((heads,)),
+        ],
         compiler_params=GRANT,
-        name="mask_tiles",
-    )(shard_index, in_hbm(slash), in_hbm(tiles), in_hbm(counts))
+        name="pack_weight",
+    )(shard_index, group_index, in_hbm(slash), in_hbm(tiles), in_hbm(counts), in_hbm(weight))
 
 
 def attention(shard_index, masks, table, near, far, keep_rows):
@@ -208,26 +197,36 @@
             kept_at = pl.ds(pl.multiple_of(to * PAD_ROWS, PAD_ROWS), PAD_ROWS)
             kept_all[kept_at, :] = near_refs[k][length:, 0:hd].astype(jnp.float32)
         rows = jnp.zeros((block_rows, width), jnp.float32)
-        for s in range(heads):
-            seen = far_keys + (s + 1) * length
-            rows_at = s * group * length
-            scores = lax.dot_general(
-                q_all[rows_at : rows_at + group * length, :],
-                k_all[0:seen, :],
+
+        def scores_of(step):
+            s, part = step
+            rows_at = (s * group + part * 2) * length
+            return lax.dot_general(
+                q_all[rows_at : rows_at + 2 * length, :],
+                k_all[0 : far_keys + (s + 1) * length, :],
                 (((1,), (1,)), ((), ())),
                 preferred_element_type=jnp.float32,
             )
-            scores = scores.reshape(group, length, seen) * factor + mask_ref[s, :, 0:seen][None]
-            scores = scores.reshape(group * length, seen)
+
+        steps = [(s, part) for s in range(heads) for part in range(group // 2)]
+        ready = [scores_of(step) for step in steps[:1]]
+        for number, (s, part) in enumerate(steps):
+            if number + 1 < len(steps):
+                ready.append(scores_of(steps[number + 1]))
+            seen = far_keys + (s + 1) * length
+            scores = ready.pop(0).reshape(2, length, seen) * factor + mask_ref[s, :, 0:seen][None]
+            scores = scores.reshape(2 * length, seen)
             weights = jnp.exp2(scores - jnp.max(scores, axis=1, keepdims=True))
             mixed = jnp.dot(
                 weights.astype(jnp.bfloat16), v_all[0:seen, :], preferred_element_type=jnp.float32
             )
             mixed = (mixed[:, :hd] / mixed[:, hd:]).astype(jnp.bfloat16)
-            for g in range(group):
-                mixed_all[s * length : (s + 1) * length, g * hd : (g + 1) * hd] = mixed[
+            for g in range(2):
+                at = (part * 2 + g) * hd
+                mixed_all[s * length : (s + 1) * length, at : at + hd] = mixed[
                     g * length : (g + 1) * length
                 ]
+        for s in range(heads):
             kept = kept_all[s * PAD_ROWS : s * PAD_ROWS + 1, :].astype(jnp.int32)
             token = lax.broadcasted_iota(jnp.int32, (length, hd), 0)
             is_token = (token == kept).astype(jnp.float32).astype(jnp.bfloat16)
@@ -396,13 +395,18 @@
     for k in range(heads, size):
         pairs = [(i, i ^ k) for i in range(size) if i // heads < (i ^ k) // heads]
         far.append(move(packed[heads + k % heads], "ctx", pairs))
-    packed_weight = pack_weight(shard_index, group_index, out_weight, heads)
+    *packed_weight, masks, table = pack_weight(
+        shard_index,
+        group_index,
+        slash_offsets.T,
+        vertical_tiles.T,
+        kept_count,
+        out_weight,
+        query_tensor.shape[0],
+    )
     weights = [in_vmem(packed_weight[0])]
     weights += [swap(packed_weight[k], k) for k in range(1, heads)]
     weights.append(move(weights[-1], "groups", [(0, 1), (1, 0)]))
-    masks, table = mask_tiles(
-        shard_index, slash_offsets.T, vertical_tiles.T, kept_count, query_tensor.shape[0]
-    )
     *mixed, rows = attention(shard_index, in_vmem(masks), in_vmem(table), near, far, keep_rows)
     other_rows = move(rows, "ctx", xor_pairs(size, heads))
     returned = [in_vmem(mixed[0])] + [swap(mixed[k], k) for k in range(1, heads)]

time: 60.5 us -> 61.3 us (1.013)
  starting transfers between devices: 38 us -> 40.4 us
  Pallas kernels: 9.27 us -> 8.27 us
    ppermute x19, starting transfers between devices: 31.6 us -> 33.9 us  [move(): return in_vmem(lax.ppermute(x, axis, pairs))]
    pallas_call x1 -> x0, Pallas kernels: 1.21 us -> none  [mask_tiles(): pl.pallas_call(body, out_shape=[pltpu.VMEM((heads, length, size * length)...]
    pallas_call x1, Pallas kernels: 1.19 us -> 1.9 us  [pack_weight(): pl.pallas_call(body, out_shape=[pltpu.VMEM((count, width), jnp.bfloat16)...]
  transfers between devices with their start and end apart: 20 -> 20, of which waited for: 7 -> 7; matrix products, arithmetic and copies ran while one was open for 0% -> 0% of each run, Pallas kernels for 12% -> 10%
where the time goes in v6:
time: 61.3 us; the launch traced here: 61 us
  starting transfers between devices  40.4 us (66%)
  waiting for transfers between devices  11 us (18%)
  Pallas kernels  8.27 us (13%)
  between operations  0.79 us (1%)
    ppermute x19, starting transfers between devices, move(): return in_vmem(lax.ppermute(x, axis, pairs))  33.9 us
    ppermute x19, waiting for transfers between devices, move(): return in_vmem(lax.ppermute(x, axis, pairs))  10.2 us
    ppermute x1, starting transfers between devices, local_blocks(): projected = in_hbm(lax.ppermute(summed, ('ctx', 'head'), pairs))  6.48 us
    pallas_call x1, Pallas kernels, attention(): pl.pallas_call(body, out_shape=[pltpu.VMEM((length, width), jnp.bfloat16)...  3.55 us
    pallas_call x1, Pallas kernels, pack_weight(): pl.pallas_call(body, out_shape=[pltpu.VMEM((count, width), jnp.bfloat16)...  1.9 us
    pallas_call x1, Pallas kernels, pack_heads(): pl.pallas_call(body, out_shape=[pltpu.VMEM((length + PAD_ROWS, total), jn...  1.48 us
  transfers between devices with their start and end apart: 20, of which 7 were waited for; matrix products, arithmetic and copies ran while one was open for 0% of the time, Pallas kernels for 10%

profile of v6, /device:TPU:1, one launch (start us, length us, event | category | flops | bytes accessed | tf_op | source)
XLA Modules:
  0.0 61.0 jit_solution(17210335795020726395)
XLA Ops:
  0.6 1.5 %pack_heads.1 = (bf16[136,768]{1,0:T(8,128)(2,1)S(1)}, bf16[136,768]{1,0:T(8,128)(2,1)S(1)}, bf16[136,768]{1,0:T(8,128)(2,1)S(1)}, bf16[136,768]{1,0:T(8,128)(2,...) custom-call(s32[1]{0:T(128)} %bitcast.c_ref, ...), custom_call_target="tpu_custom_call" | custom-call | tf_op jit(solution)/shard_map/pack_heads/pallas_call | solution.py:83
  2.1 5.0 %collective-permute-start.3 = (bf16[128,256]{1,0:T(8,128)(2,1)S(1)}, bf16[128,256]{1,0:T(8,128)(2,1)S(1)}, u32[]{:S(2)}, u32[]{:S(2)}) collective-permute-start(bf16[128,256]{1,0:T(8,128)(2,1)S(1)} %get-tuple-element.33), channel_id=1, source_target_pairs={{0,8},{2,10},{4,12},{6,14},{1,9},{3,11},{5,13},{7,15},{16,24},{18,... | collective-permute-start | bytes 196616 | tf_op jit(solution)/shard_map/ppermute | solution.py:387
  7.2 1.9 %pack_weight.1 = (bf16[256,512]{1,0:T(8,128)(2,1)S(1)}, bf16[256,512]{1,0:T(8,128)(2,1)S(1)}, bf16[256,512]{1,0:T(8,128)(2,1)S(1)}, bf16[128,512]{1,0:T(8,128)(2...) custom-call(s32[1]{0:T(128)} %bitcast.c_ref, s32[1]{0:T(128)} %bitcast.1.g_ref, s32[2,4]{1,0:T(2,128)} %bitcast.5, ...), custom_call_target="tpu_custom_call" | custom-call | tf_op jit(solution)/shard_map/pack_weight/pallas_call | solution.py:148
  9.1 2.3 %collective-permute-start.13 = (bf16[128,512]{1,0:T(8,128)(2,1)S(1)}, bf16[128,512]{1,0:T(8,128)(2,1)S(1)}, u32[]{:S(2)}, u32[]{:S(2)}) collective-permute-start(bf16[128,512]{1,0:T(8,128)(2,1)S(1)} %get-tuple-element.45), channel_id=1, source_target_pairs={{0,6},{2,4},{4,2},{6,0},{8,14},{10,12},{12,10},{14,8},{1,7},{3,5},... | collective-permute-start | bytes 393224 | tf_op jit(solution)/shard_map/ppermute | solution.py:387
  11.4 1.3 %collective-permute-start.4 = (bf16[128,256]{1,0:T(8,128)(2,1)S(1)}, bf16[128,256]{1,0:T(8,128)(2,1)S(1)}, u32[]{:S(2)}, u32[]{:S(2)}) collective-permute-start(bf16[128,256]{1,0:T(8,128)(2,1)S(1)} %get-tuple-element.34), channel_id=1, source_target_pairs={{0,10},{2,8},{4,14},{6,12},{1,11},{3,9},{5,15},{7,13},{16,26},{18,... | collective-permute-start | bytes 196616 | tf_op jit(solution)/shard_map/ppermute | solution.py:387
  12.7 1.3 %collective-permute-start.5 = (bf16[128,256]{1,0:T(8,128)(2,1)S(1)}, bf16[128,256]{1,0:T(8,128)(2,1)S(1)}, u32[]{:S(2)}, u32[]{:S(2)}) collective-permute-start(bf16[128,256]{1,0:T(8,128)(2,1)S(1)} %get-tuple-element.35), channel_id=1, source_target_pairs={{0,12},{2,14},{4,8},{6,10},{1,13},{3,15},{5,9},{7,11},{16,28},{18,... | collective-permute-start | bytes 196616 | tf_op jit(solution)/shard_map/ppermute | solution.py:387
  14.0 1.2 %collective-permute-start = (bf16[136,768]{1,0:T(8,128)(2,1)S(1)}, bf16[136,768]{1,0:T(8,128)(2,1)S(1)}, u32[]{:S(2)}, u32[]{:S(2)}) collective-permute-start(bf16[136,768]{1,0:T(8,128)(2,1)S(1)} %get-tuple-element.30), channel_id=1, source_target_pairs={{0,2},{2,0},{4,6},{6,4},{8,10},{10,8},{12,14},{14,12},{1,3},{3,1},... | collective-permute-start | bytes 626696 | tf_op jit(solution)/shard_map/ppermute | solution.py:387
  15.2 0.0 collective-permute-done.3.rest_4_
  15.2 1.6 %collective-permute-start.6 = (bf16[128,256]{1,0:T(8,128)(2,1)S(1)}, bf16[128,256]{1,0:T(8,128)(2,1)S(1)}, u32[]{:S(2)}, u32[]{:S(2)}) collective-permute-start(bf16[128,256]{1,0:T(8,128)(2,1)S(1)} %get-tuple-element.36), channel_id=1, source_target_pairs={{0,14},{2,12},{4,10},{6,8},{1,15},{3,13},{5,11},{7,9},{16,30},{18,... | collective-permute-start | bytes 196616 | tf_op jit(solution)/shard_map/ppermute | solution.py:387
  16.9 0.0 collective-permute-done.4.rest_5_
  16.9 0.1 collective-permute-start.1
  16.9 0.0 collective-permute-done.5.rest_6_
  17.0 3.2 %collective-permute-start.2 = (bf16[136,768]{1,0:T(8,128)(2,1)S(1)}, bf16[136,768]{1,0:T(8,128)(2,1)S(1)}, u32[]{:S(2)}, u32[]{:S(2)}) collective-permute-start(bf16[136,768]{1,0:T(8,128)(2,1)S(1)} %get-tuple-element.32), channel_id=1, source_target_pairs={{0,6},{2,4},{4,2},{6,0},{8,14},{10,12},{12,10},{14,8},{1,7},{3,5},... | collective-permute-start | bytes 626696 | tf_op jit(solution)/shard_map/ppermute | solution.py:387
  20.1 0.0 collective-permute-done.6.rest_7_
  20.1 0.0 collective-permute-start.11
  20.1 0.0 collective-permute-done.13.rest_3_
  20.1 2.5 %collective-permute-start.12 = (bf16[256,512]{1,0:T(8,128)(2,1)S(1)}, bf16[256,512]{1,0:T(8,128)(2,1)S(1)}, u32[]{:S(2)}, u32[]{:S(2)}) collective-permute-start(bf16[256,512]{1,0:T(8,128)(2,1)S(1)} %get-tuple-element.44), channel_id=1, source_target_pairs={{0,4},{2,6},{4,0},{6,2},{8,12},{10,14},{12,8},{14,10},{1,5},{3,7},... | collective-permute-start | bytes 786440 | tf_op jit(solution)/shard_map/ppermute | solution.py:387
  22.7 0.0 collective-permute-done.rest_1_
  22.7 1.2 %collective-permute-start.14 = (bf16[128,512]{1,0:T(8,128)(2,1)S(1)}, bf16[128,512]{1,0:T(8,128)(2,1)S(1)}, u32[]{:S(2)}, u32[]{:S(2)}) collective-permute-start(bf16[128,512]{1,0:T(8,128)(2,1)S(1)} %collective-permute-done.13.rest_3_), channel_id=1, source_target_pairs={{0,16},{16,0},{1,17},{17,1},{2,18},{18,2},{3,19},{19,3},{4,20},{20... | collective-permute-start | bytes 393224 | tf_op jit(solution)/shard_map/ppermute | solution.py:387
  23.9 0.0 collective-permute-done.1.rest_2_
  23.9 2.8 %collective-permute-done.2.rest_3_ = bf16[136,768]{1,0:T(8,128)(2,1)S(1)} collective-permute-done((bf16[136,768]{1,0:T(8,128)(2,1)S(1)}, bf16[136,768]{1,0:T(8,128)(2,1)S(1)}, u32[]{:S(2)}, u32[]{:S(2)}) %collective-permute-start.2) | collective-permute-done | bytes 208928 | tf_op jit(solution)/shard_map/ppermute | solution.py:387
  26.7 3.5 %attention.1 = (bf16[128,512]{1,0:T(8,128)(2,1)S(1)}, bf16[128,512]{1,0:T(8,128)(2,1)S(1)}, bf16[128,512]{1,0:T(8,128)(2,1)S(1)}, bf16[128,512]{1,0:T(8,128)(2,1)S(1)}, bf16[64,512]{1,0:T(8,128)(2,1)S(1)}) custom-call(s32[1]{0:T(128)} %bitcast.c_ref, f32[4,128,1024]{2,1,0:T(8,128)S(1)} %get-tuple-element.27.mask_ref, ...), custom_call_target="tpu_custom_call" | custom-call | tf_op jit(solution)/shard_map/attention/pallas_call | solution.py:251
  30.3 2.1 %collective-permute-start.10 = (bf16[64,512]{1,0:T(8,128)(2,1)S(1)}, bf16[64,512]{1,0:T(8,128)(2,1)S(1)}, u32[]{:S(2)}, u32[]{:S(2)}) collective-permute-start(bf16[64,512]{1,0:T(8,128)(2,1)S(1)} %get-tuple-element.41.own_ref), channel_id=1, source_target_pairs={{0,8},{2,10},{4,12},{6,14},{8,0},{10,2},{12,4},{14,6},{1,9},{3,11}... | collective-permute-start | bytes 196616 | tf_op jit(solution)/shard_map/ppermute | solution.py:387
  32.4 0.0 collective-permute-done.14.rest_4_
  32.4 0.0 collective-permute-done.11.rest_1_
  32.4 0.2 collective-permute-done.12.rest_2_
  32.6 2.5 %collective-permute-done.10.other_ref = bf16[64,512]{1,0:T(8,128)(2,1)S(1)} collective-permute-done((bf16[64,512]{1,0:T(8,128)(2,1)S(1)}, bf16[64,512]{1,0:T(8,128)(2,1)S(1)}, u32[]{:S(2)}, u32[]{:S(2)}) %collective-permute-start.10) | collective-permute-done | bytes 65568 | tf_op jit(solution)/shard_map/ppermute | solution.py:387
  35.1 0.5 project.1
  35.5 6.0 %collective-permute-start.15 = (f32[64,1024]{1,0:T(8,128)S(1)}, f32[64,1024]{1,0:T(8,128)S(1)}, u32[]{:S(2)}, u32[]{:S(2)}) collective-permute-start(f32[64,1024]{1,0:T(8,128)S(1)} %get-tuple-element.47), channel_id=1, source_target_pairs={{0,1},{1,0},{2,3},{3,2},{4,5},{5,4},{6,7},{7,6},{8,9},{9,8},{10,11... | collective-permute-start | bytes 786440 | tf_op jit(solution)/shard_map/ppermute | solution.py:387
  41.5 2.2 %collective-permute-start.7 = (bf16[128,512]{1,0:T(8,128)(2,1)S(1)}, bf16[128,512]{1,0:T(8,128)(2,1)S(1)}, u32[]{:S(2)}, u32[]{:S(2)}) collective-permute-start(bf16[128,512]{1,0:T(8,128)(2,1)S(1)} %get-tuple-element.38), channel_id=1, source_target_pairs={{0,2},{2,0},{4,6},{6,4},{8,10},{10,8},{12,14},{14,12},{1,3},{3,1},... | collective-permute-start | bytes 393224 | tf_op jit(solution)/shard_map/ppermute | solution.py:387
  43.7 0.0 collective-permute-start.8
  43.7 1.2 %collective-permute-start.9 = (bf16[128,512]{1,0:T(8,128)(2,1)S(1)}, bf16[128,512]{1,0:T(8,128)(2,1)S(1)}, u32[]{:S(2)}, u32[]{:S(2)}) collective-permute-start(bf16[128,512]{1,0:T(8,128)(2,1)S(1)} %get-tuple-element.40), channel_id=1, source_target_pairs={{0,6},{2,4},{4,2},{6,0},{8,14},{10,12},{12,10},{14,8},{1,7},{3,5},... | collective-permute-start | bytes 393224 | tf_op jit(solution)/shard_map/ppermute | solution.py:387
  44.9 0.0 collective-permute-done.15.b_ref
  44.9 1.5 %collective-permute-start.16 = (bf16[16,1024]{1,0:T(8,128)(2,1)S(1)}, bf16[16,1024]{1,0:T(8,128)(2,1)S(1)}, u32[]{:S(2)}, u32[]{:S(2)}) collective-permute-start(bf16[16,1024]{1,0:T(8,128)(2,1)S(1)} %get-tuple-element.49), channel_id=1, source_target_pairs={{0,2},{2,0},{4,6},{6,4},{8,10},{10,8},{12,14},{14,12},{1,3},{3,1},... | collective-permute-start | bytes 98312 | tf_op jit(solution)/shard_map/ppermute | solution.py:387
  46.4 0.0 collective-permute-start.17
  46.4 1.6 %collective-permute-done.16.rest_1_ = bf16[16,1024]{1,0:T(8,128)(2,1)S(1)} collective-permute-done((bf16[16,1024]{1,0:T(8,128)(2,1)S(1)}, bf16[16,1024]{1,0:T(8,128)(2,1)S(1)}, u32[]{:S(2)}, u32[]{:S(2)}) %collective-permute-start.16) | collective-permute-done | bytes 32800 | tf_op jit(solution)/shard_map/ppermute | solution.py:387
  48.1 1.1 %collective-permute-start.18 = (bf16[16,1024]{1,0:T(8,128)(2,1)S(1)}, bf16[16,1024]{1,0:T(8,128)(2,1)S(1)}, u32[]{:S(2)}, u32[]{:S(2)}) collective-permute-start(bf16[16,1024]{1,0:T(8,128)(2,1)S(1)} %get-tuple-element.51), channel_id=1, source_target_pairs={{0,6},{2,4},{4,2},{6,0},{8,14},{10,12},{12,10},{14,8},{1,7},{3,5},... | collective-permute-start | bytes 98312 | tf_op jit(solution)/shard_map/ppermute | solution.py:387
  49.2 2.7 %collective-permute-done.17.rest_2_ = bf16[16,1024]{1,0:T(8,128)(2,1)S(1)} collective-permute-done((bf16[16,1024]{1,0:T(8,128)(2,1)S(1)}, bf16[16,1024]{1,0:T(8,128)(2,1)S(1)}, u32[]{:S(2)}, u32[]{:S(2)}) %collective-permute-start.17) | collective-permute-done | bytes 32800 | tf_op jit(solution)/shard_map/ppermute | solution.py:387
  51.9 0.4 collective-permute-done.18.rest_3_
  52.4 6.5 %collective-permute-start.19 = (bf16[16,1024]{1,0:T(8,128)(2,1)S(1)}, bf16[16,1024]{1,0:T(8,128)(2,1)S(1)}, u32[]{:S(2)}, u32[]{:S(2)}) collective-permute-start(bf16[16,1024]{1,0:T(8,128)(2,1)S(1)} %add_shares.1), channel_id=1, source_target_pairs={{0,0},{1,8},{2,2},{3,10},{4,4},{5,12},{6,6},{7,14},{8,1},{9,9},{10... | collective-permute-start | bytes 98312 | tf_op jit(solution)/shard_map/ppermute | solution.py:422
  58.8 0.0 collective-permute-done.7.rest_1_
  58.9 0.0 collective-permute-done.8.rest_2_
  58.9 0.0 collective-permute-done.9.rest_3_
  58.9 0.8 %join_heads.1 = bf16[128,2048]{1,0:T(8,128)(2,1)} custom-call(s32[1]{0:T(128)} %bitcast.c_ref, bf16[128,512]{1,0:T(8,128)(2,1)S(1)} %get-tuple-element.37.rest_0_, bf16[128,512]{1,0:T(8,128)(2,1)S(1)} %collective-permute-done.7.rest_1_, bf16[128,512]{1,0:T(8,128)(2,1)S(1)} %collective-permute-done.8.rest_2_, bf16[128,512]{1,0:T(8,128)(2,1)S(1)} %collective-permute-done.9.rest_3_), custom_call_target="tpu_custom_call" | custom-call | tf_op jit(solution)/shard_map/join_heads/pallas_call | solution.py:356
  59.7 0.7 %collective-permute-done.19 = bf16[16,1024]{1,0:T(8,128)(2,1)S(1)} collective-permute-done((bf16[16,1024]{1,0:T(8,128)(2,1)S(1)}, bf16[16,1024]{1,0:T(8,128)(2,1)S(1)}, u32[]{:S(2)}, u32[]{:S(2)}) %collective-permute-start.19) | collective-permute-done | bytes 32800 | tf_op jit(solution)/shard_map/ppermute | solution.py:422
  60.4 0.6 %copy.11 = bf16[16,1024]{1,0:T(8,128)(2,1)} copy(bf16[16,1024]{1,0:T(8,128)(2,1)S(1)} %collective-permute-done.19) | data formatting | bytes 65536
  (2 shorter events, 0.1 us)
Async XLA Ops:
  2.1 13.1 %collective-permute-start.3 = (bf16[128,256]{1,0:T(8,128)(2,1)S(1)}, bf16[128,256]{1,0:T(8,128)(2,1)S(1)}, u32[]{:S(2)}, u32[]{:S(2)}) collective-permute-start(bf16[128,256]{1,0:T(8,128)(2,1)S(1)} %get-tuple-element.33), channel_id=1, source_target_pairs={{0,8},{2,10},{4,12},{6,14},{1,9},{3,11},{5,13},{7,15},{16,24},{18,... | collective-permute-start | bytes 196616 | tf_op jit(solution)/shard_map/ppermute | solution.py:387
  9.1 11.1 %collective-permute-start.13 = (bf16[128,512]{1,0:T(8,128)(2,1)S(1)}, bf16[128,512]{1,0:T(8,128)(2,1)S(1)}, u32[]{:S(2)}, u32[]{:S(2)}) collective-permute-start(bf16[128,512]{1,0:T(8,128)(2,1)S(1)} %get-tuple-element.45), channel_id=1, source_target_pairs={{0,6},{2,4},{4,2},{6,0},{8,14},{10,12},{12,10},{14,8},{1,7},{3,5},... | collective-permute-start | bytes 393224 | tf_op jit(solution)/shard_map/ppermute | solution.py:387
  11.4 5.5 %collective-permute-start.4 = (bf16[128,256]{1,0:T(8,128)(2,1)S(1)}, bf16[128,256]{1,0:T(8,128)(2,1)S(1)}, u32[]{:S(2)}, u32[]{:S(2)}) collective-permute-start(bf16[128,256]{1,0:T(8,128)(2,1)S(1)} %get-tuple-element.34), channel_id=1, source_target_pairs={{0,10},{2,8},{4,14},{6,12},{1,11},{3,9},{5,15},{7,13},{16,26},{18,... | collective-permute-start | bytes 196616 | tf_op jit(solution)/shard_map/ppermute | solution.py:387
  12.7 4.3 %collective-permute-start.5 = (bf16[128,256]{1,0:T(8,128)(2,1)S(1)}, bf16[128,256]{1,0:T(8,128)(2,1)S(1)}, u32[]{:S(2)}, u32[]{:S(2)}) collective-permute-start(bf16[128,256]{1,0:T(8,128)(2,1)S(1)} %get-tuple-element.35), channel_id=1, source_target_pairs={{0,12},{2,14},{4,8},{6,10},{1,13},{3,15},{5,9},{7,11},{16,28},{18,... | collective-permute-start | bytes 196616 | tf_op jit(solution)/shard_map/ppermute | solution.py:387
  14.0 8.7 %collective-permute-start = (bf16[136,768]{1,0:T(8,128)(2,1)S(1)}, bf16[136,768]{1,0:T(8,128)(2,1)S(1)}, u32[]{:S(2)}, u32[]{:S(2)}) collective-permute-start(bf16[136,768]{1,0:T(8,128)(2,1)S(1)} %get-tuple-element.30), channel_id=1, source_target_pairs={{0,2},{2,0},{4,6},{6,4},{8,10},{10,8},{12,14},{14,12},{1,3},{3,1},... | collective-permute-start | bytes 626696 | tf_op jit(solution)/shard_map/ppermute | solution.py:387
  15.2 4.9 %collective-permute-start.6 = (bf16[128,256]{1,0:T(8,128)(2,1)S(1)}, bf16[128,256]{1,0:T(8,128)(2,1)S(1)}, u32[]{:S(2)}, u32[]{:S(2)}) collective-permute-start(bf16[128,256]{1,0:T(8,128)(2,1)S(1)} %get-tuple-element.36), channel_id=1, source_target_pairs={{0,14},{2,12},{4,10},{6,8},{1,15},{3,13},{5,11},{7,9},{16,30},{18,... | collective-permute-start | bytes 196616 | tf_op jit(solution)/shard_map/ppermute | solution.py:387
  16.9 7.0 %collective-permute-start.1 = (bf16[136,768]{1,0:T(8,128)(2,1)S(1)}, bf16[136,768]{1,0:T(8,128)(2,1)S(1)}, u32[]{:S(2)}, u32[]{:S(2)}) collective-permute-start(bf16[136,768]{1,0:T(8,128)(2,1)S(1)} %get-tuple-element.31), channel_id=1, source_target_pairs={{0,4},{2,6},{4,0},{6,2},{8,12},{10,14},{12,8},{14,10},{1,5},{3,7},... | collective-permute-start | bytes 626696 | tf_op jit(solution)/shard_map/ppermute | solution.py:387
  17.0 9.8 %collective-permute-start.2 = (bf16[136,768]{1,0:T(8,128)(2,1)S(1)}, bf16[136,768]{1,0:T(8,128)(2,1)S(1)}, u32[]{:S(2)}, u32[]{:S(2)}) collective-permute-start(bf16[136,768]{1,0:T(8,128)(2,1)S(1)} %get-tuple-element.32), channel_id=1, source_target_pairs={{0,6},{2,4},{4,2},{6,0},{8,14},{10,12},{12,10},{14,8},{1,7},{3,5},... | collective-permute-start | bytes 626696 | tf_op jit(solution)/shard_map/ppermute | solution.py:387
  20.1 12.3 %collective-permute-start.11 = (bf16[256,512]{1,0:T(8,128)(2,1)S(1)}, bf16[256,512]{1,0:T(8,128)(2,1)S(1)}, u32[]{:S(2)}, u32[]{:S(2)}) collective-permute-start(bf16[256,512]{1,0:T(8,128)(2,1)S(1)} %get-tuple-element.43), channel_id=1, source_target_pairs={{0,2},{2,0},{4,6},{6,4},{8,10},{10,8},{12,14},{14,12},{1,3},{3,1},... | collective-permute-start | bytes 786440 | tf_op jit(solution)/shard_map/ppermute | solution.py:387
  20.1 12.4 %collective-permute-start.12 = (bf16[256,512]{1,0:T(8,128)(2,1)S(1)}, bf16[256,512]{1,0:T(8,128)(2,1)S(1)}, u32[]{:S(2)}, u32[]{:S(2)}) collective-permute-start(bf16[256,512]{1,0:T(8,128)(2,1)S(1)} %get-tuple-element.44), channel_id=1, source_target_pairs={{0,4},{2,6},{4,0},{6,2},{8,12},{10,14},{12,8},{14,10},{1,5},{3,7},... | collective-permute-start | bytes 786440 | tf_op jit(solution)/shard_map/ppermute | solution.py:387
  22.7 9.8 %collective-permute-start.14 = (bf16[128,512]{1,0:T(8,128)(2,1)S(1)}, bf16[128,512]{1,0:T(8,128)(2,1)S(1)}, u32[]{:S(2)}, u32[]{:S(2)}) collective-permute-start(bf16[128,512]{1,0:T(8,128)(2,1)S(1)} %collective-permute-done.13.rest_3_), channel_id=1, source_target_pairs={{0,16},{16,0},{1,17},{17,1},{2,18},{18,2},{3,19},{19,3},{4,20},{20... | collective-permute-start | bytes 393224 | tf_op jit(solution)/shard_map/ppermute | solution.py:387
  30.3 4.8 %collective-permute-start.10 = (bf16[64,512]{1,0:T(8,128)(2,1)S(1)}, bf16[64,512]{1,0:T(8,128)(2,1)S(1)}, u32[]{:S(2)}, u32[]{:S(2)}) collective-permute-start(bf16[64,512]{1,0:T(8,128)(2,1)S(1)} %get-tuple-element.41.own_ref), channel_id=1, source_target_pairs={{0,8},{2,10},{4,12},{6,14},{8,0},{10,2},{12,4},{14,6},{1,9},{3,11}... | collective-permute-start | bytes 196616 | tf_op jit(solution)/shard_map/ppermute | solution.py:387
  35.5 9.3 %collective-permute-start.15 = (f32[64,1024]{1,0:T(8,128)S(1)}, f32[64,1024]{1,0:T(8,128)S(1)}, u32[]{:S(2)}, u32[]{:S(2)}) collective-permute-start(f32[64,1024]{1,0:T(8,128)S(1)} %get-tuple-element.47), channel_id=1, source_target_pairs={{0,1},{1,0},{2,3},{3,2},{4,5},{5,4},{6,7},{7,6},{8,9},{9,8},{10,11... | collective-permute-start | bytes 786440 | tf_op jit(solution)/shard_map/ppermute | solution.py:387
  41.5 17.3 %collective-permute-start.7 = (bf16[128,512]{1,0:T(8,128)(2,1)S(1)}, bf16[128,512]{1,0:T(8,128)(2,1)S(1)}, u32[]{:S(2)}, u32[]{:S(2)}) collective-permute-start(bf16[128,512]{1,0:T(8,128)(2,1)S(1)} %get-tuple-element.38), channel_id=1, source_target_pairs={{0,2},{2,0},{4,6},{6,4},{8,10},{10,8},{12,14},{14,12},{1,3},{3,1},... | collective-permute-start | bytes 393224 | tf_op jit(solution)/shard_map/ppermute | solution.py:387
  43.7 15.2 %collective-permute-start.8 = (bf16[128,512]{1,0:T(8,128)(2,1)S(1)}, bf16[128,512]{1,0:T(8,128)(2,1)S(1)}, u32[]{:S(2)}, u32[]{:S(2)}) collective-permute-start(bf16[128,512]{1,0:T(8,128)(2,1)S(1)} %get-tuple-element.39), channel_id=1, source_target_pairs={{0,4},{2,6},{4,0},{6,2},{8,12},{10,14},{12,8},{14,10},{1,5},{3,7},... | collective-permute-start | bytes 393224 | tf_op jit(solution)/shard_map/ppermute | solution.py:387
  43.7 15.2 %collective-permute-start.9 = (bf16[128,512]{1,0:T(8,128)(2,1)S(1)}, bf16[128,512]{1,0:T(8,128)(2,1)S(1)}, u32[]{:S(2)}, u32[]{:S(2)}) collective-permute-start(bf16[128,512]{1,0:T(8,128)(2,1)S(1)} %get-tuple-element.40), channel_id=1, source_target_pairs={{0,6},{2,4},{4,2},{6,0},{8,14},{10,12},{12,10},{14,8},{1,7},{3,5},... | collective-permute-start | bytes 393224 | tf_op jit(solution)/shard_map/ppermute | solution.py:387
  44.9 3.2 %collective-permute-start.16 = (bf16[16,1024]{1,0:T(8,128)(2,1)S(1)}, bf16[16,1024]{1,0:T(8,128)(2,1)S(1)}, u32[]{:S(2)}, u32[]{:S(2)}) collective-permute-start(bf16[16,1024]{1,0:T(8,128)(2,1)S(1)} %get-tuple-element.49), channel_id=1, source_target_pairs={{0,2},{2,0},{4,6},{6,4},{8,10},{10,8},{12,14},{14,12},{1,3},{3,1},... | collective-permute-start | bytes 98312 | tf_op jit(solution)/shard_map/ppermute | solution.py:387
  46.4 5.4 %collective-permute-start.17 = (bf16[16,1024]{1,0:T(8,128)(2,1)S(1)}, bf16[16,1024]{1,0:T(8,128)(2,1)S(1)}, u32[]{:S(2)}, u32[]{:S(2)}) collective-permute-start(bf16[16,1024]{1,0:T(8,128)(2,1)S(1)} %get-tuple-element.50), channel_id=1, source_target_pairs={{0,4},{2,6},{4,0},{6,2},{8,12},{10,14},{12,8},{14,10},{1,5},{3,7},... | collective-permute-start | bytes 98312 | tf_op jit(solution)/shard_map/ppermute | solution.py:387
  48.1 4.2 %collective-permute-start.18 = (bf16[16,1024]{1,0:T(8,128)(2,1)S(1)}, bf16[16,1024]{1,0:T(8,128)(2,1)S(1)}, u32[]{:S(2)}, u32[]{:S(2)}) collective-permute-start(bf16[16,1024]{1,0:T(8,128)(2,1)S(1)} %get-tuple-element.51), channel_id=1, source_target_pairs={{0,6},{2,4},{4,2},{6,0},{8,14},{10,12},{12,10},{14,8},{1,7},{3,5},... | collective-permute-start | bytes 98312 | tf_op jit(solution)/shard_map/ppermute | solution.py:387
  52.4 8.1 %collective-permute-start.19 = (bf16[16,1024]{1,0:T(8,128)(2,1)S(1)}, bf16[16,1024]{1,0:T(8,128)(2,1)S(1)}, u32[]{:S(2)}, u32[]{:S(2)}) collective-permute-start(bf16[16,1024]{1,0:T(8,128)(2,1)S(1)} %add_shares.1), channel_id=1, source_target_pairs={{0,0},{1,8},{2,2},{3,10},{4,4},{5,12},{6,6},{7,14},{8,1},{9,9},{10... | collective-permute-start | bytes 98312 | tf_op jit(solution)/shard_map/ppermute | solution.py:422

commit v7 on v6

--- a/solution.py
+++ b/solution.py
@@ -48,10 +48,10 @@
 
 def pack_heads(shard_index, query, key, value, kept_rows, heads):
     length = query.shape[0]
-    width = query.shape[1] // heads
     hd = HEAD_SIZE
+    group = query.shape[1] // heads // hd
     capacity = kept_rows.shape[1]
-    total = 2 * hd + width
+    total = (2 + group) * length
 
     def body(c_ref, q_ref, k_ref, v_ref, kept_ref, *rest):
         out, (kept_buf, sems) = rest[: 2 * heads], rest[2 * heads :]
@@ -59,36 +59,38 @@
         copies = [(kept_ref, kept_buf)]
         for j in range(heads):
             head = slot ^ j
-            q_from = q_ref.at[:, pl.ds(pl.multiple_of(head * width, hd), width)]
             k_from = k_ref.at[:, pl.ds(pl.multiple_of(head * hd, hd), hd)]
             v_from = v_ref.at[:, pl.ds(pl.multiple_of(head * hd, hd), hd)]
-            rows = pl.ds(0, length)
+            blocks = [k_from, v_from]
+            for g in range(group):
+                at = pl.multiple_of((head * group + g) * hd, hd)
+                blocks.append(q_ref.at[:, pl.ds(at, hd)])
             copies += [
-                (q_from, out[j].at[rows, pl.ds(2 * hd, width)]),
-                (k_from, out[j].at[rows, pl.ds(0, hd)]),
-                (v_from, out[j].at[rows, pl.ds(hd, hd)]),
+                (block, out[j].at[pl.ds(i * length, length), :]) for i, block in enumerate(blocks)
+            ]
+            copies += [
                 (k_from, out[heads + j].at[:, pl.ds(0, hd)]),
                 (v_from, out[heads + j].at[:, pl.ds(hd, hd)]),
             ]
         started = start_all(copies, sems)
         for j in range(heads):
-            out[j][length:, :] = jnp.zeros((PAD_ROWS, total), jnp.bfloat16)
+            out[j][total:, :] = jnp.zeros((PAD_ROWS, hd), jnp.bfloat16)
         started[0].wait()
         kept = kept_buf[...].astype(jnp.float32).astype(jnp.bfloat16)
         for j in range(heads):
-            out[j][length : length + 1, 0:capacity] = kept
+            out[j][total : total + 1, 0:capacity] = kept
         for copy in started[1:]:
             copy.wait()
 
     return pl.pallas_call(
         body,
-        out_shape=[pltpu.VMEM((length + PAD_ROWS, total), jnp.bfloat16)] * heads
+        out_shape=[pltpu.VMEM((total + PAD_ROWS, hd), jnp.bfloat16)] * heads
         + [pltpu.VMEM((length, 2 * hd), jnp.bfloat16)] * heads,
         in_specs=[SMEM] + [ANY] * 4,
         out_specs=[VMEM] * (2 * heads),
         scratch_shapes=[
             pltpu.VMEM((1, capacity), jnp.int32),
-            pltpu.SemaphoreType.DMA((1 + 5 * heads,)),
+            pltpu.SemaphoreType.DMA((1 + (4 + group) * heads,)),
         ],
         compiler_params=GRANT,
         name="pack_heads",
@@ -165,10 +167,10 @@
 
 def attention(shard_index, masks, table, near, far, keep_rows):
     heads = len(near)
-    length = near[0].shape[0] - PAD_ROWS
+    length = far[0].shape[0]
     hd = HEAD_SIZE
-    width = near[0].shape[1] - 2 * hd
-    group = width // hd
+    group = (near[0].shape[0] - PAD_ROWS) // length - 2
+    width = group * hd
     far_keys = len(far) * length
     keys = far_keys + heads * length
     block_rows = heads * keep_rows
@@ -187,15 +189,14 @@
         for k in range(heads):
             to = slot ^ k
             at = pl.ds(pl.multiple_of(far_keys + to * length, length), length)
-            k_all[at, :] = near_refs[k][0:length, 0:hd]
-            v_all[at, 0:hd] = near_refs[k][0:length, hd : 2 * hd]
-            for g in range(group):
-                q_at = pl.multiple_of((to * group + g) * length, length)
-                q_all[pl.ds(q_at, length), :] = near_refs[k][
-                    0:length, (2 + g) * hd : (3 + g) * hd
-                ]
+            k_all[at, :] = near_refs[k][0:length, :]
+            v_all[at, 0:hd] = near_refs[k][length : 2 * length, :]
+            q_at = pl.multiple_of(to * group * length, length)
+            q_all[pl.ds(q_at, group * length), :] = near_refs[k][
+                2 * length : (2 + group) * length, :
+            ]
             kept_at = pl.ds(pl.multiple_of(to * PAD_ROWS, PAD_ROWS), PAD_ROWS)
-            kept_all[kept_at, :] = near_refs[k][length:, 0:hd].astype(jnp.float32)
+            kept_all[kept_at, :] = near_refs[k][(2 + group) * length :, :].astype(jnp.float32)
         rows = jnp.zeros((block_rows, width), jnp.float32)
 
         def scores_of(step):
@@ -289,11 +290,14 @@
                 both, w_ref[...], (((1,), (1,)), ((), ())), preferred_element_type=jnp.float32
             )
             keep_ref[:, at] = share[:count]
-            send_ref[:, at] = share[count:]
+            send_ref[:, at] = share[count:].astype(jnp.bfloat16)
 
     return pl.pallas_call(
         body,
-        out_shape=[pltpu.VMEM((count, heads * outs), jnp.float32)] * 2,
+        out_shape=[
+            pltpu.VMEM((count, heads * outs), jnp.float32),
+            pltpu.VMEM((count, heads * outs), jnp.bfloat16),
+        ],
         in_specs=[SMEM] * 3 + [VMEM] * (3 + heads),
         out_specs=[VMEM] * 2,
         compiler_params=GRANT,
@@ -308,9 +312,9 @@
         slot = c_ref[0] % heads
         for j in range(heads):
             at = pl.multiple_of((slot ^ j) * keep_rows, 8)
-            out[j][...] = (a_ref[pl.ds(at, keep_rows), :] + b_ref[pl.ds(at, keep_rows), :]).astype(
-                jnp.bfloat16
-            )
+            out[j][...] = (
+                a_ref[pl.ds(at, keep_rows), :] + b_ref[pl.ds(at, keep_rows), :].astype(jnp.float32)
+            ).astype(jnp.bfloat16)
 
     return pl.pallas_call(
         body,

time: 61.3 us -> 60.9 us (level)
  waiting for transfers between devices: 11 us -> 10 us
    ppermute x19, waiting for transfers between devices: 10.2 us -> 9.32 us  [move(): return in_vmem(lax.ppermute(x, axis, pairs))]
  transfers between devices with their start and end apart: 20 -> 20, of which waited for: 7 -> 6; matrix products, arithmetic and copies ran while one was open for 0% -> 0% of each run, Pallas kernels for 10% -> 10%
where the time goes in v7:
time: 60.9 us; the launch traced here: 60.6 us
  starting transfers between devices  40.9 us (67%)
  waiting for transfers between devices  10 us (16%)
  Pallas kernels  8.2 us (13%)
  between operations  0.79 us (1%)
  local copies, waits for them, and re-layouts  0.61 us (1%)
    ppermute x19, starting transfers between devices, move(): return in_vmem(lax.ppermute(x, axis, pairs))  34.4 us
    ppermute x19, waiting for transfers between devices, move(): return in_vmem(lax.ppermute(x, axis, pairs))  9.32 us
    ppermute x1, starting transfers between devices, local_blocks(): projected = in_hbm(lax.ppermute(summed, ('ctx', 'head'), pairs))  6.5 us
    pallas_call x1, Pallas kernels, attention(): pl.pallas_call(body, out_shape=[pltpu.VMEM((length, width), jnp.bfloat16)...  3.47 us
    pallas_call x1, Pallas kernels, pack_weight(): pl.pallas_call(body, out_shape=[pltpu.VMEM((count, width), jnp.bfloat16)...  1.9 us
    pallas_call x1, Pallas kernels, pack_heads(): pl.pallas_call(body, out_shape=[pltpu.VMEM((total + PAD_ROWS, hd), jnp.bf...  1.5 us
  transfers between devices with their start and end apart: 20, of which 6 were waited for; matrix products, arithmetic and copies ran while one was open for 0% of the time, Pallas kernels for 10%

profile of v7, /device:TPU:1, one launch (start us, length us, event | category | flops | bytes accessed | tf_op | source)
XLA Modules:
  0.0 60.6 jit_solution(4353070574183200566)
XLA Ops:
  0.6 1.5 %pack_heads.1 = (bf16[776,128]{1,0:T(8,128)(2,1)S(1)}, bf16[776,128]{1,0:T(8,128)(2,1)S(1)}, bf16[776,128]{1,0:T(8,128)(2,1)S(1)}, bf16[776,128]{1,0:T(8,128)(2,...) custom-call(s32[1]{0:T(128)} %bitcast.c_ref, ...), custom_call_target="tpu_custom_call" | custom-call | tf_op jit(solution)/shard_map/pack_heads/pallas_call | solution.py:85
  2.1 5.0 %collective-permute-start.3 = (bf16[128,256]{1,0:T(8,128)(2,1)S(1)}, bf16[128,256]{1,0:T(8,128)(2,1)S(1)}, u32[]{:S(2)}, u32[]{:S(2)}) collective-permute-start(bf16[128,256]{1,0:T(8,128)(2,1)S(1)} %get-tuple-element.33), channel_id=1, source_target_pairs={{0,8},{2,10},{4,12},{6,14},{1,9},{3,11},{5,13},{7,15},{16,24},{18,... | collective-permute-start | bytes 196616 | tf_op jit(solution)/shard_map/ppermute | solution.py:391
  7.2 1.9 %pack_weight.1 = (bf16[256,512]{1,0:T(8,128)(2,1)S(1)}, bf16[256,512]{1,0:T(8,128)(2,1)S(1)}, bf16[256,512]{1,0:T(8,128)(2,1)S(1)}, bf16[128,512]{1,0:T(8,128)(2...) custom-call(s32[1]{0:T(128)} %bitcast.c_ref, s32[1]{0:T(128)} %bitcast.1.g_ref, s32[2,4]{1,0:T(2,128)} %bitcast.5, ...), custom_call_target="tpu_custom_call" | custom-call | tf_op jit(solution)/shard_map/pack_weight/pallas_call | solution.py:150
  9.1 2.3 %collective-permute-start.13 = (bf16[128,512]{1,0:T(8,128)(2,1)S(1)}, bf16[128,512]{1,0:T(8,128)(2,1)S(1)}, u32[]{:S(2)}, u32[]{:S(2)}) collective-permute-start(bf16[128,512]{1,0:T(8,128)(2,1)S(1)} %get-tuple-element.45), channel_id=1, source_target_pairs={{0,6},{2,4},{4,2},{6,0},{8,14},{10,12},{12,10},{14,8},{1,7},{3,5},... | collective-permute-start | bytes 393224 | tf_op jit(solution)/shard_map/ppermute | solution.py:391
  11.4 1.3 %collective-permute-start.4 = (bf16[128,256]{1,0:T(8,128)(2,1)S(1)}, bf16[128,256]{1,0:T(8,128)(2,1)S(1)}, u32[]{:S(2)}, u32[]{:S(2)}) collective-permute-start(bf16[128,256]{1,0:T(8,128)(2,1)S(1)} %get-tuple-element.34), channel_id=1, source_target_pairs={{0,10},{2,8},{4,14},{6,12},{1,11},{3,9},{5,15},{7,13},{16,26},{18,... | collective-permute-start | bytes 196616 | tf_op jit(solution)/shard_map/ppermute | solution.py:391
  12.7 1.3 %collective-permute-start.5 = (bf16[128,256]{1,0:T(8,128)(2,1)S(1)}, bf16[128,256]{1,0:T(8,128)(2,1)S(1)}, u32[]{:S(2)}, u32[]{:S(2)}) collective-permute-start(bf16[128,256]{1,0:T(8,128)(2,1)S(1)} %get-tuple-element.35), channel_id=1, source_target_pairs={{0,12},{2,14},{4,8},{6,10},{1,13},{3,15},{5,9},{7,11},{16,28},{18,... | collective-permute-start | bytes 196616 | tf_op jit(solution)/shard_map/ppermute | solution.py:391
  14.0 1.2 %collective-permute-start = (bf16[776,128]{1,0:T(8,128)(2,1)S(1)}, bf16[776,128]{1,0:T(8,128)(2,1)S(1)}, u32[]{:S(2)}, u32[]{:S(2)}) collective-permute-start(bf16[776,128]{1,0:T(8,128)(2,1)S(1)} %get-tuple-element.30), channel_id=1, source_target_pairs={{0,2},{2,0},{4,6},{6,4},{8,10},{10,8},{12,14},{14,12},{1,3},{3,1},... | collective-permute-start | bytes 595976 | tf_op jit(solution)/shard_map/ppermute | solution.py:391
  15.2 0.0 collective-permute-done.3.rest_4_
  15.2 1.6 %collective-permute-start.6 = (bf16[128,256]{1,0:T(8,128)(2,1)S(1)}, bf16[128,256]{1,0:T(8,128)(2,1)S(1)}, u32[]{:S(2)}, u32[]{:S(2)}) collective-permute-start(bf16[128,256]{1,0:T(8,128)(2,1)S(1)} %get-tuple-element.36), channel_id=1, source_target_pairs={{0,14},{2,12},{4,10},{6,8},{1,15},{3,13},{5,11},{7,9},{16,30},{18,... | collective-permute-start | bytes 196616 | tf_op jit(solution)/shard_map/ppermute | solution.py:391
  16.9 0.0 collective-permute-done.4.rest_5_
  16.9 0.1 collective-permute-start.1
  17.0 0.0 collective-permute-done.5.rest_6_
  17.0 3.2 %collective-permute-start.2 = (bf16[776,128]{1,0:T(8,128)(2,1)S(1)}, bf16[776,128]{1,0:T(8,128)(2,1)S(1)}, u32[]{:S(2)}, u32[]{:S(2)}) collective-permute-start(bf16[776,128]{1,0:T(8,128)(2,1)S(1)} %get-tuple-element.32), channel_id=1, source_target_pairs={{0,6},{2,4},{4,2},{6,0},{8,14},{10,12},{12,10},{14,8},{1,7},{3,5},... | collective-permute-start | bytes 595976 | tf_op jit(solution)/shard_map/ppermute | solution.py:391
  20.2 0.0 collective-permute-done.6.rest_7_
  20.2 0.0 collective-permute-start.11
  20.2 0.0 collective-permute-done.13.rest_3_
  20.2 2.5 %collective-permute-start.12 = (bf16[256,512]{1,0:T(8,128)(2,1)S(1)}, bf16[256,512]{1,0:T(8,128)(2,1)S(1)}, u32[]{:S(2)}, u32[]{:S(2)}) collective-permute-start(bf16[256,512]{1,0:T(8,128)(2,1)S(1)} %get-tuple-element.44), channel_id=1, source_target_pairs={{0,4},{2,6},{4,0},{6,2},{8,12},{10,14},{12,8},{14,10},{1,5},{3,7},... | collective-permute-start | bytes 786440 | tf_op jit(solution)/shard_map/ppermute | solution.py:391
  22.7 0.0 collective-permute-done.rest_1_
  22.7 1.2 %collective-permute-start.14 = (bf16[128,512]{1,0:T(8,128)(2,1)S(1)}, bf16[128,512]{1,0:T(8,128)(2,1)S(1)}, u32[]{:S(2)}, u32[]{:S(2)}) collective-permute-start(bf16[128,512]{1,0:T(8,128)(2,1)S(1)} %collective-permute-done.13.rest_3_), channel_id=1, source_target_pairs={{0,16},{16,0},{1,17},{17,1},{2,18},{18,2},{3,19},{19,3},{4,20},{20... | collective-permute-start | bytes 393224 | tf_op jit(solution)/shard_map/ppermute | solution.py:391
  23.9 0.0 collective-permute-done.1.rest_2_
  23.9 2.4 %collective-permute-done.2.rest_3_ = bf16[776,128]{1,0:T(8,128)(2,1)S(1)} collective-permute-done((bf16[776,128]{1,0:T(8,128)(2,1)S(1)}, bf16[776,128]{1,0:T(8,128)(2,1)S(1)}, u32[]{:S(2)}, u32[]{:S(2)}) %collective-permute-start.2) | collective-permute-done | bytes 198688 | tf_op jit(solution)/shard_map/ppermute | solution.py:391
  26.3 3.5 %attention.1 = (bf16[128,512]{1,0:T(8,128)(2,1)S(1)}, bf16[128,512]{1,0:T(8,128)(2,1)S(1)}, bf16[128,512]{1,0:T(8,128)(2,1)S(1)}, bf16[128,512]{1,0:T(8,128)(2,1)S(1)}, bf16[64,512]{1,0:T(8,128)(2,1)S(1)}) custom-call(s32[1]{0:T(128)} %bitcast.c_ref, f32[4,128,1024]{2,1,0:T(8,128)S(1)} %get-tuple-element.27.mask_ref, ...), custom_call_target="tpu_custom_call" | custom-call | tf_op jit(solution)/shard_map/attention/pallas_call | solution.py:252
  29.8 2.4 %collective-permute-start.10 = (bf16[64,512]{1,0:T(8,128)(2,1)S(1)}, bf16[64,512]{1,0:T(8,128)(2,1)S(1)}, u32[]{:S(2)}, u32[]{:S(2)}) collective-permute-start(bf16[64,512]{1,0:T(8,128)(2,1)S(1)} %get-tuple-element.41.own_ref), channel_id=1, source_target_pairs={{0,8},{2,10},{4,12},{6,14},{8,0},{10,2},{12,4},{14,6},{1,9},{3,11}... | collective-permute-start | bytes 196616 | tf_op jit(solution)/shard_map/ppermute | solution.py:391
  32.1 0.0 collective-permute-done.14.rest_4_
  32.1 0.0 collective-permute-done.11.rest_1_
  32.2 0.0 collective-permute-done.12.rest_2_
  32.2 2.1 %collective-permute-done.10.other_ref = bf16[64,512]{1,0:T(8,128)(2,1)S(1)} collective-permute-done((bf16[64,512]{1,0:T(8,128)(2,1)S(1)}, bf16[64,512]{1,0:T(8,128)(2,1)S(1)}, u32[]{:S(2)}, u32[]{:S(2)}) %collective-permute-start.10) | collective-permute-done | bytes 65568 | tf_op jit(solution)/shard_map/ppermute | solution.py:391
  34.3 0.5 project.1
  34.7 6.3 %collective-permute-start.15 = (bf16[64,1024]{1,0:T(8,128)(2,1)S(1)}, bf16[64,1024]{1,0:T(8,128)(2,1)S(1)}, u32[]{:S(2)}, u32[]{:S(2)}) collective-permute-start(bf16[64,1024]{1,0:T(8,128)(2,1)S(1)} %get-tuple-element.47), channel_id=1, source_target_pairs={{0,1},{1,0},{2,3},{3,2},{4,5},{5,4},{6,7},{7,6},{8,9},{9,8},{10,11... | collective-permute-start | bytes 393224 | tf_op jit(solution)/shard_map/ppermute | solution.py:391
  41.0 2.1 %collective-permute-start.7 = (bf16[128,512]{1,0:T(8,128)(2,1)S(1)}, bf16[128,512]{1,0:T(8,128)(2,1)S(1)}, u32[]{:S(2)}, u32[]{:S(2)}) collective-permute-start(bf16[128,512]{1,0:T(8,128)(2,1)S(1)} %get-tuple-element.38), channel_id=1, source_target_pairs={{0,2},{2,0},{4,6},{6,4},{8,10},{10,8},{12,14},{14,12},{1,3},{3,1},... | collective-permute-start | bytes 393224 | tf_op jit(solution)/shard_map/ppermute | solution.py:391
  43.2 0.0 collective-permute-start.8
  43.2 1.2 %collective-permute-start.9 = (bf16[128,512]{1,0:T(8,128)(2,1)S(1)}, bf16[128,512]{1,0:T(8,128)(2,1)S(1)}, u32[]{:S(2)}, u32[]{:S(2)}) collective-permute-start(bf16[128,512]{1,0:T(8,128)(2,1)S(1)} %get-tuple-element.40), channel_id=1, source_target_pairs={{0,6},{2,4},{4,2},{6,0},{8,14},{10,12},{12,10},{14,8},{1,7},{3,5},... | collective-permute-start | bytes 393224 | tf_op jit(solution)/shard_map/ppermute | solution.py:391
  44.4 0.0 collective-permute-done.15.b_ref
  44.4 1.5 %collective-permute-start.16 = (bf16[16,1024]{1,0:T(8,128)(2,1)S(1)}, bf16[16,1024]{1,0:T(8,128)(2,1)S(1)}, u32[]{:S(2)}, u32[]{:S(2)}) collective-permute-start(bf16[16,1024]{1,0:T(8,128)(2,1)S(1)} %get-tuple-element.49), channel_id=1, source_target_pairs={{0,2},{2,0},{4,6},{6,4},{8,10},{10,8},{12,14},{14,12},{1,3},{3,1},... | collective-permute-start | bytes 98312 | tf_op jit(solution)/shard_map/ppermute | solution.py:391
  45.9 0.0 collective-permute-start.17
  45.9 1.6 %collective-permute-done.16.rest_1_ = bf16[16,1024]{1,0:T(8,128)(2,1)S(1)} collective-permute-done((bf16[16,1024]{1,0:T(8,128)(2,1)S(1)}, bf16[16,1024]{1,0:T(8,128)(2,1)S(1)}, u32[]{:S(2)}, u32[]{:S(2)}) %collective-permute-start.16) | collective-permute-done | bytes 32800 | tf_op jit(solution)/shard_map/ppermute | solution.py:391
  47.6 1.1 %collective-permute-start.18 = (bf16[16,1024]{1,0:T(8,128)(2,1)S(1)}, bf16[16,1024]{1,0:T(8,128)(2,1)S(1)}, u32[]{:S(2)}, u32[]{:S(2)}) collective-permute-start(bf16[16,1024]{1,0:T(8,128)(2,1)S(1)} %get-tuple-element.51), channel_id=1, source_target_pairs={{0,6},{2,4},{4,2},{6,0},{8,14},{10,12},{12,10},{14,8},{1,7},{3,5},... | collective-permute-start | bytes 98312 | tf_op jit(solution)/shard_map/ppermute | solution.py:391
  48.7 2.7 %collective-permute-done.17.rest_2_ = bf16[16,1024]{1,0:T(8,128)(2,1)S(1)} collective-permute-done((bf16[16,1024]{1,0:T(8,128)(2,1)S(1)}, bf16[16,1024]{1,0:T(8,128)(2,1)S(1)}, u32[]{:S(2)}, u32[]{:S(2)}) %collective-permute-start.17) | collective-permute-done | bytes 32800 | tf_op jit(solution)/shard_map/ppermute | solution.py:391
  51.4 0.4 collective-permute-done.18.rest_3_
  51.8 6.5 %collective-permute-start.19 = (bf16[16,1024]{1,0:T(8,128)(2,1)S(1)}, bf16[16,1024]{1,0:T(8,128)(2,1)S(1)}, u32[]{:S(2)}, u32[]{:S(2)}) collective-permute-start(bf16[16,1024]{1,0:T(8,128)(2,1)S(1)} %add_shares.1), channel_id=1, source_target_pairs={{0,0},{1,8},{2,2},{3,10},{4,4},{5,12},{6,6},{7,14},{8,1},{9,9},{10... | collective-permute-start | bytes 98312 | tf_op jit(solution)/shard_map/ppermute | solution.py:426
  58.4 0.0 collective-permute-done.7.rest_1_
  58.4 0.0 collective-permute-done.8.rest_2_
  58.4 0.0 collective-permute-done.9.rest_3_
  58.4 0.8 %join_heads.1 = bf16[128,2048]{1,0:T(8,128)(2,1)} custom-call(s32[1]{0:T(128)} %bitcast.c_ref, bf16[128,512]{1,0:T(8,128)(2,1)S(1)} %get-tuple-element.37.rest_0_, bf16[128,512]{1,0:T(8,128)(2,1)S(1)} %collective-permute-done.7.rest_1_, bf16[128,512]{1,0:T(8,128)(2,1)S(1)} %collective-permute-done.8.rest_2_, bf16[128,512]{1,0:T(8,128)(2,1)S(1)} %collective-permute-done.9.rest_3_), custom_call_target="tpu_custom_call" | custom-call | tf_op jit(solution)/shard_map/join_heads/pallas_call | solution.py:360
  59.2 0.7 %collective-permute-done.19 = bf16[16,1024]{1,0:T(8,128)(2,1)S(1)} collective-permute-done((bf16[16,1024]{1,0:T(8,128)(2,1)S(1)}, bf16[16,1024]{1,0:T(8,128)(2,1)S(1)}, u32[]{:S(2)}, u32[]{:S(2)}) %collective-permute-start.19) | collective-permute-done | bytes 32800 | tf_op jit(solution)/shard_map/ppermute | solution.py:426
  59.9 0.6 %copy.11 = bf16[16,1024]{1,0:T(8,128)(2,1)} copy(bf16[16,1024]{1,0:T(8,128)(2,1)S(1)} %collective-permute-done.19) | data formatting | bytes 65536
  (2 shorter events, 0.1 us)
Async XLA Ops:
  2.1 13.1 %collective-permute-start.3 = (bf16[128,256]{1,0:T(8,128)(2,1)S(1)}, bf16[128,256]{1,0:T(8,128)(2,1)S(1)}, u32[]{:S(2)}, u32[]{:S(2)}) collective-permute-start(bf16[128,256]{1,0:T(8,128)(2,1)S(1)} %get-tuple-element.33), channel_id=1, source_target_pairs={{0,8},{2,10},{4,12},{6,14},{1,9},{3,11},{5,13},{7,15},{16,24},{18,... | collective-permute-start | bytes 196616 | tf_op jit(solution)/shard_map/ppermute | solution.py:391
  9.1 11.1 %collective-permute-start.13 = (bf16[128,512]{1,0:T(8,128)(2,1)S(1)}, bf16[128,512]{1,0:T(8,128)(2,1)S(1)}, u32[]{:S(2)}, u32[]{:S(2)}) collective-permute-start(bf16[128,512]{1,0:T(8,128)(2,1)S(1)} %get-tuple-element.45), channel_id=1, source_target_pairs={{0,6},{2,4},{4,2},{6,0},{8,14},{10,12},{12,10},{14,8},{1,7},{3,5},... | collective-permute-start | bytes 393224 | tf_op jit(solution)/shard_map/ppermute | solution.py:391
  11.4 5.5 %collective-permute-start.4 = (bf16[128,256]{1,0:T(8,128)(2,1)S(1)}, bf16[128,256]{1,0:T(8,128)(2,1)S(1)}, u32[]{:S(2)}, u32[]{:S(2)}) collective-permute-start(bf16[128,256]{1,0:T(8,128)(2,1)S(1)} %get-tuple-element.34), channel_id=1, source_target_pairs={{0,10},{2,8},{4,14},{6,12},{1,11},{3,9},{5,15},{7,13},{16,26},{18,... | collective-permute-start | bytes 196616 | tf_op jit(solution)/shard_map/ppermute | solution.py:391
  12.7 4.3 %collective-permute-start.5 = (bf16[128,256]{1,0:T(8,128)(2,1)S(1)}, bf16[128,256]{1,0:T(8,128)(2,1)S(1)}, u32[]{:S(2)}, u32[]{:S(2)}) collective-permute-start(bf16[128,256]{1,0:T(8,128)(2,1)S(1)} %get-tuple-element.35), channel_id=1, source_target_pairs={{0,12},{2,14},{4,8},{6,10},{1,13},{3,15},{5,9},{7,11},{16,28},{18,... | collective-permute-start | bytes 196616 | tf_op jit(solution)/shard_map/ppermute | solution.py:391
  14.0 8.7 %collective-permute-start = (bf16[776,128]{1,0:T(8,128)(2,1)S(1)}, bf16[776,128]{1,0:T(8,128)(2,1)S(1)}, u32[]{:S(2)}, u32[]{:S(2)}) collective-permute-start(bf16[776,128]{1,0:T(8,128)(2,1)S(1)} %get-tuple-element.30), channel_id=1, source_target_pairs={{0,2},{2,0},{4,6},{6,4},{8,10},{10,8},{12,14},{14,12},{1,3},{3,1},... | collective-permute-start | bytes 595976 | tf_op jit(solution)/shard_map/ppermute | solution.py:391
  15.2 4.9 %collective-permute-start.6 = (bf16[128,256]{1,0:T(8,128)(2,1)S(1)}, bf16[128,256]{1,0:T(8,128)(2,1)S(1)}, u32[]{:S(2)}, u32[]{:S(2)}) collective-permute-start(bf16[128,256]{1,0:T(8,128)(2,1)S(1)} %get-tuple-element.36), channel_id=1, source_target_pairs={{0,14},{2,12},{4,10},{6,8},{1,15},{3,13},{5,11},{7,9},{16,30},{18,... | collective-permute-start | bytes 196616 | tf_op jit(solution)/shard_map/ppermute | solution.py:391
  16.9 7.0 %collective-permute-start.1 = (bf16[776,128]{1,0:T(8,128)(2,1)S(1)}, bf16[776,128]{1,0:T(8,128)(2,1)S(1)}, u32[]{:S(2)}, u32[]{:S(2)}) collective-permute-start(bf16[776,128]{1,0:T(8,128)(2,1)S(1)} %get-tuple-element.31), channel_id=1, source_target_pairs={{0,4},{2,6},{4,0},{6,2},{8,12},{10,14},{12,8},{14,10},{1,5},{3,7},... | collective-permute-start | bytes 595976 | tf_op jit(solution)/shard_map/ppermute | solution.py:391
  17.0 9.3 %collective-permute-start.2 = (bf16[776,128]{1,0:T(8,128)(2,1)S(1)}, bf16[776,128]{1,0:T(8,128)(2,1)S(1)}, u32[]{:S(2)}, u32[]{:S(2)}) collective-permute-start(bf16[776,128]{1,0:T(8,128)(2,1)S(1)} %get-tuple-element.32), channel_id=1, source_target_pairs={{0,6},{2,4},{4,2},{6,0},{8,14},{10,12},{12,10},{14,8},{1,7},{3,5},... | collective-permute-start | bytes 595976 | tf_op jit(solution)/shard_map/ppermute | solution.py:391
  20.2 12.0 %collective-permute-start.11 = (bf16[256,512]{1,0:T(8,128)(2,1)S(1)}, bf16[256,512]{1,0:T(8,128)(2,1)S(1)}, u32[]{:S(2)}, u32[]{:S(2)}) collective-permute-start(bf16[256,512]{1,0:T(8,128)(2,1)S(1)} %get-tuple-element.43), channel_id=1, source_target_pairs={{0,2},{2,0},{4,6},{6,4},{8,10},{10,8},{12,14},{14,12},{1,3},{3,1},... | collective-permute-start | bytes 786440 | tf_op jit(solution)/shard_map/ppermute | solution.py:391
  20.2 12.0 %collective-permute-start.12 = (bf16[256,512]{1,0:T(8,128)(2,1)S(1)}, bf16[256,512]{1,0:T(8,128)(2,1)S(1)}, u32[]{:S(2)}, u32[]{:S(2)}) collective-permute-start(bf16[256,512]{1,0:T(8,128)(2,1)S(1)} %get-tuple-element.44), channel_id=1, source_target_pairs={{0,4},{2,6},{4,0},{6,2},{8,12},{10,14},{12,8},{14,10},{1,5},{3,7},... | collective-permute-start | bytes 786440 | tf_op jit(solution)/shard_map/ppermute | solution.py:391
  22.7 9.5 %collective-permute-start.14 = (bf16[128,512]{1,0:T(8,128)(2,1)S(1)}, bf16[128,512]{1,0:T(8,128)(2,1)S(1)}, u32[]{:S(2)}, u32[]{:S(2)}) collective-permute-start(bf16[128,512]{1,0:T(8,128)(2,1)S(1)} %collective-permute-done.13.rest_3_), channel_id=1, source_target_pairs={{0,16},{16,0},{1,17},{17,1},{2,18},{18,2},{3,19},{19,3},{4,20},{20... | collective-permute-start | bytes 393224 | tf_op jit(solution)/shard_map/ppermute | solution.py:391
  29.8 4.5 %collective-permute-start.10 = (bf16[64,512]{1,0:T(8,128)(2,1)S(1)}, bf16[64,512]{1,0:T(8,128)(2,1)S(1)}, u32[]{:S(2)}, u32[]{:S(2)}) collective-permute-start(bf16[64,512]{1,0:T(8,128)(2,1)S(1)} %get-tuple-element.41.own_ref), channel_id=1, source_target_pairs={{0,8},{2,10},{4,12},{6,14},{8,0},{10,2},{12,4},{14,6},{1,9},{3,11}... | collective-permute-start | bytes 196616 | tf_op jit(solution)/shard_map/ppermute | solution.py:391
  34.7 9.6 %collective-permute-start.15 = (bf16[64,1024]{1,0:T(8,128)(2,1)S(1)}, bf16[64,1024]{1,0:T(8,128)(2,1)S(1)}, u32[]{:S(2)}, u32[]{:S(2)}) collective-permute-start(bf16[64,1024]{1,0:T(8,128)(2,1)S(1)} %get-tuple-element.47), channel_id=1, source_target_pairs={{0,1},{1,0},{2,3},{3,2},{4,5},{5,4},{6,7},{7,6},{8,9},{9,8},{10,11... | collective-permute-start | bytes 393224 | tf_op jit(solution)/shard_map/ppermute | solution.py:391
  41.0 17.3 %collective-permute-start.7 = (bf16[128,512]{1,0:T(8,128)(2,1)S(1)}, bf16[128,512]{1,0:T(8,128)(2,1)S(1)}, u32[]{:S(2)}, u32[]{:S(2)}) collective-permute-start(bf16[128,512]{1,0:T(8,128)(2,1)S(1)} %get-tuple-element.38), channel_id=1, source_target_pairs={{0,2},{2,0},{4,6},{6,4},{8,10},{10,8},{12,14},{14,12},{1,3},{3,1},... | collective-permute-start | bytes 393224 | tf_op jit(solution)/shard_map/ppermute | solution.py:391
  43.2 15.2 %collective-permute-start.8 = (bf16[128,512]{1,0:T(8,128)(2,1)S(1)}, bf16[128,512]{1,0:T(8,128)(2,1)S(1)}, u32[]{:S(2)}, u32[]{:S(2)}) collective-permute-start(bf16[128,512]{1,0:T(8,128)(2,1)S(1)} %get-tuple-element.39), channel_id=1, source_target_pairs={{0,4},{2,6},{4,0},{6,2},{8,12},{10,14},{12,8},{14,10},{1,5},{3,7},... | collective-permute-start | bytes 393224 | tf_op jit(solution)/shard_map/ppermute | solution.py:391
  43.2 15.2 %collective-permute-start.9 = (bf16[128,512]{1,0:T(8,128)(2,1)S(1)}, bf16[128,512]{1,0:T(8,128)(2,1)S(1)}, u32[]{:S(2)}, u32[]{:S(2)}) collective-permute-start(bf16[128,512]{1,0:T(8,128)(2,1)S(1)} %get-tuple-element.40), channel_id=1, source_target_pairs={{0,6},{2,4},{4,2},{6,0},{8,14},{10,12},{12,10},{14,8},{1,7},{3,5},... | collective-permute-start | bytes 393224 | tf_op jit(solution)/shard_map/ppermute | solution.py:391
  44.4 3.2 %collective-permute-start.16 = (bf16[16,1024]{1,0:T(8,128)(2,1)S(1)}, bf16[16,1024]{1,0:T(8,128)(2,1)S(1)}, u32[]{:S(2)}, u32[]{:S(2)}) collective-permute-start(bf16[16,1024]{1,0:T(8,128)(2,1)S(1)} %get-tuple-element.49), channel_id=1, source_target_pairs={{0,2},{2,0},{4,6},{6,4},{8,10},{10,8},{12,14},{14,12},{1,3},{3,1},... | collective-permute-start | bytes 98312 | tf_op jit(solution)/shard_map/ppermute | solution.py:391
  45.9 5.4 %collective-permute-start.17 = (bf16[16,1024]{1,0:T(8,128)(2,1)S(1)}, bf16[16,1024]{1,0:T(8,128)(2,1)S(1)}, u32[]{:S(2)}, u32[]{:S(2)}) collective-permute-start(bf16[16,1024]{1,0:T(8,128)(2,1)S(1)} %get-tuple-element.50), channel_id=1, source_target_pairs={{0,4},{2,6},{4,0},{6,2},{8,12},{10,14},{12,8},{14,10},{1,5},{3,7},... | collective-permute-start | bytes 98312 | tf_op jit(solution)/shard_map/ppermute | solution.py:391
  47.6 4.2 %collective-permute-start.18 = (bf16[16,1024]{1,0:T(8,128)(2,1)S(1)}, bf16[16,1024]{1,0:T(8,128)(2,1)S(1)}, u32[]{:S(2)}, u32[]{:S(2)}) collective-permute-start(bf16[16,1024]{1,0:T(8,128)(2,1)S(1)} %get-tuple-element.51), channel_id=1, source_target_pairs={{0,6},{2,4},{4,2},{6,0},{8,14},{10,12},{12,10},{14,8},{1,7},{3,5},... | collective-permute-start | bytes 98312 | tf_op jit(solution)/shard_map/ppermute | solution.py:391
  51.8 8.1 %collective-permute-start.19 = (bf16[16,1024]{1,0:T(8,128)(2,1)S(1)}, bf16[16,1024]{1,0:T(8,128)(2,1)S(1)}, u32[]{:S(2)}, u32[]{:S(2)}) collective-permute-start(bf16[16,1024]{1,0:T(8,128)(2,1)S(1)} %add_shares.1), channel_id=1, source_target_pairs={{0,0},{1,8},{2,2},{3,10},{4,4},{5,12},{6,6},{7,14},{8,1},{9,9},{10... | collective-permute-start | bytes 98312 | tf_op jit(solution)/shard_map/ppermute | solution.py:426

commit v8 on v7

--- a/solution.py
+++ b/solution.py
@@ -105,8 +105,9 @@
     outs = weight.shape[0]
     sent = [outs] * (heads - 1) + [outs // 2]
 
-    def body(c_ref, g_ref, slash_ref, tile_ref, count_ref, w_ref, *rest):
-        out, (mask_ref, table_ref, tile_buf, sems) = rest[:heads], rest[heads:]
+    def body(c_ref, g_ref, slash_hbm, tile_hbm, count_hbm, w_ref, *rest):
+        out, rest = rest[:heads], rest[heads:]
+        mask_ref, table_ref, tile_buf, slash_ref, tile_ref, count_ref, sems = rest
         c = c_ref[0]
         slot = c % heads
         first = c - slot
@@ -115,10 +116,13 @@
             at = pl.multiple_of((slot ^ j) * width, HEAD_SIZE)
             row = pl.multiple_of(g_ref[0] * sent[j], sent[j]) if sent[j] < outs else 0
             copies.append((w_ref.at[pl.ds(row, sent[j]), pl.ds(at, width)], out[j]))
-        started = start_all(copies, sems)
+        tables = [(slash_hbm, slash_ref), (tile_hbm, tile_ref), (count_hbm, count_ref)]
+        started = start_all(tables + copies, sems)
         difference = lax.broadcasted_iota(jnp.int32, (length, length), 0) - lax.broadcasted_iota(
             jnp.int32, (length, length), 1
         )
+        for copy in started[: len(tables)]:
+            copy.wait()
         for d in range(size):
             distance = difference + d * length
             allowed = (distance >= 0) & (distance < LOCAL_BAND_KEYS)
@@ -144,7 +148,7 @@
             table_ref[s, 0:1, :] = jnp.full((1, lanes), count, jnp.int32)
             table_ref[s, 1:2, :] = jnp.full((1, lanes), before, jnp.int32)
             before = before + count
-        for copy in started:
+        for copy in started[len(tables) :]:
             copy.wait()
 
     return pl.pallas_call(
@@ -154,11 +158,14 @@
             pltpu.VMEM((heads, length, size * length), jnp.float32),
             pltpu.VMEM((heads, 8, lanes), jnp.int32),
         ],
-        in_specs=[SMEM] * 5 + [ANY],
+        in_specs=[SMEM] * 2 + [ANY] * 4,
         out_specs=[VMEM] * (heads + 2),
         scratch_shapes=[
             pltpu.VMEM((size + 3, length, length), jnp.float32),
-            pltpu.SemaphoreType.DMA((heads,)),
+            pltpu.SMEM(slash.shape, jnp.int32),
+            pltpu.SMEM(tiles.shape, jnp.int32),
+            pltpu.SMEM(counts.shape, jnp.int32),
+            pltpu.SemaphoreType.DMA((heads + 3,)),
         ],
         compiler_params=GRANT,
         name="pack_weight",

time: 60.9 us -> 61.4 us (level)
  waiting for transfers between devices: 10 us -> 11.4 us
    ppermute x19, starting transfers between devices: 34.4 us -> 32.6 us  [move(): return in_vmem(lax.ppermute(x, axis, pairs))]
    ppermute x1, starting transfers between devices: 6.5 us -> 8.04 us  [local_blocks(): projected = in_hbm(lax.ppermute(summed, ('ctx', 'head'), pairs))]
    ppermute x19, waiting for transfers between devices: 9.32 us -> 10.6 us  [move(): return in_vmem(lax.ppermute(x, axis, pairs))]
  transfers between devices with their start and end apart: 20 -> 20, of which waited for: 6 -> 7; matrix products, arithmetic and copies ran while one was open for 0% -> 0% of each run, Pallas kernels for 10% -> 9%
where the time goes in v8:
time: 61.4 us; the launch traced here: 61.1 us
  starting transfers between devices  40.7 us (66%)
  waiting for transfers between devices  11.4 us (19%)
  Pallas kernels  7.6 us (12%)
  between operations  0.79 us (1%)
    ppermute x19, starting transfers between devices, move(): return in_vmem(lax.ppermute(x, axis, pairs))  32.6 us
    ppermute x19, waiting for transfers between devices, move(): return in_vmem(lax.ppermute(x, axis, pairs))  10.6 us
    ppermute x1, starting transfers between devices, local_blocks(): projected = in_hbm(lax.ppermute(summed, ('ctx', 'head'), pairs))  8.04 us
    pallas_call x1, Pallas kernels, attention(): pl.pallas_call(body, out_shape=[pltpu.VMEM((length, width), jnp.bfloat16)...  3.46 us
    pallas_call x1, Pallas kernels, pack_heads(): pl.pallas_call(body, out_shape=[pltpu.VMEM((total + PAD_ROWS, hd), jnp.bf...  1.5 us
    pallas_call x1, Pallas kernels, pack_weight(): pl.pallas_call(body, out_shape=[pltpu.VMEM((count, width), jnp.bfloat16)...  1.3 us
  transfers between devices with their start and end apart: 20, of which 7 were waited for; matrix products, arithmetic and copies ran while one was open for 0% of the time, Pallas kernels for 9%

profile of v8, /device:TPU:1, one launch (start us, length us, event | category | flops | bytes accessed | tf_op | source)
XLA Modules:
  0.0 61.1 jit_solution(5534373939297292134)
XLA Ops:
  0.6 1.5 %pack_heads.1 = (bf16[776,128]{1,0:T(8,128)(2,1)S(1)}, bf16[776,128]{1,0:T(8,128)(2,1)S(1)}, bf16[776,128]{1,0:T(8,128)(2,1)S(1)}, bf16[776,128]{1,0:T(8,128)(2,...) custom-call(s32[1]{0:T(128)} %bitcast.c_ref, ...), custom_call_target="tpu_custom_call" | custom-call | tf_op jit(solution)/shard_map/pack_heads/pallas_call | solution.py:85
  2.1 5.0 %collective-permute-start.3 = (bf16[128,256]{1,0:T(8,128)(2,1)S(1)}, bf16[128,256]{1,0:T(8,128)(2,1)S(1)}, u32[]{:S(2)}, u32[]{:S(2)}) collective-permute-start(bf16[128,256]{1,0:T(8,128)(2,1)S(1)} %get-tuple-element.33), channel_id=1, source_target_pairs={{0,8},{2,10},{4,12},{6,14},{1,9},{3,11},{5,13},{7,15},{16,24},{18,... | collective-permute-start | bytes 196616 | tf_op jit(solution)/shard_map/ppermute | solution.py:398
  7.2 1.3 %pack_weight.1 = (bf16[256,512]{1,0:T(8,128)(2,1)S(1)}, bf16[256,512]{1,0:T(8,128)(2,1)S(1)}, bf16[256,512]{1,0:T(8,128)(2,1)S(1)}, bf16[128,512]{1,0:T(8,128)(2...) custom-call(s32[1]{0:T(128)} %bitcast.c_ref, s32[1]{0:T(128)} %bitcast.1.g_ref, s32[2,4]{1,0:T(2,128)} %bitcast.5, ...), custom_call_target="tpu_custom_call" | custom-call | tf_op jit(solution)/shard_map/pack_weight/pallas_call | solution.py:154
  8.5 2.3 %collective-permute-start.13 = (bf16[128,512]{1,0:T(8,128)(2,1)S(1)}, bf16[128,512]{1,0:T(8,128)(2,1)S(1)}, u32[]{:S(2)}, u32[]{:S(2)}) collective-permute-start(bf16[128,512]{1,0:T(8,128)(2,1)S(1)} %get-tuple-element.45), channel_id=1, source_target_pairs={{0,6},{2,4},{4,2},{6,0},{8,14},{10,12},{12,10},{14,8},{1,7},{3,5},... | collective-permute-start | bytes 393224 | tf_op jit(solution)/shard_map/ppermute | solution.py:398
  10.8 1.3 %collective-permute-start.4 = (bf16[128,256]{1,0:T(8,128)(2,1)S(1)}, bf16[128,256]{1,0:T(8,128)(2,1)S(1)}, u32[]{:S(2)}, u32[]{:S(2)}) collective-permute-start(bf16[128,256]{1,0:T(8,128)(2,1)S(1)} %get-tuple-element.34), channel_id=1, source_target_pairs={{0,10},{2,8},{4,14},{6,12},{1,11},{3,9},{5,15},{7,13},{16,26},{18,... | collective-permute-start | bytes 196616 | tf_op jit(solution)/shard_map/ppermute | solution.py:398
  12.1 1.3 %collective-permute-start.5 = (bf16[128,256]{1,0:T(8,128)(2,1)S(1)}, bf16[128,256]{1,0:T(8,128)(2,1)S(1)}, u32[]{:S(2)}, u32[]{:S(2)}) collective-permute-start(bf16[128,256]{1,0:T(8,128)(2,1)S(1)} %get-tuple-element.35), channel_id=1, source_target_pairs={{0,12},{2,14},{4,8},{6,10},{1,13},{3,15},{5,9},{7,11},{16,28},{18,... | collective-permute-start | bytes 196616 | tf_op jit(solution)/shard_map/ppermute | solution.py:398
  13.4 1.2 %collective-permute-start = (bf16[776,128]{1,0:T(8,128)(2,1)S(1)}, bf16[776,128]{1,0:T(8,128)(2,1)S(1)}, u32[]{:S(2)}, u32[]{:S(2)}) collective-permute-start(bf16[776,128]{1,0:T(8,128)(2,1)S(1)} %get-tuple-element.30), channel_id=1, source_target_pairs={{0,2},{2,0},{4,6},{6,4},{8,10},{10,8},{12,14},{14,12},{1,3},{3,1},... | collective-permute-start | bytes 595976 | tf_op jit(solution)/shard_map/ppermute | solution.py:398
  14.6 0.0 collective-permute-done.3.rest_4_
  14.6 2.2 %collective-permute-start.6 = (bf16[128,256]{1,0:T(8,128)(2,1)S(1)}, bf16[128,256]{1,0:T(8,128)(2,1)S(1)}, u32[]{:S(2)}, u32[]{:S(2)}) collective-permute-start(bf16[128,256]{1,0:T(8,128)(2,1)S(1)} %get-tuple-element.36), channel_id=1, source_target_pairs={{0,14},{2,12},{4,10},{6,8},{1,15},{3,13},{5,11},{7,9},{16,30},{18,... | collective-permute-start | bytes 196616 | tf_op jit(solution)/shard_map/ppermute | solution.py:398
  16.9 0.0 collective-permute-done.4.rest_5_
  16.9 0.1 collective-permute-start.1
  17.0 0.0 collective-permute-done.5.rest_6_
  17.0 2.5 %collective-permute-start.2 = (bf16[776,128]{1,0:T(8,128)(2,1)S(1)}, bf16[776,128]{1,0:T(8,128)(2,1)S(1)}, u32[]{:S(2)}, u32[]{:S(2)}) collective-permute-start(bf16[776,128]{1,0:T(8,128)(2,1)S(1)} %get-tuple-element.32), channel_id=1, source_target_pairs={{0,6},{2,4},{4,2},{6,0},{8,14},{10,12},{12,10},{14,8},{1,7},{3,5},... | collective-permute-start | bytes 595976 | tf_op jit(solution)/shard_map/ppermute | solution.py:398
  19.5 0.0 collective-permute-done.6.rest_7_
  19.5 0.1 collective-permute-start.11
  19.6 0.0 collective-permute-done.13.rest_3_
  19.6 2.3 %collective-permute-start.12 = (bf16[256,512]{1,0:T(8,128)(2,1)S(1)}, bf16[256,512]{1,0:T(8,128)(2,1)S(1)}, u32[]{:S(2)}, u32[]{:S(2)}) collective-permute-start(bf16[256,512]{1,0:T(8,128)(2,1)S(1)} %get-tuple-element.44), channel_id=1, source_target_pairs={{0,4},{2,6},{4,0},{6,2},{8,12},{10,14},{12,8},{14,10},{1,5},{3,7},... | collective-permute-start | bytes 786440 | tf_op jit(solution)/shard_map/ppermute | solution.py:398
  21.9 0.0 collective-permute-done.rest_1_
  21.9 1.2 %collective-permute-start.14 = (bf16[128,512]{1,0:T(8,128)(2,1)S(1)}, bf16[128,512]{1,0:T(8,128)(2,1)S(1)}, u32[]{:S(2)}, u32[]{:S(2)}) collective-permute-start(bf16[128,512]{1,0:T(8,128)(2,1)S(1)} %collective-permute-done.13.rest_3_), channel_id=1, source_target_pairs={{0,16},{16,0},{1,17},{17,1},{2,18},{18,2},{3,19},{19,3},{4,20},{20... | collective-permute-start | bytes 393224 | tf_op jit(solution)/shard_map/ppermute | solution.py:398
  23.1 0.0 collective-permute-done.1.rest_2_
  23.1 3.1 %collective-permute-done.2.rest_3_ = bf16[776,128]{1,0:T(8,128)(2,1)S(1)} collective-permute-done((bf16[776,128]{1,0:T(8,128)(2,1)S(1)}, bf16[776,128]{1,0:T(8,128)(2,1)S(1)}, u32[]{:S(2)}, u32[]{:S(2)}) %collective-permute-start.2) | collective-permute-done | bytes 198688 | tf_op jit(solution)/shard_map/ppermute | solution.py:398
  26.2 3.5 %attention.1 = (bf16[128,512]{1,0:T(8,128)(2,1)S(1)}, bf16[128,512]{1,0:T(8,128)(2,1)S(1)}, bf16[128,512]{1,0:T(8,128)(2,1)S(1)}, bf16[128,512]{1,0:T(8,128)(2,1)S(1)}, bf16[64,512]{1,0:T(8,128)(2,1)S(1)}) custom-call(s32[1]{0:T(128)} %bitcast.c_ref, f32[4,128,1024]{2,1,0:T(8,128)S(1)} %get-tuple-element.27.mask_ref, ...), custom_call_target="tpu_custom_call" | custom-call | tf_op jit(solution)/shard_map/attention/pallas_call | solution.py:259
  29.7 1.0 %collective-permute-start.10 = (bf16[64,512]{1,0:T(8,128)(2,1)S(1)}, bf16[64,512]{1,0:T(8,128)(2,1)S(1)}, u32[]{:S(2)}, u32[]{:S(2)}) collective-permute-start(bf16[64,512]{1,0:T(8,128)(2,1)S(1)} %get-tuple-element.41.own_ref), channel_id=1, source_target_pairs={{0,8},{2,10},{4,12},{6,14},{8,0},{10,2},{12,4},{14,6},{1,9},{3,11}... | collective-permute-start | bytes 196616 | tf_op jit(solution)/shard_map/ppermute | solution.py:398
  30.7 0.0 collective-permute-done.14.rest_4_
  30.8 0.0 collective-permute-done.11.rest_1_
  30.8 1.4 %collective-permute-done.12.rest_2_ = bf16[256,512]{1,0:T(8,128)(2,1)S(1)} collective-permute-done((bf16[256,512]{1,0:T(8,128)(2,1)S(1)}, bf16[256,512]{1,0:T(8,128)(2,1)S(1)}, u32[]{:S(2)}, u32[]{:S(2)}) %collective-permute-start.12) | collective-permute-done | bytes 262176 | tf_op jit(solution)/shard_map/ppermute | solution.py:398
  32.1 2.1 %collective-permute-done.10.other_ref = bf16[64,512]{1,0:T(8,128)(2,1)S(1)} collective-permute-done((bf16[64,512]{1,0:T(8,128)(2,1)S(1)}, bf16[64,512]{1,0:T(8,128)(2,1)S(1)}, u32[]{:S(2)}, u32[]{:S(2)}) %collective-permute-start.10) | collective-permute-done | bytes 65568 | tf_op jit(solution)/shard_map/ppermute | solution.py:398
  34.2 0.5 project.1
  34.7 5.1 %collective-permute-start.15 = (bf16[64,1024]{1,0:T(8,128)(2,1)S(1)}, bf16[64,1024]{1,0:T(8,128)(2,1)S(1)}, u32[]{:S(2)}, u32[]{:S(2)}) collective-permute-start(bf16[64,1024]{1,0:T(8,128)(2,1)S(1)} %get-tuple-element.47), channel_id=1, source_target_pairs={{0,1},{1,0},{2,3},{3,2},{4,5},{5,4},{6,7},{7,6},{8,9},{9,8},{10,11... | collective-permute-start | bytes 393224 | tf_op jit(solution)/shard_map/ppermute | solution.py:398
  39.7 2.3 %collective-permute-start.7 = (bf16[128,512]{1,0:T(8,128)(2,1)S(1)}, bf16[128,512]{1,0:T(8,128)(2,1)S(1)}, u32[]{:S(2)}, u32[]{:S(2)}) collective-permute-start(bf16[128,512]{1,0:T(8,128)(2,1)S(1)} %get-tuple-element.38), channel_id=1, source_target_pairs={{0,2},{2,0},{4,6},{6,4},{8,10},{10,8},{12,14},{14,12},{1,3},{3,1},... | collective-permute-start | bytes 393224 | tf_op jit(solution)/shard_map/ppermute | solution.py:398
  42.1 0.3 collective-permute-start.8
  42.4 0.8 %collective-permute-start.9 = (bf16[128,512]{1,0:T(8,128)(2,1)S(1)}, bf16[128,512]{1,0:T(8,128)(2,1)S(1)}, u32[]{:S(2)}, u32[]{:S(2)}) collective-permute-start(bf16[128,512]{1,0:T(8,128)(2,1)S(1)} %get-tuple-element.40), channel_id=1, source_target_pairs={{0,6},{2,4},{4,2},{6,0},{8,14},{10,12},{12,10},{14,8},{1,7},{3,5},... | collective-permute-start | bytes 393224 | tf_op jit(solution)/shard_map/ppermute | solution.py:398
  43.3 0.0 collective-permute-done.15.b_ref
  43.3 1.5 %collective-permute-start.16 = (bf16[16,1024]{1,0:T(8,128)(2,1)S(1)}, bf16[16,1024]{1,0:T(8,128)(2,1)S(1)}, u32[]{:S(2)}, u32[]{:S(2)}) collective-permute-start(bf16[16,1024]{1,0:T(8,128)(2,1)S(1)} %get-tuple-element.49), channel_id=1, source_target_pairs={{0,2},{2,0},{4,6},{6,4},{8,10},{10,8},{12,14},{14,12},{1,3},{3,1},... | collective-permute-start | bytes 98312 | tf_op jit(solution)/shard_map/ppermute | solution.py:398
  44.8 0.3 collective-permute-start.17
  45.2 1.3 %collective-permute-done.16.rest_1_ = bf16[16,1024]{1,0:T(8,128)(2,1)S(1)} collective-permute-done((bf16[16,1024]{1,0:T(8,128)(2,1)S(1)}, bf16[16,1024]{1,0:T(8,128)(2,1)S(1)}, u32[]{:S(2)}, u32[]{:S(2)}) %collective-permute-start.16) | collective-permute-done | bytes 32800 | tf_op jit(solution)/shard_map/ppermute | solution.py:398
  46.5 1.5 %collective-permute-start.18 = (bf16[16,1024]{1,0:T(8,128)(2,1)S(1)}, bf16[16,1024]{1,0:T(8,128)(2,1)S(1)}, u32[]{:S(2)}, u32[]{:S(2)}) collective-permute-start(bf16[16,1024]{1,0:T(8,128)(2,1)S(1)} %get-tuple-element.51), channel_id=1, source_target_pairs={{0,6},{2,4},{4,2},{6,0},{8,14},{10,12},{12,10},{14,8},{1,7},{3,5},... | collective-permute-start | bytes 98312 | tf_op jit(solution)/shard_map/ppermute | solution.py:398
  48.0 2.3 %collective-permute-done.17.rest_2_ = bf16[16,1024]{1,0:T(8,128)(2,1)S(1)} collective-permute-done((bf16[16,1024]{1,0:T(8,128)(2,1)S(1)}, bf16[16,1024]{1,0:T(8,128)(2,1)S(1)}, u32[]{:S(2)}, u32[]{:S(2)}) %collective-permute-start.17) | collective-permute-done | bytes 32800 | tf_op jit(solution)/shard_map/ppermute | solution.py:398
  50.3 0.4 collective-permute-done.18.rest_3_
  50.7 8.0 %collective-permute-start.19 = (bf16[16,1024]{1,0:T(8,128)(2,1)S(1)}, bf16[16,1024]{1,0:T(8,128)(2,1)S(1)}, u32[]{:S(2)}, u32[]{:S(2)}) collective-permute-start(bf16[16,1024]{1,0:T(8,128)(2,1)S(1)} %add_shares.1), channel_id=1, source_target_pairs={{0,0},{1,8},{2,2},{3,10},{4,4},{5,12},{6,6},{7,14},{8,1},{9,9},{10... | collective-permute-start | bytes 98312 | tf_op jit(solution)/shard_map/ppermute | solution.py:433
  58.8 0.0 collective-permute-done.7.rest_1_
  58.8 0.0 collective-permute-done.8.rest_2_
  58.8 0.0 collective-permute-done.9.rest_3_
  58.8 0.8 %join_heads.1 = bf16[128,2048]{1,0:T(8,128)(2,1)} custom-call(s32[1]{0:T(128)} %bitcast.c_ref, bf16[128,512]{1,0:T(8,128)(2,1)S(1)} %get-tuple-element.37.rest_0_, bf16[128,512]{1,0:T(8,128)(2,1)S(1)} %collective-permute-done.7.rest_1_, bf16[128,512]{1,0:T(8,128)(2,1)S(1)} %collective-permute-done.8.rest_2_, bf16[128,512]{1,0:T(8,128)(2,1)S(1)} %collective-permute-done.9.rest_3_), custom_call_target="tpu_custom_call" | custom-call | tf_op jit(solution)/shard_map/join_heads/pallas_call | solution.py:367
  59.7 0.8 %collective-permute-done.19 = bf16[16,1024]{1,0:T(8,128)(2,1)S(1)} collective-permute-done((bf16[16,1024]{1,0:T(8,128)(2,1)S(1)}, bf16[16,1024]{1,0:T(8,128)(2,1)S(1)}, u32[]{:S(2)}, u32[]{:S(2)}) %collective-permute-start.19) | collective-permute-done | bytes 32800 | tf_op jit(solution)/shard_map/ppermute | solution.py:433
  60.5 0.6 %copy.11 = bf16[16,1024]{1,0:T(8,128)(2,1)} copy(bf16[16,1024]{1,0:T(8,128)(2,1)S(1)} %collective-permute-done.19) | data formatting | bytes 65536
  (2 shorter events, 0.1 us)
Async XLA Ops:
  2.1 12.5 %collective-permute-start.3 = (bf16[128,256]{1,0:T(8,128)(2,1)S(1)}, bf16[128,256]{1,0:T(8,128)(2,1)S(1)}, u32[]{:S(2)}, u32[]{:S(2)}) collective-permute-start(bf16[128,256]{1,0:T(8,128)(2,1)S(1)} %get-tuple-element.33), channel_id=1, source_target_pairs={{0,8},{2,10},{4,12},{6,14},{1,9},{3,11},{5,13},{7,15},{16,24},{18,... | collective-permute-start | bytes 196616 | tf_op jit(solution)/shard_map/ppermute | solution.py:398
  8.5 11.1 %collective-permute-start.13 = (bf16[128,512]{1,0:T(8,128)(2,1)S(1)}, bf16[128,512]{1,0:T(8,128)(2,1)S(1)}, u32[]{:S(2)}, u32[]{:S(2)}) collective-permute-start(bf16[128,512]{1,0:T(8,128)(2,1)S(1)} %get-tuple-element.45), channel_id=1, source_target_pairs={{0,6},{2,4},{4,2},{6,0},{8,14},{10,12},{12,10},{14,8},{1,7},{3,5},... | collective-permute-start | bytes 393224 | tf_op jit(solution)/shard_map/ppermute | solution.py:398
  10.8 6.1 %collective-permute-start.4 = (bf16[128,256]{1,0:T(8,128)(2,1)S(1)}, bf16[128,256]{1,0:T(8,128)(2,1)S(1)}, u32[]{:S(2)}, u32[]{:S(2)}) collective-permute-start(bf16[128,256]{1,0:T(8,128)(2,1)S(1)} %get-tuple-element.34), channel_id=1, source_target_pairs={{0,10},{2,8},{4,14},{6,12},{1,11},{3,9},{5,15},{7,13},{16,26},{18,... | collective-permute-start | bytes 196616 | tf_op jit(solution)/shard_map/ppermute | solution.py:398
  12.1 4.9 %collective-permute-start.5 = (bf16[128,256]{1,0:T(8,128)(2,1)S(1)}, bf16[128,256]{1,0:T(8,128)(2,1)S(1)}, u32[]{:S(2)}, u32[]{:S(2)}) collective-permute-start(bf16[128,256]{1,0:T(8,128)(2,1)S(1)} %get-tuple-element.35), channel_id=1, source_target_pairs={{0,12},{2,14},{4,8},{6,10},{1,13},{3,15},{5,9},{7,11},{16,28},{18,... | collective-permute-start | bytes 196616 | tf_op jit(solution)/shard_map/ppermute | solution.py:398
  13.4 8.5 %collective-permute-start = (bf16[776,128]{1,0:T(8,128)(2,1)S(1)}, bf16[776,128]{1,0:T(8,128)(2,1)S(1)}, u32[]{:S(2)}, u32[]{:S(2)}) collective-permute-start(bf16[776,128]{1,0:T(8,128)(2,1)S(1)} %get-tuple-element.30), channel_id=1, source_target_pairs={{0,2},{2,0},{4,6},{6,4},{8,10},{10,8},{12,14},{14,12},{1,3},{3,1},... | collective-permute-start | bytes 595976 | tf_op jit(solution)/shard_map/ppermute | solution.py:398
  14.6 4.9 %collective-permute-start.6 = (bf16[128,256]{1,0:T(8,128)(2,1)S(1)}, bf16[128,256]{1,0:T(8,128)(2,1)S(1)}, u32[]{:S(2)}, u32[]{:S(2)}) collective-permute-start(bf16[128,256]{1,0:T(8,128)(2,1)S(1)} %get-tuple-element.36), channel_id=1, source_target_pairs={{0,14},{2,12},{4,10},{6,8},{1,15},{3,13},{5,11},{7,9},{16,30},{18,... | collective-permute-start | bytes 196616 | tf_op jit(solution)/shard_map/ppermute | solution.py:398
  16.9 6.2 %collective-permute-start.1 = (bf16[776,128]{1,0:T(8,128)(2,1)S(1)}, bf16[776,128]{1,0:T(8,128)(2,1)S(1)}, u32[]{:S(2)}, u32[]{:S(2)}) collective-permute-start(bf16[776,128]{1,0:T(8,128)(2,1)S(1)} %get-tuple-element.31), channel_id=1, source_target_pairs={{0,4},{2,6},{4,0},{6,2},{8,12},{10,14},{12,8},{14,10},{1,5},{3,7},... | collective-permute-start | bytes 595976 | tf_op jit(solution)/shard_map/ppermute | solution.py:398
  17.0 9.2 %collective-permute-start.2 = (bf16[776,128]{1,0:T(8,128)(2,1)S(1)}, bf16[776,128]{1,0:T(8,128)(2,1)S(1)}, u32[]{:S(2)}, u32[]{:S(2)}) collective-permute-start(bf16[776,128]{1,0:T(8,128)(2,1)S(1)} %get-tuple-element.32), channel_id=1, source_target_pairs={{0,6},{2,4},{4,2},{6,0},{8,14},{10,12},{12,10},{14,8},{1,7},{3,5},... | collective-permute-start | bytes 595976 | tf_op jit(solution)/shard_map/ppermute | solution.py:398
  19.5 11.3 %collective-permute-start.11 = (bf16[256,512]{1,0:T(8,128)(2,1)S(1)}, bf16[256,512]{1,0:T(8,128)(2,1)S(1)}, u32[]{:S(2)}, u32[]{:S(2)}) collective-permute-start(bf16[256,512]{1,0:T(8,128)(2,1)S(1)} %get-tuple-element.43), channel_id=1, source_target_pairs={{0,2},{2,0},{4,6},{6,4},{8,10},{10,8},{12,14},{14,12},{1,3},{3,1},... | collective-permute-start | bytes 786440 | tf_op jit(solution)/shard_map/ppermute | solution.py:398
  19.6 12.5 %collective-permute-start.12 = (bf16[256,512]{1,0:T(8,128)(2,1)S(1)}, bf16[256,512]{1,0:T(8,128)(2,1)S(1)}, u32[]{:S(2)}, u32[]{:S(2)}) collective-permute-start(bf16[256,512]{1,0:T(8,128)(2,1)S(1)} %get-tuple-element.44), channel_id=1, source_target_pairs={{0,4},{2,6},{4,0},{6,2},{8,12},{10,14},{12,8},{14,10},{1,5},{3,7},... | collective-permute-start | bytes 786440 | tf_op jit(solution)/shard_map/ppermute | solution.py:398
  21.9 8.9 %collective-permute-start.14 = (bf16[128,512]{1,0:T(8,128)(2,1)S(1)}, bf16[128,512]{1,0:T(8,128)(2,1)S(1)}, u32[]{:S(2)}, u32[]{:S(2)}) collective-permute-start(bf16[128,512]{1,0:T(8,128)(2,1)S(1)} %collective-permute-done.13.rest_3_), channel_id=1, source_target_pairs={{0,16},{16,0},{1,17},{17,1},{2,18},{18,2},{3,19},{19,3},{4,20},{20... | collective-permute-start | bytes 393224 | tf_op jit(solution)/shard_map/ppermute | solution.py:398
  29.7 4.5 %collective-permute-start.10 = (bf16[64,512]{1,0:T(8,128)(2,1)S(1)}, bf16[64,512]{1,0:T(8,128)(2,1)S(1)}, u32[]{:S(2)}, u32[]{:S(2)}) collective-permute-start(bf16[64,512]{1,0:T(8,128)(2,1)S(1)} %get-tuple-element.41.own_ref), channel_id=1, source_target_pairs={{0,8},{2,10},{4,12},{6,14},{8,0},{10,2},{12,4},{14,6},{1,9},{3,11}... | collective-permute-start | bytes 196616 | tf_op jit(solution)/shard_map/ppermute | solution.py:398
  34.7 8.6 %collective-permute-start.15 = (bf16[64,1024]{1,0:T(8,128)(2,1)S(1)}, bf16[64,1024]{1,0:T(8,128)(2,1)S(1)}, u32[]{:S(2)}, u32[]{:S(2)}) collective-permute-start(bf16[64,1024]{1,0:T(8,128)(2,1)S(1)} %get-tuple-element.47), channel_id=1, source_target_pairs={{0,1},{1,0},{2,3},{3,2},{4,5},{5,4},{6,7},{7,6},{8,9},{9,8},{10,11... | collective-permute-start | bytes 393224 | tf_op jit(solution)/shard_map/ppermute | solution.py:398
  39.7 19.1 %collective-permute-start.7 = (bf16[128,512]{1,0:T(8,128)(2,1)S(1)}, bf16[128,512]{1,0:T(8,128)(2,1)S(1)}, u32[]{:S(2)}, u32[]{:S(2)}) collective-permute-start(bf16[128,512]{1,0:T(8,128)(2,1)S(1)} %get-tuple-element.38), channel_id=1, source_target_pairs={{0,2},{2,0},{4,6},{6,4},{8,10},{10,8},{12,14},{14,12},{1,3},{3,1},... | collective-permute-start | bytes 393224 | tf_op jit(solution)/shard_map/ppermute | solution.py:398
  42.1 16.7 %collective-permute-start.8 = (bf16[128,512]{1,0:T(8,128)(2,1)S(1)}, bf16[128,512]{1,0:T(8,128)(2,1)S(1)}, u32[]{:S(2)}, u32[]{:S(2)}) collective-permute-start(bf16[128,512]{1,0:T(8,128)(2,1)S(1)} %get-tuple-element.39), channel_id=1, source_target_pairs={{0,4},{2,6},{4,0},{6,2},{8,12},{10,14},{12,8},{14,10},{1,5},{3,7},... | collective-permute-start | bytes 393224 | tf_op jit(solution)/shard_map/ppermute | solution.py:398
  42.4 16.4 %collective-permute-start.9 = (bf16[128,512]{1,0:T(8,128)(2,1)S(1)}, bf16[128,512]{1,0:T(8,128)(2,1)S(1)}, u32[]{:S(2)}, u32[]{:S(2)}) collective-permute-start(bf16[128,512]{1,0:T(8,128)(2,1)S(1)} %get-tuple-element.40), channel_id=1, source_target_pairs={{0,6},{2,4},{4,2},{6,0},{8,14},{10,12},{12,10},{14,8},{1,7},{3,5},... | collective-permute-start | bytes 393224 | tf_op jit(solution)/shard_map/ppermute | solution.py:398
  43.3 3.2 %collective-permute-start.16 = (bf16[16,1024]{1,0:T(8,128)(2,1)S(1)}, bf16[16,1024]{1,0:T(8,128)(2,1)S(1)}, u32[]{:S(2)}, u32[]{:S(2)}) collective-permute-start(bf16[16,1024]{1,0:T(8,128)(2,1)S(1)} %get-tuple-element.49), channel_id=1, source_target_pairs={{0,2},{2,0},{4,6},{6,4},{8,10},{10,8},{12,14},{14,12},{1,3},{3,1},... | collective-permute-start | bytes 98312 | tf_op jit(solution)/shard_map/ppermute | solution.py:398
  44.8 5.4 %collective-permute-start.17 = (bf16[16,1024]{1,0:T(8,128)(2,1)S(1)}, bf16[16,1024]{1,0:T(8,128)(2,1)S(1)}, u32[]{:S(2)}, u32[]{:S(2)}) collective-permute-start(bf16[16,1024]{1,0:T(8,128)(2,1)S(1)} %get-tuple-element.50), channel_id=1, source_target_pairs={{0,4},{2,6},{4,0},{6,2},{8,12},{10,14},{12,8},{14,10},{1,5},{3,7},... | collective-permute-start | bytes 98312 | tf_op jit(solution)/shard_map/ppermute | solution.py:398
  46.5 4.2 %collective-permute-start.18 = (bf16[16,1024]{1,0:T(8,128)(2,1)S(1)}, bf16[16,1024]{1,0:T(8,128)(2,1)S(1)}, u32[]{:S(2)}, u32[]{:S(2)}) collective-permute-start(bf16[16,1024]{1,0:T(8,128)(2,1)S(1)} %get-tuple-element.51), channel_id=1, source_target_pairs={{0,6},{2,4},{4,2},{6,0},{8,14},{10,12},{12,10},{14,8},{1,7},{3,5},... | collective-permute-start | bytes 98312 | tf_op jit(solution)/shard_map/ppermute | solution.py:398
  50.7 9.7 %collective-permute-start.19 = (bf16[16,1024]{1,0:T(8,128)(2,1)S(1)}, bf16[16,1024]{1,0:T(8,128)(2,1)S(1)}, u32[]{:S(2)}, u32[]{:S(2)}) collective-permute-start(bf16[16,1024]{1,0:T(8,128)(2,1)S(1)} %add_shares.1), channel_id=1, source_target_pairs={{0,0},{1,8},{2,2},{3,10},{4,4},{5,12},{6,6},{7,14},{8,1},{9,9},{10... | collective-permute-start | bytes 98312 | tf_op jit(solution)/shard_map/ppermute | solution.py:433
